TPU v7x, 256 devices: a whole 4x4x8 slice. The times are simulated.
256 devices in a mesh: dp: 8 (over z_lo, x), fsdp: 32 (over y, z_hi, core).
Axes of the slice: x: 4, y: 4, z: 8 (z_hi: 4, z_lo: 2; z = z_hi * 2 + z_lo), core: 2. Of those that a mesh axis runs over, the one named last changes fastest.
Arguments:
- glu_out: bfloat16 [256, 768, 1536], P(('dp', 'fsdp')), may hold values from -6 to 6
- residual_in: bfloat16 [256, 768, 1536], P(('dp', 'fsdp')), may hold values from -6 to 6
- cotangent: bfloat16 [256, 768, 1536], P(('dp', 'fsdp')), may hold values from -6 to 6
- lengths: int32 [256], P(('dp', 'fsdp')), may hold values from 192 to 768, as said below
- conv_kernel: bfloat16 [5, 1536], P(None, 'fsdp'), may hold values from -2.5 to 2.5
- norm_gain: bfloat16 [1536], P('fsdp'), may hold values from 0.099609375 to 1.8984375
- norm_bias: bfloat16 [1536], P('fsdp'), may hold values from -3 to 3
- proj_weight: bfloat16 [1536, 1536], P('fsdp'), may hold values from -0.15625 to 0.15625
Outputs:
- block_out: bfloat16 [256, 768, 1536], P(('dp', 'fsdp'))
- glu_grad: bfloat16 [256, 768, 1536], P(('dp', 'fsdp'))
- proj_grad: float32 [1536, 1536], P('fsdp')
- kernel_grad: float32 [5, 1536], P(None, 'fsdp')
- norm_grads: float32 [2, 1536], P(None, 'fsdp')
Inputs may be any that keep to these rules, and one draw needn't show every extreme that they name: `lengths`: lengths are drawn independently for each utterance; one utterance has all 768 frames valid and another has 192.
All inputs are finite; a program needn't handle non-finite values.
Results may differ from a plain program's by a relative error of at most 0.0029.
Values may be sent and summed in bfloat16 or wider, within the bound.
No kernel may reach another device: no remote copies, remote signals or barrier semaphores. Data moves between devices by JAX's collectives and lax.ppermute only.
A program may use at most 128 MiB of HBM per device.

v0:
```python
import jax
import jax.numpy as jnp
from jax import lax
from jax.sharding import PartitionSpec as P

TAPS = 5


def local(glu_out, residual_in, cotangent, lengths, conv_kernel, norm_gain, norm_bias, proj_weight):
    kernel, gain, bias = (
        lax.all_gather(conv_kernel, "fsdp", axis=1, tiled=True),
        lax.all_gather(norm_gain, "fsdp", axis=0, tiled=True),
        lax.all_gather(norm_bias, "fsdp", axis=0, tiled=True),
    )
    kernel = kernel.astype(jnp.float32)
    gain = gain.astype(jnp.float32)
    bias = bias.astype(jnp.float32)
    utt_count, frame_count, width = glu_out.shape
    rows_count = utt_count * frame_count
    half = (TAPS - 1) // 2
    frame_ids = jnp.arange(frame_count, dtype=jnp.int32)
    mask = (frame_ids[None, :] < lengths[:, None]).astype(jnp.float32)[:, :, None]
    masked = glu_out.astype(jnp.float32) * mask
    padded = jnp.pad(masked, ((0, 0), (half, half), (0, 0)))
    conv = jnp.zeros_like(masked)
    for k in range(TAPS):
        conv = conv + kernel[k] * padded[:, k : k + frame_count, :]
    mean_val = jnp.mean(conv, axis=-1, keepdims=True)
    centred = conv - mean_val
    rstd = lax.rsqrt(jnp.mean(centred * centred, axis=-1, keepdims=True) + 1e-05)
    normed = centred * rstd
    pre = normed * gain + bias
    sig = jax.nn.sigmoid(pre)
    swished = (pre * sig).astype(jnp.bfloat16)
    flat = swished.reshape(rows_count, width)
    cols = flat
    proj = jnp.dot(
        cols,
        lax.all_gather(proj_weight, "fsdp", axis=0, tiled=True),
        preferred_element_type=jnp.float32,
    )
    proj = proj.reshape(glu_out.shape)
    block_out = (residual_in.astype(jnp.float32) + mask * proj).astype(jnp.bfloat16)
    gout = (cotangent.astype(jnp.float32) * mask).astype(jnp.bfloat16)
    gflat = gout.reshape(rows_count, width)
    gswish = lax.dot_general(
        gflat,
        lax.all_gather(proj_weight, "fsdp", axis=0, tiled=True),
        (((1,), (1,)), ((), ())),
        preferred_element_type=jnp.float32,
    )
    gswish = gswish.reshape(glu_out.shape)
    gpre = gswish * sig * (1.0 + pre * (1.0 - sig))
    gain_term = jnp.sum(gpre * normed, axis=(0, 1))
    bias_term = jnp.sum(gpre, axis=(0, 1))
    gnorm = gpre * gain
    gconv = rstd * (
        gnorm
        - jnp.mean(gnorm, axis=-1, keepdims=True)
        - normed * jnp.mean(gnorm * normed, axis=-1, keepdims=True)
    )
    kernel_terms = jnp.stack(
        [jnp.sum(gconv * padded[:, k : k + frame_count, :], axis=(0, 1)) for k in range(TAPS)]
    )
    gpad = jnp.pad(gconv, ((0, 0), (half, half), (0, 0)))
    gin = jnp.zeros_like(gconv)
    for k in range(TAPS):
        gin = gin + kernel[k] * gpad[:, TAPS - 1 - k : TAPS - 1 - k + frame_count, :]
    glu_grad = (gin * mask).astype(jnp.bfloat16)
    small = jnp.concatenate([kernel_terms, gain_term[None], bias_term[None]], axis=0)
    small_share = lax.psum_scatter(small, "fsdp", scatter_dimension=1, tiled=True)
    cols = flat
    share = lax.psum_scatter(
        lax.dot_general(cols, gflat, (((0,), (0,)), ((), ())), preferred_element_type=jnp.float32),
        "fsdp",
        scatter_dimension=0,
        tiled=True,
    )
    proj_grad, small_total = lax.psum((share, small_share), "dp")
    return (block_out, glu_grad, proj_grad, small_total[:TAPS], small_total[TAPS:])


def solution(mesh):
    placed = (
        P(("dp", "fsdp"), None, None),
        P(("dp", "fsdp"), None, None),
        P(("dp", "fsdp"), None, None),
        P(("dp", "fsdp")),
        P(None, "fsdp"),
        P("fsdp"),
        P("fsdp"),
        P("fsdp", None),
    )
    return jax.shard_map(
        local,
        mesh=mesh,
        in_specs=placed,
        out_specs=(
            P(("dp", "fsdp"), None, None),
            P(("dp", "fsdp"), None, None),
            P("fsdp", None),
            P(None, "fsdp"),
            P(None, "fsdp"),
        ),
        check_vma=False,
    )
```

profile of v0, /device:TPU:32, one launch (start us, length us, event | category | flops | bytes accessed | tf_op | source)
XLA Modules:
  0.0 448.4 jit_solution(17166549743025896024)
XLA Ops:
  7.2 0.0 all-gather.3.cloned.1.call-start
  7.2 0.7 all-gather.3.cloned.1.call-update
  7.9 0.0 reduce-scatter.5.cloned.1.call-start
  8.6 1.3 dynamic-slice
  10.5 0.9 dynamic-update-slice.1
  11.4 0.8 dynamic-update-slice
  12.2 79.9 %all-reduce.4 = (bf16[1536]{0:T(1024)(128)(2,1)S(1)}, bf16[1536]{0:T(1024)(128)(2,1)S(1)}) all-reduce(bf16[1536]{0:T(1024)(128)(2,1)S(1)} %dynamic-update-slice.1, bf16[1536]{0:T(1024)(128)(2,1)S(1)} %dynamic-update-slice), channel_id=1, replica_groups=mesh['dp'=8,'fsdp'=32] {'fsdp'}, use_global_device_ids=true, to_apply=%add.3 | all-reduce | flops 3072 | bytes 12288
  92.2 39.3 %all-gather = bf16[32,48,5]{1,2,0:T(8,128)(2,1)S(1)} all-gather(bf16[1,48,5]{1,2,0:T(8,128)(2,1)} %bitcast.37), channel_id=1, replica_groups=mesh['dp'=8,'fsdp'=32] {'fsdp'}, dimensions={0}, use_global_device_ids=true | all-gather | bytes 15840 | tf_op jit(solution)/shard_map/all_gather | solution.py:11
  131.5 0.1 reshape.110
  131.6 0.1 slice_reduce_fusion.4
  131.7 2.0 convert_multiply_fusion
  133.8 0.0 copy-start.1
  133.8 3.6 fusion.10
  137.4 0.0 copy-done.1
  137.4 0.0 copy-start
  137.4 0.0 copy-start.4
  137.5 0.6 multiply_reduce_fusion.7
  138.1 1.8 copy-done
  139.8 1.0 copy-done.4
  140.8 7.2 %fusion.4 = f32[1536,1536]{1,0:T(8,128)} fusion(bf16[1,768,1536]{2,1,0:T(8,128)(2,1)S(1)} %copy-done.4, f32[768]{0:T(1024)S(1)} %fusion.9, f32[1,768,1536]{2,1,0:T(8,128)S(1)} %get-tuple-element.23, f32[1536]{0:T(1024)S(1)} %convert_element_type.47, f32[1536]{0:T(1024)S(1)} %convert_element_type.46, f32[768]{0:T(1024)S(1)} %add_rsqrt_fusion, ...), kind=kOutput, calls=%fused_computation.28 | convolution fusion | flops 3638034432 | bytes 16536576 | tf_op jit(solution)/shard_map/dot_general | solution.py:74
  148.0 0.0 reduce-scatter.5.cloned.1.call-update
  148.1 0.0 copy-start.2
  148.1 0.2 reduce-scatter.7.cloned.1.call-start
  148.3 0.0 all-gather.3.cloned.1.call-done
  148.3 10.1 %multiply_reduce_fusion = (f32[1536]{0:T(1024)S(1)}, f32[768]{0:T(1024)S(1)}, f32[768]{0:T(1024)S(1)}, f32[1536]{0:T(1024)S(1)}, f32[1,768,1536]{2,1,0:T(8,128)S(1)}) fusion(f32[1,768,1536]{2,1,0:T(8,128)} %copy-done, f32[768]{0:T(1024)S(1)} %add_rsqrt_fusion, f32[768]{0:T(1024)S(1)} %broadcast_multiply_fusion.2, f32[1536]{0:T(1024)S(1)} %convert_element_type.46, ...), kind=kOutput, calls=%fused_computation.4 | convolution fusion | flops 3649826304 | bytes 16555008 | tf_op jit(solution)/shard_map/dot_general | solution.py:46
  158.5 0.0 copy-done.2
  158.5 17.8 %multiply_reduce_fusion.1 = (f32[1536]{0:T(1024)S(1)}, f32[1536]{0:T(1024)S(1)}, f32[1536]{0:T(1024)S(1)}, f32[1536]{0:T(1024)S(1)}, f32[1536]{0:T(1024)S(1)}, /*index=5*/f32[1,768,1536]{2,1,0:T(8,128)}) fusion(f32[1,768,1536]{2,1,0:T(8,128)} %copy-done.1, f32[768]{0:T(1024)S(1)} %fusion.9, bf16[1,768,1536]{2,1,0:T(8,128)(2,1)S(1)} %copy-done.2, ...), kind=kLoop, calls=%fused_computation.5 | loop fusion | flops 22405632 | bytes 21285888 | tf_op jit(solution)/shard_map/reduce_sum | solution.py:63
  176.3 0.1 concatenate.3
  176.4 1.2 copy.16
  177.6 0.0 reduce-scatter.7.cloned.1.call-update
  177.6 0.0 all-reduce.7.cloned.1.call-start
  177.7 10.8 %fusion.1 = bf16[1,768,1536]{2,1,0:T(8,128)(2,1)} fusion(bf16[1,768,1536]{2,1,0:T(8,128)(2,1)} %param.9, bf16[1536,1536]{1,0:T(8,128)(2,1)} %all-gather.3.cloned.1.call-done, f32[768]{0:T(1024)S(1)} %fusion.9, f32[1,768,1536]{2,1,0:T(8,128)} %copy-done, f32[1536]{0:T(1024)S(1)} %convert_element_type.47, f32[1536]{0:T(1024)S(1)} %convert_element_type.46, ...), kind=kOutput, calls=%fused_computation.3 | convolution fusion | flops 3639214080 | bytes 14177280 | tf_op jit(solution)/shard_map/dot_general | solution.py:37
  188.4 82.4 %reduce-scatter.5.cloned.1.call-done = f32[48,1536]{1,0:T(8,128)} async-done(((f32[1536,1536]{1,0:T(8,128)}), f32[48,1536]{1,0:T(8,128)}) %reduce-scatter.5.cloned.1.call-update) | async-done | bytes 294928 | tf_op jit(solution)/shard_map/reduce_scatter | solution.py:73
  270.8 0.0 all-reduce.7.cloned.1.call-update
  270.9 12.9 %multiply_convert_fusion = bf16[1,768,1536]{2,1,0:T(8,128)(2,1)} fusion(f32[1,768,1536]{2,1,0:T(8,128)} %get-tuple-element.21, f32[1536]{0:T(1024)S(1)} %get-tuple-element.15, f32[1536]{0:T(1024)S(1)} %get-tuple-element.16, f32[1536]{0:T(1024)S(1)} %get-tuple-element.17, f32[1536]{0:T(1024)S(1)} %get-tuple-element.18, f32[768]{0:T(1024)S(1)} %fusion.9, ...), kind=kLoop, calls=%fused_computation.10 | loop fusion | flops 12976128 | bytes 7111680 | tf_op jit(solution)/shard_map/convert_element_type | solution.py:69
  283.7 78.2 %reduce-scatter.7.cloned.1.call-done = f32[48,7]{1,0:T(8,128)} async-done(((f32[1536,7]{1,0:T(8,128)}), f32[48,7]{1,0:T(8,128)}) %reduce-scatter.7.cloned.1.call-update) | async-done | bytes 1360
  362.0 0.8 copy.17
  362.8 19.4 %psum.15 = f32[7,48]{1,0:T(8,128)S(1)} all-reduce(f32[7,48]{1,0:T(8,128)S(1)} %copy.17), channel_id=1, replica_groups=mesh['dp'=8,'fsdp'=32] {'dp'}, use_global_device_ids=true, to_apply=%region_14.15 | all-reduce | flops 336 | bytes 2688 | tf_op jit(solution)/shard_map/psum | solution.py:79
  382.2 0.0 copy-start.3
  382.3 0.6 slice.71
  382.8 57.4 %all-reduce.7.cloned.1.call-done = f32[48,1536]{1,0:T(8,128)} async-done(((f32[48,1536]{1,0:T(8,128)}), f32[48,1536]{1,0:T(8,128)}) %all-reduce.7.cloned.1.call-update) | async-done | bytes 294928 | tf_op jit(solution)/shard_map/psum | solution.py:79
  440.2 1.7 copy.23
  441.9 0.0 copy-done.3
  (16 shorter events, 0.1 us)
Async XLA Ops:
  7.2 141.2 %all-gather.3.cloned.1.call-start = ((), (), s32[]{:S(2)}) async-start(), calls=%async_computation.2 | async-start | bytes 4866048 | tf_op jit(solution)/shard_map/all_gather | solution.py:39
  7.9 262.9 %reduce-scatter.5.cloned.1.call-start = ((), (), s32[]{:S(2)}) async-start(), calls=%async_computation.3 | async-start | bytes 9732096 | tf_op jit(solution)/shard_map/reduce_scatter | solution.py:73
  133.8 3.6 copy-start.1
  137.4 2.4 copy-start
  137.4 3.4 copy-start.4
  148.1 10.4 %copy-start.2 = (bf16[1,768,1536]{2,1,0:T(8,128)(2,1)S(1)}, bf16[1,768,1536]{2,1,0:T(8,128)(2,1)}, u32[]{:S(2)}) copy-start(bf16[1,768,1536]{2,1,0:T(8,128)(2,1)} %param.8) | copy-start | bytes 7077892
  148.1 213.9 %reduce-scatter.7.cloned.1.call-start = ((), (), s32[]{:S(2)}) async-start(), calls=%async_computation.5 | async-start | bytes 811008
  177.6 262.6 %all-reduce.7.cloned.1.call-start = ((), (), s32[]{:S(2)}) async-start(), calls=%async_computation.4 | async-start | bytes 589824 | tf_op jit(solution)/shard_map/psum | solution.py:79
  382.2 59.7 %copy-start.3 = (f32[7,48]{1,0:T(8,128)}, f32[7,48]{1,0:T(8,128)S(1)}, u32[]{:S(2)}) copy-start(f32[7,48]{1,0:T(8,128)S(1)} %psum.15) | copy-start | bytes 4036
Sparse Core Ops, SparseCore 0:
  10.5 65.2 all-gather.2
  148.2 122.6 reduce-scatter.4
  275.1 86.8 reduce-scatter.6
  364.7 75.5 all-reduce.6
where the time goes:
time: 451 us; the launch traced here: 448 us
  waiting for transfers between devices  219 us (49%)
  blocking collectives  139 us (31%)
  other arithmetic  36.9 us (8%)
  matrix products  28.1 us (6%)
  between operations  15.3 us (3%)
  local copies, waits for them, and re-layouts  10.3 us (2%)
    reduce_scatter x1, waiting for transfers between devices, local(): lax.psum_scatter(lax.dot_general(cols, gflat, (((0,), (0,)), ((), ())), p...  82.4 us
    unnamed x1, blocking collectives  79.9 us
    unnamed x5, waiting for transfers between devices  79 us
    psum x1, waiting for transfers between devices, local(): proj_grad, small_total = lax.psum((share, small_share), 'dp')  57.4 us
    all_gather x1, blocking collectives, local(): lax.all_gather(conv_kernel, 'fsdp', axis=1, tiled=True)  39.3 us
    psum x1, blocking collectives, local(): proj_grad, small_total = lax.psum((share, small_share), 'dp')  19.4 us
    reduce_sum x1, other arithmetic, local(): jnp.sum(gconv * padded[:, k:k + frame_count, :], axis=(0, 1))  17.8 us
    convert_element_type x1, other arithmetic, local(): glu_grad = (gin * mask).astype(jnp.bfloat16)  12.9 us
  transfers between devices with their start and end apart: 4, of which 3 were waited for; matrix products, arithmetic and copies ran while one was open for 16% of the time, Pallas kernels for 0%

commit v1 on v0

v1 whole, which is shorter than its diff:
```python
import functools

import jax
import jax.numpy as jnp
from jax import lax
from jax.experimental import pallas as pl
from jax.experimental.pallas import tpu as pltpu
from jax.sharding import PartitionSpec as P

TAPS = 5
NX, NY, NZ = 4, 4, 4
F32, BF16 = jnp.float32, jnp.bfloat16
PAD = 8
VMEM_LIMIT = 60 * 1024 * 1024


def fsdp_move(value, y=0, z=0, core=0):
    perm = [(i, i ^ (y * 8 + z * 2 + core)) for i in range(32)]
    return lax.ppermute(value, "fsdp", perm)


def dp_move(value, x=0, low=0):
    perm = [(i, i ^ (low * 4 + x)) for i in range(8)]
    return lax.ppermute(value, "dp", perm)


def params(flops, read, exps=0):
    return dict(
        cost_estimate=pl.CostEstimate(flops=flops, bytes_accessed=read, transcendentals=exps),
    )


def compiler():
    return pltpu.CompilerParams(vmem_limit_bytes=VMEM_LIMIT)


def shifted(near, by, count):
    if by != 0:
        near = pltpu.roll(near, (-by) % near.shape[0], 0)
    return near[PAD : PAD + count]


def sds(shape, dtype):
    return jax.ShapeDtypeStruct(shape, dtype)


def whole(shape):
    return pl.BlockSpec(shape, lambda *_: (0,) * len(shape))


def forward_kernel(lens, par, glu, swished, normed, rstds, masked, *, rows, frames, chunk):
    step = pl.program_id(0)
    length = lens[0]
    width = glu.shape[1]

    @pl.when(step == 0)
    def _():
        masked[pl.ds(0, PAD), :] = jnp.zeros((PAD, width), F32)
        masked[pl.ds(PAD + frames, PAD), :] = jnp.zeros((PAD, width), F32)

        def fill(i, _):
            at = pl.multiple_of(i * 16, 16)
            ids = at + lax.broadcasted_iota(jnp.int32, (16, 1), 0)
            v = glu[pl.ds(at, 16), :].astype(F32)
            masked[pl.ds(pl.multiple_of(at + PAD, 8), 16), :] = jnp.where(ids < length, v, 0.0)
            return 0

        lax.fori_loop(0, frames // 16, fill, 0, unroll=4)

    def one(i, _):
        local = pl.multiple_of(i * chunk, chunk)
        base = step * rows + local
        near = masked[pl.ds(pl.multiple_of(base, 8), chunk + 2 * PAD), :]
        conv = par[0:1, :] * shifted(near, -2, chunk)
        for k in range(1, TAPS):
            conv = conv + par[k : k + 1, :] * shifted(near, k - 2, chunk)
        mean = jnp.sum(conv, axis=1, keepdims=True) * (1.0 / width)
        cent = conv - mean
        var = jnp.sum(cent * cent, axis=1, keepdims=True) * (1.0 / width)
        rstd = lax.rsqrt(var + 1e-05)
        norm = cent * rstd
        pre = norm * par[5:6, :] + par[6:7, :]
        sig = 0.5 * jnp.tanh(0.5 * pre) + 0.5
        ids = base + lax.broadcasted_iota(jnp.int32, (chunk, 1), 0)
        out = jnp.where(ids < length, pre * sig, 0.0)
        swished[pl.ds(local, chunk), :] = out.astype(BF16)
        normed[pl.ds(local, chunk), :] = norm
        rstds[pl.ds(local, chunk), :] = jnp.broadcast_to(rstd, (chunk, 128))
        return 0

    lax.fori_loop(0, rows // chunk, one, 0, unroll=2)


def forward(lens, par, glu, rows=128, chunk=16):
    frames, width = glu.shape
    block = lambda w: pl.BlockSpec((rows, w), lambda i, *_: (i, 0))
    return pl.pallas_call(
        functools.partial(forward_kernel, rows=rows, frames=frames, chunk=chunk),
        out_shape=(sds((frames, width), BF16), sds((frames, width), F32), sds((frames, 128), F32)),
        grid_spec=pltpu.PrefetchScalarGridSpec(
            num_scalar_prefetch=1,
            grid=(frames // rows,),
            in_specs=[whole((8, width)), whole((frames, width))],
            out_specs=(block(width), block(width), block(128)),
            scratch_shapes=[pltpu.VMEM((frames + 2 * PAD, width), F32)],
        ),
        compiler_params=compiler(),
        name="forward",
        **params(frames * width * 40, frames * width * 8, frames * width),
    )(lens, par, glu)


def outer_kernel(core, sw, cot, keep, send):
    res = lax.dot_general(
        sw[...], cot[...], (((0,), (0,)), ((), ())), preferred_element_type=F32
    )
    first = core[0] == 0
    for j in range(4):
        a = res[j * 96 : j * 96 + 48]
        b = res[j * 96 + 48 : j * 96 + 96]
        keep[j] = jnp.where(first, a, b)
        send[j] = jnp.where(first, b, a).astype(BF16)


def outer(core, sw, cot):
    frames, width = sw.shape
    return pl.pallas_call(
        outer_kernel,
        out_shape=(sds((16, 48, width), F32), sds((16, 48, width), BF16)),
        grid_spec=pltpu.PrefetchScalarGridSpec(
            num_scalar_prefetch=1,
            grid=(4,),
            in_specs=[
                pl.BlockSpec((frames, 384), lambda i, *_: (0, i)),
                whole((frames, width)),
            ],
            out_specs=(
                pl.BlockSpec((4, 48, width), lambda i, *_: (i, 0, 0)),
                pl.BlockSpec((4, 48, width), lambda i, *_: (i, 0, 0)),
            ),
        ),
        compiler_params=compiler(),
        name="outer",
        **params(2 * frames * width * width, 4 * frames * width + 6 * 768 * width),
    )(core, sw, cot)


def stage1_kernel(pos, keep, recv, a0, a1, a2, a3, b0, b1, b2, b3, tmp):
    j = pl.program_id(0)
    x = pos[1]
    for n, out in enumerate((a0, a1, a2, a3)):

        @pl.when(j == n)
        def _(out=out):
            out[...] = (keep[0, 0:2] + recv[0, 0:2].astype(F32)).astype(out.dtype)

    tmp[...] = keep[0, 2:4] + recv[0, 2:4].astype(F32)
    for n, out in enumerate((b0, b1, b2, b3)):
        at = pl.multiple_of((x ^ n) * 384, 128)
        out[0] = tmp[:, :, pl.ds(at, 384)].astype(out.dtype)


def stage1(pos, keep, recv):
    width = keep.shape[-1]
    keep = keep.reshape(4, 4, 48, width)
    recv = recv.reshape(4, 4, 48, width)
    src = pl.BlockSpec((1, 4, 48, width), lambda j, pos: (pos[0] ^ j, 0, 0, 0))
    a = whole((2, 48, width))
    b = pl.BlockSpec((1, 2, 48, 384), lambda j, pos: (pos[0] ^ j, 0, 0, 0))
    kinds = (F32, BF16, BF16, BF16)
    return pl.pallas_call(
        stage1_kernel,
        out_shape=tuple(sds((2, 48, width), t) for t in kinds) + tuple(sds((4, 2, 48, 384), t) for t in kinds),
        grid_spec=pltpu.PrefetchScalarGridSpec(
            num_scalar_prefetch=1,
            grid=(4,),
            in_specs=[src, src],
            out_specs=(a,) * 4 + (b,) * 4,
            scratch_shapes=[pltpu.VMEM((2, 48, width), F32)],
        ),
        compiler_params=compiler(),
        name="stage1",
        **params(768 * width, 768 * width * 9),
    )(pos, keep, recv)


def stage2_kernel(pos, a0, a1, a2, a3, b0, b1, b2, b3, *rest):
    outs, ta, tb = rest[:8], rest[8], rest[9]
    y, x = pos[0], pos[1]
    ta[...] = (a0[...] + a1[...].astype(F32)) + (a2[...].astype(F32) + a3[...].astype(F32))
    tb[...] = (b0[...] + b1[...].astype(F32)) + (b2[...].astype(F32) + b3[...].astype(F32))
    for n in range(4):
        at = pl.multiple_of((x ^ n) * 384, 128)
        outs[n][...] = ta[:, :, pl.ds(at, 384)]
        outs[4 + n][...] = tb[y ^ n]


def stage2(pos, a, b):
    width = a[0].shape[-1]
    return pl.pallas_call(
        stage2_kernel,
        out_shape=(sds((2, 48, 384), F32),) * 8,
        grid_spec=pltpu.PrefetchScalarGridSpec(
            num_scalar_prefetch=1,
            grid=(1,),
            in_specs=[whole((2, 48, width))] * 4 + [whole((4, 2, 48, 384))] * 4,
            out_specs=(whole((2, 48, 384)),) * 8,
            scratch_shapes=[pltpu.VMEM((2, 48, width), F32), pltpu.VMEM((4, 2, 48, 384), F32)],
        ),
        compiler_params=compiler(),
        name="stage2",
        **params(8 * 96 * width, 96 * width * 30),
    )(pos, *a, *b)


def stage3_kernel(pos, a0, a1, a2, a3, b0, b1, b2, b3, o0, o1, o2, o3, tmp):
    z = pos[2]
    tmp[0:2] = (a0[...] + a1[...]) + (a2[...] + a3[...])
    tmp[2:4] = (b0[...] + b1[...]) + (b2[...] + b3[...])
    for n, out in enumerate((o0, o1, o2, o3)):
        out[...] = tmp[z ^ n]


def stage3(pos, a, b):
    return pl.pallas_call(
        stage3_kernel,
        out_shape=(sds((48, 384), F32),) * 4,
        grid_spec=pltpu.PrefetchScalarGridSpec(
            num_scalar_prefetch=1,
            grid=(1,),
            in_specs=[whole((2, 48, 384))] * 8,
            out_specs=(whole((48, 384)),) * 4,
            scratch_shapes=[pltpu.VMEM((4, 48, 384), F32)],
        ),
        compiler_params=compiler(),
        name="stage3",
        **params(8 * 96 * 384, 96 * 384 * 48),
    )(pos, *a, *b)


def join_kernel(pos, v0, v1, v2, v3, out):
    x = pos[1]
    for n, v in enumerate((v0, v1, v2, v3)):
        at = pl.multiple_of((x ^ n) * 384, 128)
        out[:, pl.ds(at, 384)] = v[...]


def join(pos, parts):
    return pl.pallas_call(
        join_kernel,
        out_shape=sds((48, 1536), F32),
        grid_spec=pltpu.PrefetchScalarGridSpec(
            num_scalar_prefetch=1,
            grid=(1,),
            in_specs=[whole((48, 384))] * 4,
            out_specs=whole((48, 1536)),
        ),
        compiler_params=compiler(),
        name="join",
        **params(0, 48 * 1536 * 8),
    )(pos, *parts)


def fetch_weight(pos, pieces, buf, sem):
    y, z, core = pos[0], pos[2], pos[3]
    copies = []
    for n, piece in enumerate(pieces):
        dc, dy = n // 4, n % 4
        for dz in range(4):
            index = ((y ^ dy) * 4 + (z ^ dz)) * 2 + (core ^ dc)
            at = pl.multiple_of(index * 48, 48)
            copies.append(
                pltpu.make_async_copy(
                    piece.at[pl.ds(dz * 48, 48), :], buf.at[pl.ds(at, 48), :], sem.at[n * 4 + dz]
                )
            )
    for c in copies:
        c.start()
    for c in copies:
        c.wait()


def project_kernel(pos, *refs):
    pieces, (sw, res, out, buf, sem) = refs[:8], refs[8:]

    @pl.when(pl.program_id(0) == 0)
    def _():
        fetch_weight(pos, pieces, buf, sem)

    prod = jnp.dot(sw[...], buf[...], preferred_element_type=F32)
    out[...] = (res[...].astype(F32) + prod).astype(BF16)


def project(pos, pieces, sw, res, rows=128):
    frames, width = sw.shape
    block = pl.BlockSpec((rows, width), lambda i, *_: (i, 0))
    return pl.pallas_call(
        project_kernel,
        out_shape=sds((frames, width), BF16),
        grid_spec=pltpu.PrefetchScalarGridSpec(
            num_scalar_prefetch=1,
            grid=(frames // rows,),
            in_specs=[pl.BlockSpec(memory_space=pl.ANY)] * 8 + [block, block],
            out_specs=block,
            scratch_shapes=[pltpu.VMEM((width, width), BF16), pltpu.SemaphoreType.DMA((32,))],
        ),
        compiler_params=compiler(),
        name="project",
        **params(2 * frames * width * width, 6 * frames * width + 2 * width * width),
    )(pos, *pieces, sw, res)


def backward_kernel(pos, *refs, rows, chunk):
    pieces = refs[:8]
    par, cot, nrm, rst, gconv, sums, buf, sem, grad = refs[8:]
    step = pl.program_id(0)
    width = cot.shape[1]
    length = pos[4]

    @pl.when(step == 0)
    def _():
        fetch_weight(pos, pieces, buf, sem)
        sums[...] = jnp.zeros_like(sums)

    grad[...] = lax.dot_general(
        cot[...], buf[...], (((1,), (1,)), ((), ())), preferred_element_type=F32
    )

    def one(i, _):
        at = pl.multiple_of(i * chunk, chunk)
        gain = par[5:6, :]
        norm = nrm[pl.ds(at, chunk), :]
        pre = norm * gain + par[6:7, :]
        sig = 0.5 * jnp.tanh(0.5 * pre) + 0.5
        ids = step * rows + at + lax.broadcasted_iota(jnp.int32, (chunk, 1), 0)
        gs = jnp.where(ids < length, grad[pl.ds(at, chunk), :], 0.0)
        gpre = gs * (sig * (1.0 + pre * (1.0 - sig)))
        gn = gpre * norm
        for h in range(chunk // 8):
            sums[0] += gn[h * 8 : h * 8 + 8]
            sums[1] += gpre[h * 8 : h * 8 + 8]
        gnorm = gpre * gain
        m1 = jnp.sum(gnorm, axis=1, keepdims=True) * (1.0 / width)
        m2 = jnp.sum(gnorm * norm, axis=1, keepdims=True) * (1.0 / width)
        gconv[pl.ds(at, chunk), :] = rst[pl.ds(at, chunk), 0:1] * (gnorm - m1 - norm * m2)
        return 0

    lax.fori_loop(0, rows // chunk, one, 0, unroll=2)


def backward(pos, pieces, par, cot, nrm, rst, rows=128, chunk=16):
    frames, width = cot.shape
    block = lambda w: pl.BlockSpec((rows, w), lambda i, *_: (i, 0))
    return pl.pallas_call(
        functools.partial(backward_kernel, rows=rows, chunk=chunk),
        out_shape=(sds((frames, width), F32), sds((2, 8, width), F32)),
        grid_spec=pltpu.PrefetchScalarGridSpec(
            num_scalar_prefetch=1,
            grid=(frames // rows,),
            in_specs=[pl.BlockSpec(memory_space=pl.ANY)] * 8
            + [whole((8, width)), block(width), block(width), block(128)],
            out_specs=(block(width), whole((2, 8, width))),
            scratch_shapes=[
                pltpu.VMEM((width, width), BF16),
                pltpu.SemaphoreType.DMA((32,)),
                pltpu.VMEM((rows, width), F32),
            ],
        ),
        compiler_params=compiler(),
        name="backward",
        **params(2 * frames * width * width, 10 * frames * width + 2 * width * width, frames * width),
    )(pos, *pieces, par, cot, nrm, rst)


def taps_kernel(pos, par, glu, gconv, out, sums, pad, *, rows, frames, chunk):
    step = pl.program_id(0)
    width = glu.shape[1]
    length = pos[4]

    @pl.when(step == 0)
    def _():
        sums[...] = jnp.zeros_like(sums)
        pad[pl.ds(0, PAD), :] = jnp.zeros((PAD, width), F32)
        pad[pl.ds(PAD + frames, PAD), :] = jnp.zeros((PAD, width), F32)

    @pl.when(step < frames // rows)
    def _():
        pad[pl.ds(pl.multiple_of(PAD + step * rows, 8), rows), :] = gconv[...]

    @pl.when(step > 0)
    def _():
        def one(i, _):
            at = pl.multiple_of(i * chunk, chunk)
            base = (step - 1) * rows + at
            ids = base + lax.broadcasted_iota(jnp.int32, (chunk, 1), 0)
            live = ids < length
            mk = jnp.where(live, glu[pl.ds(at, chunk), :].astype(F32), 0.0)
            near = pad[pl.ds(pl.multiple_of(base, 8), chunk + 2 * PAD), :]
            acc = None
            for k in range(TAPS):
                g = shifted(near, 2 - k, chunk)
                term = par[k : k + 1, :] * g
                acc = term if acc is None else acc + term
                p = mk * g
                for h in range(chunk // 8):
                    sums[k] += p[h * 8 : h * 8 + 8]
            out[pl.ds(at, chunk), :] = jnp.where(live, acc, 0.0).astype(BF16)
            return 0

        lax.fori_loop(0, rows // chunk, one, 0, unroll=2)


def taps(pos, par, glu, gconv, rows=128, chunk=16):
    frames, width = glu.shape
    last = frames // rows - 1
    late = pl.BlockSpec((rows, width), lambda i, *_: (jnp.maximum(i - 1, 0), 0))
    return pl.pallas_call(
        functools.partial(taps_kernel, rows=rows, frames=frames, chunk=chunk),
        out_shape=(sds((frames, width), BF16), sds((TAPS, 8, width), F32)),
        grid_spec=pltpu.PrefetchScalarGridSpec(
            num_scalar_prefetch=1,
            grid=(frames // rows + 1,),
            in_specs=[
                whole((8, width)),
                late,
                pl.BlockSpec((rows, width), lambda i, *_: (jnp.minimum(i, last), 0)),
            ],
            out_specs=(late, whole((TAPS, 8, width))),
            scratch_shapes=[pltpu.VMEM((frames + 2 * PAD, width), F32)],
        ),
        compiler_params=compiler(),
        name="taps",
        **params(frames * width * 20, 8 * frames * width),
    )(pos, par, glu, gconv)


def local(glu_out, residual_in, cotangent, lengths, conv_kernel, norm_gain, norm_bias, proj_weight):
    _, frames, width = glu_out.shape
    glu, res, cot = glu_out[0], residual_in[0], cotangent[0]
    f, d = lax.axis_index("fsdp"), lax.axis_index("dp")
    core, z, y = f % 2, (f // 2) % 4, f // 8
    x = d % 4
    pos = jnp.stack([y, x, z, core, lengths[0]]).astype(jnp.int32)

    own = jnp.concatenate([conv_kernel, norm_gain[None], norm_bias[None]], axis=0)
    own = jnp.pad(own, ((0, 1), (0, 0)))
    par = lax.dynamic_update_slice(jnp.zeros((8, width), BF16), own, (0, f * 48))
    par = par + fsdp_move(par, core=1)
    par = par + fsdp_move(par, y=1) + fsdp_move(par, y=2) + fsdp_move(par, y=3)
    par = par + fsdp_move(par, z=1) + fsdp_move(par, z=2) + fsdp_move(par, z=3)
    par = par.astype(F32)

    block = jnp.concatenate([proj_weight] + [fsdp_move(proj_weight, z=k) for k in (1, 2, 3)], axis=0)
    near = [block] + [fsdp_move(block, y=k) for k in (1, 2, 3)]
    pieces = near + [fsdp_move(p, core=1) for p in near]

    swished, normed, rstd = forward(lengths, par, glu)
    keep, send = outer(core[None].astype(jnp.int32), swished, cot)
    recv = fsdp_move(send, core=1)

    s = stage1(pos, keep, recv)
    a = (s[0],) + tuple(fsdp_move(s[k], y=k) for k in (1, 2, 3))
    b = (s[4],) + tuple(dp_move(s[4 + k], x=k) for k in (1, 2, 3))
    s = stage2(pos, a, b)
    a = (s[0],) + tuple(dp_move(s[k], x=k) for k in (1, 2, 3))
    b = (s[4],) + tuple(fsdp_move(s[4 + k], y=k) for k in (1, 2, 3))
    s = stage3(pos, a, b)
    v = (s[0] + fsdp_move(s[1], z=1)) + (fsdp_move(s[2], z=2) + fsdp_move(s[3], z=3))
    v = v + dp_move(v, low=1)
    proj_grad = join(pos, [v] + [dp_move(v, x=k) for k in (1, 2, 3)])

    gconv, sums = backward(pos, pieces, par, cot, normed, rstd)
    glu_grad, tap_sums = taps(pos, par, glu, gconv)
    block_out = project(pos, pieces, swished, res)

    small = jnp.concatenate([tap_sums, sums, jnp.zeros((1, 8, width), F32)], axis=0).sum(axis=1)
    small = small + fsdp_move(small, core=1)
    small = (small + fsdp_move(small, y=1)) + (fsdp_move(small, y=2) + fsdp_move(small, y=3))
    small = (small + fsdp_move(small, z=1)) + (fsdp_move(small, z=2) + fsdp_move(small, z=3))
    small = lax.dynamic_slice(small, (0, f * 48), (8, 48))
    small = (small + dp_move(small, x=1)) + (dp_move(small, x=2) + dp_move(small, x=3))
    small = small + dp_move(small, low=1)
    return (block_out[None], glu_grad[None], proj_grad, small[:TAPS], small[TAPS : TAPS + 2])


def solution(mesh):
    rows = P(("dp", "fsdp"), None, None)
    return jax.shard_map(
        local,
        mesh=mesh,
        in_specs=(rows, rows, rows, P(("dp", "fsdp")), P(None, "fsdp"), P("fsdp"), P("fsdp"), P("fsdp", None)),
        out_specs=(rows, rows, P("fsdp", None), P(None, "fsdp"), P(None, "fsdp")),
        check_vma=False,
    )
```

time: 451 us -> 216 us (0.48)
  waiting for transfers between devices: 219 us -> 53.7 us
  blocking collectives: 139 us -> 0 us
  Pallas kernels: 0 us -> 78 us
  starting transfers between devices: 0.34 us -> 72.9 us
  other arithmetic: 36.9 us -> 3.34 us
  matrix products: 28.1 us -> 0 us
  between operations: 15.3 us -> 1.69 us
    reduce_scatter x1 -> x0, waiting for transfers between devices: 82.4 us -> none  [local(): lax.psum_scatter(lax.dot_general(cols, gflat, (((0,), (0,)), ((), ())), p...]
    unnamed x1 -> x0, blocking collectives: 79.9 us -> none
    unnamed x5 -> x0, waiting for transfers between devices: 79 us -> none
    pallas_call x0 -> x9, Pallas kernels: none -> 78 us  [the longest x1 21.8 us: backward(): pl.pallas_call(functools.partial(backward_kernel, rows=rows, chunk=chunk)...]
    ppermute x0 -> x48, starting transfers between devices: none -> 72.9 us  [the longest x34 50.7 us: fsdp_move(): return lax.ppermute(value, 'fsdp', perm)]
    psum x1 -> x0, waiting for transfers between devices: 57.4 us -> none  [local(): proj_grad, small_total = lax.psum((share, small_share), 'dp')]
    ppermute x0 -> x48, waiting for transfers between devices: none -> 53.7 us  [the longest x34 51.4 us: fsdp_move(): return lax.ppermute(value, 'fsdp', perm)]
    all_gather x1 -> x0, blocking collectives: 39.3 us -> none  [local(): lax.all_gather(conv_kernel, 'fsdp', axis=1, tiled=True)]
  transfers between devices with their start and end apart: 4 -> 48, of which waited for: 3 -> 12; matrix products, arithmetic and copies ran while one was open for 16% -> 1% of each run, Pallas kernels for 0% -> 24%
where the time goes in v1:
time: 216 us
  Pallas kernels  78 us (36%)
  starting transfers between devices  72.9 us (34%)
  waiting for transfers between devices  53.7 us (25%)
  local copies, waits for them, and re-layouts  5.97 us (3%)
  other arithmetic  3.34 us (2%)
    ppermute x34, waiting for transfers between devices, fsdp_move(): return lax.ppermute(value, 'fsdp', perm)  51.4 us
    ppermute x34, starting transfers between devices, fsdp_move(): return lax.ppermute(value, 'fsdp', perm)  50.7 us
    ppermute x14, starting transfers between devices, dp_move(): return lax.ppermute(value, 'dp', perm)  22.2 us
    pallas_call x1, Pallas kernels, backward(): pl.pallas_call(functools.partial(backward_kernel, rows=rows, chunk=chunk)...  21.8 us
    pallas_call x1, Pallas kernels, forward(): pl.pallas_call(functools.partial(forward_kernel, rows=rows, frames=frames...  11.9 us
    pallas_call x1, Pallas kernels, project(): pl.pallas_call(project_kernel, out_shape=sds((frames, width), BF16), grid...  11 us
    pallas_call x1, Pallas kernels, taps(): pl.pallas_call(functools.partial(taps_kernel, rows=rows, frames=frames, c...  10.4 us
    pallas_call x1, Pallas kernels, outer(): pl.pallas_call(outer_kernel, out_shape=(sds((16, 48, width), F32), sds((1...  8.11 us
  transfers between devices with their start and end apart: 48, of which 12 were waited for; matrix products, arithmetic and copies ran while one was open for 1% of the time, Pallas kernels for 24%

profile of v1, /device:TPU:32, one launch (start us, length us, event | category | flops | bytes accessed | tf_op | source)
XLA Modules:
  0.0 215.5 jit_solution(975132984761658683)
XLA Ops:
  1.6 1.2 collective-permute-done.10
  3.7 3.1 %collective-permute-start.13 = (bf16[8,1536]{1,0:T(8,128)(2,1)S(1)}, bf16[8,1536]{1,0:T(8,128)(2,1)S(1)}, u32[]{:S(2)}, u32[]{:S(2)}) collective-permute-start(bf16[8,1536]{1,0:T(8,128)(2,1)S(1)} %add.89), channel_id=1, source_target_pairs={{0,24},{1,25},{2,26},{3,27},{4,28},{5,29},{6,30},{7,31},{8,16},{9,... | collective-permute-start | bytes 73736 | tf_op jit(solution)/shard_map/ppermute | solution.py:19
  8.8 3.3 %collective-permute-done.12 = bf16[8,1536]{1,0:T(8,128)(2,1)S(1)} collective-permute-done((bf16[8,1536]{1,0:T(8,128)(2,1)S(1)}, bf16[8,1536]{1,0:T(8,128)(2,1)S(1)}, u32[]{:S(2)}, u32[]{:S(2)}) %collective-permute-start.12) | collective-permute-done | bytes 24608 | tf_op jit(solution)/shard_map/ppermute | solution.py:19
  12.2 5.6 %collective-permute-start.16 = (bf16[8,1536]{1,0:T(8,128)(2,1)S(1)}, bf16[8,1536]{1,0:T(8,128)(2,1)S(1)}, u32[]{:S(2)}, u32[]{:S(2)}) collective-permute-start(bf16[8,1536]{1,0:T(8,128)(2,1)S(1)} %add_add_fusion.2), channel_id=1, source_target_pairs={{0,6},{1,7},{2,4},{3,5},{4,2},{5,3},{6,0},{7,1},{8,14},{9,15},{10,... | collective-permute-start | bytes 73736 | tf_op jit(solution)/shard_map/ppermute | solution.py:19
  17.7 1.5 collective-permute-start.15
  20.9 4.6 %collective-permute-done.15 = bf16[8,1536]{1,0:T(8,128)(2,1)S(1)} collective-permute-done((bf16[8,1536]{1,0:T(8,128)(2,1)S(1)}, bf16[8,1536]{1,0:T(8,128)(2,1)S(1)}, u32[]{:S(2)}, u32[]{:S(2)}) %collective-permute-start.15) | collective-permute-done | bytes 24608 | tf_op jit(solution)/shard_map/ppermute | solution.py:19
  26.1 11.9 %forward.1 = (bf16[768,1536]{1,0:T(8,128)(2,1)}, f32[768,1536]{1,0:T(8,128)}, f32[768,128]{1,0:T(8,128)}) custom-call(s32[1]{0:T(128)S(6)} %copy.18.lens, f32[8,1536]{1,0:T(8,128)} %add_convert_fusion.par.refs_8_, bf16[768,1536]{1,0:T(8,128)(2,1)} %bitcast.15), custom_call_target="tpu_custom_call" | custom-call | flops 47185920 | bytes 9437184 | tf_op jit(solution)/shard_map/forward/pallas_call | solution.py:97
  38.0 8.1 %outer.1 = (f32[16,48,1536]{2,1,0:T(8,128)}, bf16[16,48,1536]{2,1,0:T(8,128)(2,1)}) custom-call(s32[1]{0:T(128)} %bitcast.3.core, bf16[768,1536]{1,0:T(8,128)(2,1)} %get-tuple-element.34.refs_8_.sw, bf16[768,1536]{1,0:T(8,128)(2,1)} %bitcast.24), custom_call_target="tpu_custom_call" | custom-call | flops 3623878656 | bytes 11796480 | tf_op jit(solution)/shard_map/outer/pallas_call | solution.py:127
  46.1 3.0 %collective-permute-start.1 = (bf16[48,1536]{1,0:T(8,128)(2,1)S(1)}, bf16[48,1536]{1,0:T(8,128)(2,1)S(1)}, u32[]{:S(2)}, u32[]{:S(2)}) collective-permute-start(bf16[48,1536]{1,0:T(8,128)(2,1)S(1)} %copy-done.9), channel_id=1, source_target_pairs={{0,4},{1,5},{2,6},{3,7},{4,0},{5,1},{6,2},{7,3},{8,12},{9,13},{10,... | collective-permute-start | bytes 442376 | tf_op jit(solution)/shard_map/ppermute | solution.py:19
  49.1 1.5 collective-permute-start
  50.6 2.1 collective-permute-start.2
  52.7 10.1 %collective-permute-done = bf16[48,1536]{1,0:T(8,128)(2,1)S(1)} collective-permute-done((bf16[48,1536]{1,0:T(8,128)(2,1)S(1)}, bf16[48,1536]{1,0:T(8,128)(2,1)S(1)}, u32[]{:S(2)}, u32[]{:S(2)}) %collective-permute-start) | collective-permute-done | bytes 147488 | tf_op jit(solution)/shard_map/ppermute | solution.py:19
  62.9 2.5 %collective-permute-done.2 = bf16[48,1536]{1,0:T(8,128)(2,1)S(1)} collective-permute-done((bf16[48,1536]{1,0:T(8,128)(2,1)S(1)}, bf16[48,1536]{1,0:T(8,128)(2,1)S(1)}, u32[]{:S(2)}, u32[]{:S(2)}) %collective-permute-start.2) | collective-permute-done | bytes 147488 | tf_op jit(solution)/shard_map/ppermute | solution.py:19
  65.4 1.4 collective-permute-start.5
  66.8 1.1 collective-permute-start.4
  67.9 1.7 collective-permute-start.3
  69.6 25.0 %collective-permute-done.5.refs_3_ = bf16[192,1536]{1,0:T(8,128)(2,1)S(1)} collective-permute-done((bf16[192,1536]{1,0:T(8,128)(2,1)S(1)}, bf16[192,1536]{1,0:T(8,128)(2,1)S(1)}, u32[]{:S(2)}, u32[]{:S(2)}) %collective-permute-start.5) | collective-permute-done | bytes 589856 | tf_op jit(solution)/shard_map/ppermute | solution.py:19
  96.0 1.4 copy-done
  97.4 5.8 %stage1.1 = (f32[2,48,1536]{2,1,0:T(8,128)}, bf16[2,48,1536]{2,1,0:T(8,128)(2,1)}, bf16[2,48,1536]{2,1,0:T(8,128)(2,1)}, bf16[2,48,1536]{2,1,0:T(8,128)(2,1)}, f...) custom-call(s32[5]{0:T(128)} %stack.19.pos, ...), custom_call_target="tpu_custom_call" | custom-call | flops 1179648 | bytes 10616832 | tf_op jit(solution)/shard_map/stage1/pallas_call | solution.py:171
  103.7 2.5 %collective-permute-start.19 = (bf16[2,48,1536]{2,1,0:T(8,128)(2,1)}, bf16[2,48,1536]{2,1,0:T(8,128)(2,1)S(1)}, u32[]{:S(2)}, u32[]{:S(2)}) collective-permute-start(bf16[2,48,1536]{2,1,0:T(8,128)(2,1)} %get-tuple-element.43), channel_id=1, source_target_pairs={{0,16},{1,17},{2,18},{3,19},{4,20},{5,21},{6,22},{7,23},{8,24},{9,... | collective-permute-start | bytes 884744 | tf_op jit(solution)/shard_map/ppermute | solution.py:19
  106.2 1.9 collective-permute-start.20
  108.1 1.5 collective-permute-start.21
  109.6 2.7 %collective-permute-start.22 = (bf16[4,2,48,384]{3,2,1,0:T(8,128)(2,1)}, bf16[4,2,48,384]{3,2,1,0:T(8,128)(2,1)S(1)}, u32[]{:S(2)}, u32[]{:S(2)}) collective-permute-start(bf16[4,2,48,384]{3,2,1,0:T(8,128)(2,1)} %get-tuple-element.47), channel_id=1, source_target_pairs={{0,64},{32,96},{64,0},{96,32},{128,192},{160,224},{192,128},{224,1... | collective-permute-start | bytes 884744 | tf_op jit(solution)/shard_map/ppermute | solution.py:24
  113.3 2.8 %collective-permute-start.23 = (bf16[4,2,48,384]{3,2,1,0:T(8,128)(2,1)}, bf16[4,2,48,384]{3,2,1,0:T(8,128)(2,1)S(1)}, u32[]{:S(2)}, u32[]{:S(2)}) collective-permute-start(bf16[4,2,48,384]{3,2,1,0:T(8,128)(2,1)} %get-tuple-element.48), channel_id=1, source_target_pairs={{0,96},{32,64},{64,32},{96,0},{128,224},{160,192},{192,160},{224,1... | collective-permute-start | bytes 884744 | tf_op jit(solution)/shard_map/ppermute | solution.py:24
  116.1 21.8 %backward.1 = (f32[768,1536]{1,0:T(8,128)}, f32[2,8,1536]{2,1,0:T(8,128)}) custom-call(s32[5]{0:T(128)} %stack.19.pos, bf16[192,1536]{1,0:T(8,128)(2,1)} %copy-done.20, bf16[192,1536]{1,0:T(8,128)(2,1)} %collective-permute-done.3.refs_1_, bf16[192,1536]{1,0:T(8,128)(2,1)} %collective-permute-done.4.refs_2_, bf16[192,1536]{1,0:T(8,128)(2,1)} %copy-done.22, ...), custom_call_target="tpu_custom_call" | custom-call | flops 3623878656 | bytes 16515072 | tf_op jit(solution)/shard_map/backward/pallas_call | solution.py:354
  137.9 10.4 %taps.1 = (bf16[768,1536]{1,0:T(8,128)(2,1)}, f32[5,8,1536]{2,1,0:T(8,128)}) custom-call(s32[5]{0:T(128)} %stack.19.pos, f32[8,1536]{1,0:T(8,128)} %add_convert_fusion.par.refs_8_, bf16[768,1536]{1,0:T(8,128)(2,1)} %bitcast.16, f32[768,1536]{1,0:T(8,128)} %get-tuple-element.37.gconv), custom_call_target="tpu_custom_call" | custom-call | flops 23592960 | bytes 9437184 | tf_op jit(solution)/shard_map/taps/pallas_call | solution.py:417
  149.5 3.7 %stage2.1 = (f32[2,48,384]{2,1,0:T(8,128)}, f32[2,48,384]{2,1,0:T(8,128)}, f32[2,48,384]{2,1,0:T(8,128)}, f32[2,48,384]{2,1,0:T(8,128)}, f32[2,48,384]{2,1,0:T(8...) custom-call(s32[5]{0:T(128)} %stack.19.pos, f32[2,48,1536]{2,1,0:T(8,128)} %get-tuple-element.41.a0, ...), custom_call_target="tpu_custom_call" | custom-call | flops 1179648 | bytes 4423680 | tf_op jit(solution)/shard_map/stage2/pallas_call | solution.py:200
  153.8 1.2 collective-permute-done.37
  155.0 1.4 collective-permute-start.40
  157.4 1.8 collective-permute-start.38
  159.2 1.7 collective-permute-start.25
  160.9 2.7 %collective-permute-start.26 = (f32[2,48,384]{2,1,0:T(8,128)}, f32[2,48,384]{2,1,0:T(8,128)S(1)}, u32[]{:S(2)}, u32[]{:S(2)}) collective-permute-start(f32[2,48,384]{2,1,0:T(8,128)} %get-tuple-element.52), channel_id=1, source_target_pairs={{0,96},{32,64},{64,32},{96,0},{128,224},{160,192},{192,160},{224,1... | collective-permute-start | bytes 442376 | tf_op jit(solution)/shard_map/ppermute | solution.py:24
  163.9 2.5 %collective-permute-start.28 = (f32[2,48,384]{2,1,0:T(8,128)}, f32[2,48,384]{2,1,0:T(8,128)S(1)}, u32[]{:S(2)}, u32[]{:S(2)}) collective-permute-start(f32[2,48,384]{2,1,0:T(8,128)} %get-tuple-element.55), channel_id=1, source_target_pairs={{0,16},{1,17},{2,18},{3,19},{4,20},{5,21},{6,22},{7,23},{8,24},{9,... | collective-permute-start | bytes 442376 | tf_op jit(solution)/shard_map/ppermute | solution.py:19
  166.5 1.9 collective-permute-start.29
  168.4 1.9 collective-permute-start.43
  170.3 2.9 %collective-permute-start.42 = (f32[8,1536]{1,0:T(8,128)S(1)}, f32[8,1536]{1,0:T(8,128)S(1)}, u32[]{:S(2)}, u32[]{:S(2)}) collective-permute-start(f32[8,1536]{1,0:T(8,128)S(1)} %add_add_fusion.1), channel_id=1, source_target_pairs={{0,4},{1,5},{2,6},{3,7},{4,0},{5,1},{6,2},{7,3},{8,12},{9,13},{10,... | collective-permute-start | bytes 147464 | tf_op jit(solution)/shard_map/ppermute | solution.py:19
  173.2 2.0 collective-permute-start.41
  175.9 2.8 %stage3.1 = (f32[48,384]{1,0:T(8,128)}, f32[48,384]{1,0:T(8,128)}, f32[48,384]{1,0:T(8,128)}, f32[48,384]{1,0:T(8,128)}) custom-call(s32[5]{0:T(128)} %stack.19.pos, f32[2,48,384]{2,1,0:T(8,128)} %get-tuple-element.49.a0, f32[2,48,384]{2,1,0:T(8,128)} %copy-done.10, f32[2,48,384]{2,1,0:T(8,128)} %copy-done.11, f32[2,48,384]{2,1,0:T(8,128)} %copy-done.12, ...), custom_call_target="tpu_custom_call" | custom-call | flops 294912 | bytes 1769472 | tf_op jit(solution)/shard_map/stage3/pallas_call | solution.py:225
  179.6 3.0 %collective-permute-start.31 = (f32[48,384]{1,0:T(8,128)}, f32[48,384]{1,0:T(8,128)S(1)}, u32[]{:S(2)}, u32[]{:S(2)}) collective-permute-start(f32[48,384]{1,0:T(8,128)} %get-tuple-element.59), channel_id=1, source_target_pairs={{0,4},{1,5},{2,6},{3,7},{4,0},{5,1},{6,2},{7,3},{8,12},{9,13},{10,... | collective-permute-start | bytes 221192 | tf_op jit(solution)/shard_map/ppermute | solution.py:19
  182.7 2.6 %collective-permute-start.32 = (f32[48,384]{1,0:T(8,128)}, f32[48,384]{1,0:T(8,128)S(1)}, u32[]{:S(2)}, u32[]{:S(2)}) collective-permute-start(f32[48,384]{1,0:T(8,128)} %get-tuple-element.60), channel_id=1, source_target_pairs={{0,6},{1,7},{2,4},{3,5},{4,2},{5,3},{6,0},{7,1},{8,14},{9,15},{10,... | collective-permute-start | bytes 221192 | tf_op jit(solution)/shard_map/ppermute | solution.py:19
  186.7 2.7 %collective-permute-start.46 = (f32[8,48]{1,0:T(8,128)S(1)}, f32[8,48]{1,0:T(8,128)S(1)}, u32[]{:S(2)}, u32[]{:S(2)}) collective-permute-start(f32[8,48]{1,0:T(8,128)S(1)} %fusion), channel_id=1, source_target_pairs={{0,96},{32,64},{64,32},{96,0},{128,224},{160,192},{192,160},{224,1... | collective-permute-start | bytes 4616 | tf_op jit(solution)/shard_map/ppermute | solution.py:24
  189.4 1.3 collective-permute-done.32
  191.8 2.0 collective-permute-start.47
  193.8 2.2 %collective-permute-done.33 = f32[48,384]{1,0:T(8,128)S(1)} collective-permute-done((f32[48,384]{1,0:T(8,128)S(1)}, f32[48,384]{1,0:T(8,128)S(1)}, u32[]{:S(2)}, u32[]{:S(2)}) %collective-permute-start.33) | collective-permute-done | bytes 73760 | tf_op jit(solution)/shard_map/ppermute | solution.py:24
  196.7 1.9 collective-permute-start.35
  198.7 1.6 collective-permute-start.34
  200.3 11.0 %project.1 = bf16[768,1536]{1,0:T(8,128)(2,1)} custom-call(s32[5]{0:T(128)} %stack.19.pos, bf16[192,1536]{1,0:T(8,128)(2,1)} %copy-done.20, bf16[192,1536]{1,0:T(8,128)(2,1)} %collective-permute-done.3.refs_1_, bf16[192,1536]{1,0:T(8,128)(2,1)} %collective-permute-done.4.refs_2_, bf16[192,1536]{1,0:T(8,128)(2,1)} %copy-done.22, ...), custom_call_target="tpu_custom_call" | custom-call | flops 3623878656 | bytes 11796480 | tf_op jit(solution)/shard_map/project/pallas_call | solution.py:297
  213.2 2.4 %join.1 = f32[48,1536]{1,0:T(8,128)} custom-call(s32[5]{0:T(128)} %stack.19.pos, f32[48,384]{1,0:T(8,128)} %copy-done.7, f32[48,384]{1,0:T(8,128)} %copy-done.19, f32[48,384]{1,0:T(8,128)} %copy-done.18, f32[48,384]{1,0:T(8,128)} %copy-done.17), custom_call_target="tpu_custom_call" | custom-call | bytes 589824 | tf_op jit(solution)/shard_map/join/pallas_call | solution.py:249
  (125 shorter events, 18.0 us)
Async XLA Ops:
  1.5 1.3 collective-permute-start.10
  3.7 5.1 %collective-permute-start.13 = (bf16[8,1536]{1,0:T(8,128)(2,1)S(1)}, bf16[8,1536]{1,0:T(8,128)(2,1)S(1)}, u32[]{:S(2)}, u32[]{:S(2)}) collective-permute-start(bf16[8,1536]{1,0:T(8,128)(2,1)S(1)} %add.89), channel_id=1, source_target_pairs={{0,24},{1,25},{2,26},{3,27},{4,28},{5,29},{6,30},{7,31},{8,16},{9,... | collective-permute-start | bytes 73736 | tf_op jit(solution)/shard_map/ppermute | solution.py:19
  6.8 5.3 %collective-permute-start.12 = (bf16[8,1536]{1,0:T(8,128)(2,1)S(1)}, bf16[8,1536]{1,0:T(8,128)(2,1)S(1)}, u32[]{:S(2)}, u32[]{:S(2)}) collective-permute-start(bf16[8,1536]{1,0:T(8,128)(2,1)S(1)} %add.89), channel_id=1, source_target_pairs={{0,16},{1,17},{2,18},{3,19},{4,20},{5,21},{6,22},{7,23},{8,24},{9,... | collective-permute-start | bytes 73736 | tf_op jit(solution)/shard_map/ppermute | solution.py:19
  7.5 4.7 %collective-permute-start.11 = (bf16[8,1536]{1,0:T(8,128)(2,1)S(1)}, bf16[8,1536]{1,0:T(8,128)(2,1)S(1)}, u32[]{:S(2)}, u32[]{:S(2)}) collective-permute-start(bf16[8,1536]{1,0:T(8,128)(2,1)S(1)} %add.89), channel_id=1, source_target_pairs={{0,8},{1,9},{2,10},{3,11},{4,12},{5,13},{6,14},{7,15},{8,0},{9,1},... | collective-permute-start | bytes 73736 | tf_op jit(solution)/shard_map/ppermute | solution.py:19
  12.2 8.7 %collective-permute-start.16 = (bf16[8,1536]{1,0:T(8,128)(2,1)S(1)}, bf16[8,1536]{1,0:T(8,128)(2,1)S(1)}, u32[]{:S(2)}, u32[]{:S(2)}) collective-permute-start(bf16[8,1536]{1,0:T(8,128)(2,1)S(1)} %add_add_fusion.2), channel_id=1, source_target_pairs={{0,6},{1,7},{2,4},{3,5},{4,2},{5,3},{6,0},{7,1},{8,14},{9,15},{10,... | collective-permute-start | bytes 73736 | tf_op jit(solution)/shard_map/ppermute | solution.py:19
  17.7 7.7 %collective-permute-start.15 = (bf16[8,1536]{1,0:T(8,128)(2,1)S(1)}, bf16[8,1536]{1,0:T(8,128)(2,1)S(1)}, u32[]{:S(2)}, u32[]{:S(2)}) collective-permute-start(bf16[8,1536]{1,0:T(8,128)(2,1)S(1)} %add_add_fusion.2), channel_id=1, source_target_pairs={{0,4},{1,5},{2,6},{3,7},{4,0},{5,1},{6,2},{7,3},{8,12},{9,13},{10,... | collective-permute-start | bytes 73736 | tf_op jit(solution)/shard_map/ppermute | solution.py:19
  19.2 6.3 %collective-permute-start.14 = (bf16[8,1536]{1,0:T(8,128)(2,1)S(1)}, bf16[8,1536]{1,0:T(8,128)(2,1)S(1)}, u32[]{:S(2)}, u32[]{:S(2)}) collective-permute-start(bf16[8,1536]{1,0:T(8,128)(2,1)S(1)} %add_add_fusion.2), channel_id=1, source_target_pairs={{0,2},{1,3},{2,0},{3,1},{4,6},{5,7},{6,4},{7,5},{8,10},{9,11},{10,... | collective-permute-start | bytes 73736 | tf_op jit(solution)/shard_map/ppermute | solution.py:19
  46.1 49.9 %collective-permute-start.17 = (bf16[16,48,1536]{2,1,0:T(8,128)(2,1)}, bf16[16,48,1536]{2,1,0:T(8,128)(2,1)S(1)}, u32[]{:S(2)}, u32[]{:S(2)}) collective-permute-start(bf16[16,48,1536]{2,1,0:T(8,128)(2,1)} %get-tuple-element.40), channel_id=1, source_target_pairs={{0,1},{1,0},{2,3},{3,2},{4,5},{5,4},{6,7},{7,6},{8,9},{9,8},{10,11... | collective-permute-start | bytes 7077896 | tf_op jit(solution)/shard_map/ppermute | solution.py:19
  46.1 16.8 %collective-permute-start.1 = (bf16[48,1536]{1,0:T(8,128)(2,1)S(1)}, bf16[48,1536]{1,0:T(8,128)(2,1)S(1)}, u32[]{:S(2)}, u32[]{:S(2)}) collective-permute-start(bf16[48,1536]{1,0:T(8,128)(2,1)S(1)} %copy-done.9), channel_id=1, source_target_pairs={{0,4},{1,5},{2,6},{3,7},{4,0},{5,1},{6,2},{7,3},{8,12},{9,13},{10,... | collective-permute-start | bytes 442376 | tf_op jit(solution)/shard_map/ppermute | solution.py:19
  49.1 13.7 %collective-permute-start = (bf16[48,1536]{1,0:T(8,128)(2,1)S(1)}, bf16[48,1536]{1,0:T(8,128)(2,1)S(1)}, u32[]{:S(2)}, u32[]{:S(2)}) collective-permute-start(bf16[48,1536]{1,0:T(8,128)(2,1)S(1)} %copy-done.9), channel_id=1, source_target_pairs={{0,2},{1,3},{2,0},{3,1},{4,6},{5,7},{6,4},{7,5},{8,10},{9,11},{10,... | collective-permute-start | bytes 442376 | tf_op jit(solution)/shard_map/ppermute | solution.py:19
  50.6 14.8 %collective-permute-start.2 = (bf16[48,1536]{1,0:T(8,128)(2,1)S(1)}, bf16[48,1536]{1,0:T(8,128)(2,1)S(1)}, u32[]{:S(2)}, u32[]{:S(2)}) collective-permute-start(bf16[48,1536]{1,0:T(8,128)(2,1)S(1)} %copy-done.9), channel_id=1, source_target_pairs={{0,6},{1,7},{2,4},{3,5},{4,2},{5,3},{6,0},{7,1},{8,14},{9,15},{10,... | collective-permute-start | bytes 442376 | tf_op jit(solution)/shard_map/ppermute | solution.py:19
  65.4 29.2 %collective-permute-start.5 = (bf16[192,1536]{1,0:T(8,128)(2,1)S(1)}, bf16[192,1536]{1,0:T(8,128)(2,1)S(1)}, u32[]{:S(2)}, u32[]{:S(2)}) collective-permute-start(bf16[192,1536]{1,0:T(8,128)(2,1)S(1)} %constant_dynamic-update-slice_fusion.refs_0_), channel_id=1, source_target_pairs={{0,24},{1,25},{2,26},{3,27},{4,28},{5,29},{6,30},{7,31},{8,16},{9,... | collective-permute-start | bytes 1769480 | tf_op jit(solution)/shard_map/ppermute | solution.py:19
  66.8 27.8 %collective-permute-start.4 = (bf16[192,1536]{1,0:T(8,128)(2,1)S(1)}, bf16[192,1536]{1,0:T(8,128)(2,1)}, u32[]{:S(2)}, u32[]{:S(2)}) collective-permute-start(bf16[192,1536]{1,0:T(8,128)(2,1)S(1)} %constant_dynamic-update-slice_fusion.refs_0_), channel_id=1, source_target_pairs={{0,16},{1,17},{2,18},{3,19},{4,20},{5,21},{6,22},{7,23},{8,24},{9,... | collective-permute-start | bytes 1769480 | tf_op jit(solution)/shard_map/ppermute | solution.py:19
  67.9 27.4 %collective-permute-start.3 = (bf16[192,1536]{1,0:T(8,128)(2,1)S(1)}, bf16[192,1536]{1,0:T(8,128)(2,1)}, u32[]{:S(2)}, u32[]{:S(2)}) collective-permute-start(bf16[192,1536]{1,0:T(8,128)(2,1)S(1)} %constant_dynamic-update-slice_fusion.refs_0_), channel_id=1, source_target_pairs={{0,8},{1,9},{2,10},{3,11},{4,12},{5,13},{6,14},{7,15},{8,0},{9,1},... | collective-permute-start | bytes 1769480 | tf_op jit(solution)/shard_map/ppermute | solution.py:19
  69.6 34.0 %collective-permute-start.6 = (bf16[192,1536]{1,0:T(8,128)(2,1)S(1)}, bf16[192,1536]{1,0:T(8,128)(2,1)}, u32[]{:S(2)}, u32[]{:S(2)}) collective-permute-start(bf16[192,1536]{1,0:T(8,128)(2,1)S(1)} %constant_dynamic-update-slice_fusion.refs_0_), channel_id=1, source_target_pairs={{0,1},{1,0},{2,3},{3,2},{4,5},{5,4},{6,7},{7,6},{8,9},{9,8},{10,11... | collective-permute-start | bytes 1769480 | tf_op jit(solution)/shard_map/ppermute | solution.py:19
  94.6 11.6 %collective-permute-start.9 = (bf16[192,1536]{1,0:T(8,128)(2,1)S(1)}, bf16[192,1536]{1,0:T(8,128)(2,1)}, u32[]{:S(2)}, u32[]{:S(2)}) collective-permute-start(bf16[192,1536]{1,0:T(8,128)(2,1)S(1)} %collective-permute-done.5.refs_3_), channel_id=1, source_target_pairs={{0,1},{1,0},{2,3},{3,2},{4,5},{5,4},{6,7},{7,6},{8,9},{9,8},{10,11... | collective-permute-start | bytes 1769480 | tf_op jit(solution)/shard_map/ppermute | solution.py:19
  94.6 13.5 %collective-permute-start.8 = (bf16[192,1536]{1,0:T(8,128)(2,1)}, bf16[192,1536]{1,0:T(8,128)(2,1)}, u32[]{:S(2)}, u32[]{:S(2)}) collective-permute-start(bf16[192,1536]{1,0:T(8,128)(2,1)} %collective-permute-done.4.refs_2_), channel_id=1, source_target_pairs={{0,1},{1,0},{2,3},{3,2},{4,5},{5,4},{6,7},{7,6},{8,9},{9,8},{10,11... | collective-permute-start | bytes 1769480 | tf_op jit(solution)/shard_map/ppermute | solution.py:19
  95.4 14.3 %collective-permute-start.7 = (bf16[192,1536]{1,0:T(8,128)(2,1)}, bf16[192,1536]{1,0:T(8,128)(2,1)}, u32[]{:S(2)}, u32[]{:S(2)}) collective-permute-start(bf16[192,1536]{1,0:T(8,128)(2,1)} %collective-permute-done.3.refs_1_), channel_id=1, source_target_pairs={{0,1},{1,0},{2,3},{3,2},{4,5},{5,4},{6,7},{7,6},{8,9},{9,8},{10,11... | collective-permute-start | bytes 1769480 | tf_op jit(solution)/shard_map/ppermute | solution.py:19
  103.3 10.1 %collective-permute-start.18 = (bf16[2,48,1536]{2,1,0:T(8,128)(2,1)}, bf16[2,48,1536]{2,1,0:T(8,128)(2,1)S(1)}, u32[]{:S(2)}, u32[]{:S(2)}) collective-permute-start(bf16[2,48,1536]{2,1,0:T(8,128)(2,1)} %get-tuple-element.42), channel_id=1, source_target_pairs={{0,8},{1,9},{2,10},{3,11},{4,12},{5,13},{6,14},{7,15},{8,0},{9,1},... | collective-permute-start | bytes 884744 | tf_op jit(solution)/shard_map/ppermute | solution.py:19
  103.7 44.7 %collective-permute-start.19 = (bf16[2,48,1536]{2,1,0:T(8,128)(2,1)}, bf16[2,48,1536]{2,1,0:T(8,128)(2,1)S(1)}, u32[]{:S(2)}, u32[]{:S(2)}) collective-permute-start(bf16[2,48,1536]{2,1,0:T(8,128)(2,1)} %get-tuple-element.43), channel_id=1, source_target_pairs={{0,16},{1,17},{2,18},{3,19},{4,20},{5,21},{6,22},{7,23},{8,24},{9,... | collective-permute-start | bytes 884744 | tf_op jit(solution)/shard_map/ppermute | solution.py:19
  106.2 42.2 %collective-permute-start.20 = (bf16[2,48,1536]{2,1,0:T(8,128)(2,1)}, bf16[2,48,1536]{2,1,0:T(8,128)(2,1)S(1)}, u32[]{:S(2)}, u32[]{:S(2)}) collective-permute-start(bf16[2,48,1536]{2,1,0:T(8,128)(2,1)} %get-tuple-element.44), channel_id=1, source_target_pairs={{0,24},{1,25},{2,26},{3,27},{4,28},{5,29},{6,30},{7,31},{8,16},{9,... | collective-permute-start | bytes 884744 | tf_op jit(solution)/shard_map/ppermute | solution.py:19
  108.1 40.3 %collective-permute-start.21 = (bf16[4,2,48,384]{3,2,1,0:T(8,128)(2,1)}, bf16[4,2,48,384]{3,2,1,0:T(8,128)(2,1)S(1)}, u32[]{:S(2)}, u32[]{:S(2)}) collective-permute-start(bf16[4,2,48,384]{3,2,1,0:T(8,128)(2,1)} %get-tuple-element.46), channel_id=1, source_target_pairs={{0,32},{32,0},{64,96},{96,64},{128,160},{160,128},{192,224},{224,1... | collective-permute-start | bytes 884744 | tf_op jit(solution)/shard_map/ppermute | solution.py:24
  109.6 38.8 %collective-permute-start.22 = (bf16[4,2,48,384]{3,2,1,0:T(8,128)(2,1)}, bf16[4,2,48,384]{3,2,1,0:T(8,128)(2,1)S(1)}, u32[]{:S(2)}, u32[]{:S(2)}) collective-permute-start(bf16[4,2,48,384]{3,2,1,0:T(8,128)(2,1)} %get-tuple-element.47), channel_id=1, source_target_pairs={{0,64},{32,96},{64,0},{96,32},{128,192},{160,224},{192,128},{224,1... | collective-permute-start | bytes 884744 | tf_op jit(solution)/shard_map/ppermute | solution.py:24
  113.3 35.1 %collective-permute-start.23 = (bf16[4,2,48,384]{3,2,1,0:T(8,128)(2,1)}, bf16[4,2,48,384]{3,2,1,0:T(8,128)(2,1)S(1)}, u32[]{:S(2)}, u32[]{:S(2)}) collective-permute-start(bf16[4,2,48,384]{3,2,1,0:T(8,128)(2,1)} %get-tuple-element.48), channel_id=1, source_target_pairs={{0,96},{32,64},{64,32},{96,0},{128,224},{160,192},{192,160},{224,1... | collective-permute-start | bytes 884744 | tf_op jit(solution)/shard_map/ppermute | solution.py:24
  153.3 13.2 %collective-permute-start.24 = (f32[2,48,384]{2,1,0:T(8,128)}, f32[2,48,384]{2,1,0:T(8,128)S(1)}, u32[]{:S(2)}, u32[]{:S(2)}) collective-permute-start(f32[2,48,384]{2,1,0:T(8,128)} %get-tuple-element.50), channel_id=1, source_target_pairs={{0,32},{32,0},{64,96},{96,64},{128,160},{160,128},{192,224},{224,1... | collective-permute-start | bytes 442376 | tf_op jit(solution)/shard_map/ppermute | solution.py:24
  153.7 1.3 collective-permute-start.37
  155.0 5.9 %collective-permute-start.40 = (f32[8,1536]{1,0:T(8,128)S(1)}, f32[8,1536]{1,0:T(8,128)S(1)}, u32[]{:S(2)}, u32[]{:S(2)}) collective-permute-start(f32[8,1536]{1,0:T(8,128)S(1)} %add.100), channel_id=1, source_target_pairs={{0,24},{1,25},{2,26},{3,27},{4,28},{5,29},{6,30},{7,31},{8,16},{9,... | collective-permute-start | bytes 147464 | tf_op jit(solution)/shard_map/ppermute | solution.py:19
  156.4 7.3 %collective-permute-start.39 = (f32[8,1536]{1,0:T(8,128)S(1)}, f32[8,1536]{1,0:T(8,128)S(1)}, u32[]{:S(2)}, u32[]{:S(2)}) collective-permute-start(f32[8,1536]{1,0:T(8,128)S(1)} %add.100), channel_id=1, source_target_pairs={{0,16},{1,17},{2,18},{3,19},{4,20},{5,21},{6,22},{7,23},{8,24},{9,... | collective-permute-start | bytes 147464 | tf_op jit(solution)/shard_map/ppermute | solution.py:19
  157.4 6.5 %collective-permute-start.38 = (f32[8,1536]{1,0:T(8,128)S(1)}, f32[8,1536]{1,0:T(8,128)S(1)}, u32[]{:S(2)}, u32[]{:S(2)}) collective-permute-start(f32[8,1536]{1,0:T(8,128)S(1)} %add.100), channel_id=1, source_target_pairs={{0,8},{1,9},{2,10},{3,11},{4,12},{5,13},{6,14},{7,15},{8,0},{9,1},... | collective-permute-start | bytes 147464 | tf_op jit(solution)/shard_map/ppermute | solution.py:19
  159.2 9.2 %collective-permute-start.25 = (f32[2,48,384]{2,1,0:T(8,128)}, f32[2,48,384]{2,1,0:T(8,128)S(1)}, u32[]{:S(2)}, u32[]{:S(2)}) collective-permute-start(f32[2,48,384]{2,1,0:T(8,128)} %get-tuple-element.51), channel_id=1, source_target_pairs={{0,64},{32,96},{64,0},{96,32},{128,192},{160,224},{192,128},{224,1... | collective-permute-start | bytes 442376 | tf_op jit(solution)/shard_map/ppermute | solution.py:24
  160.9 9.4 %collective-permute-start.26 = (f32[2,48,384]{2,1,0:T(8,128)}, f32[2,48,384]{2,1,0:T(8,128)S(1)}, u32[]{:S(2)}, u32[]{:S(2)}) collective-permute-start(f32[2,48,384]{2,1,0:T(8,128)} %get-tuple-element.52), channel_id=1, source_target_pairs={{0,96},{32,64},{64,32},{96,0},{128,224},{160,192},{192,160},{224,1... | collective-permute-start | bytes 442376 | tf_op jit(solution)/shard_map/ppermute | solution.py:24
  163.7 9.6 %collective-permute-start.27 = (f32[2,48,384]{2,1,0:T(8,128)}, f32[2,48,384]{2,1,0:T(8,128)S(1)}, u32[]{:S(2)}, u32[]{:S(2)}) collective-permute-start(f32[2,48,384]{2,1,0:T(8,128)} %get-tuple-element.54), channel_id=1, source_target_pairs={{0,8},{1,9},{2,10},{3,11},{4,12},{5,13},{6,14},{7,15},{8,0},{9,1},... | collective-permute-start | bytes 442376 | tf_op jit(solution)/shard_map/ppermute | solution.py:19
  163.9 11.3 %collective-permute-start.28 = (f32[2,48,384]{2,1,0:T(8,128)}, f32[2,48,384]{2,1,0:T(8,128)S(1)}, u32[]{:S(2)}, u32[]{:S(2)}) collective-permute-start(f32[2,48,384]{2,1,0:T(8,128)} %get-tuple-element.55), channel_id=1, source_target_pairs={{0,16},{1,17},{2,18},{3,19},{4,20},{5,21},{6,22},{7,23},{8,24},{9,... | collective-permute-start | bytes 442376 | tf_op jit(solution)/shard_map/ppermute | solution.py:19
  166.5 8.8 %collective-permute-start.29 = (f32[2,48,384]{2,1,0:T(8,128)}, f32[2,48,384]{2,1,0:T(8,128)S(1)}, u32[]{:S(2)}, u32[]{:S(2)}) collective-permute-start(f32[2,48,384]{2,1,0:T(8,128)} %get-tuple-element.56), channel_id=1, source_target_pairs={{0,24},{1,25},{2,26},{3,27},{4,28},{5,29},{6,30},{7,31},{8,16},{9,... | collective-permute-start | bytes 442376 | tf_op jit(solution)/shard_map/ppermute | solution.py:19
  168.4 14.2 %collective-permute-start.43 = (f32[8,1536]{1,0:T(8,128)S(1)}, f32[8,1536]{1,0:T(8,128)S(1)}, u32[]{:S(2)}, u32[]{:S(2)}) collective-permute-start(f32[8,1536]{1,0:T(8,128)S(1)} %add_add_fusion.1), channel_id=1, source_target_pairs={{0,6},{1,7},{2,4},{3,5},{4,2},{5,3},{6,0},{7,1},{8,14},{9,15},{10,... | collective-permute-start | bytes 147464 | tf_op jit(solution)/shard_map/ppermute | solution.py:19
  170.3 14.9 %collective-permute-start.42 = (f32[8,1536]{1,0:T(8,128)S(1)}, f32[8,1536]{1,0:T(8,128)S(1)}, u32[]{:S(2)}, u32[]{:S(2)}) collective-permute-start(f32[8,1536]{1,0:T(8,128)S(1)} %add_add_fusion.1), channel_id=1, source_target_pairs={{0,4},{1,5},{2,6},{3,7},{4,0},{5,1},{6,2},{7,3},{8,12},{9,13},{10,... | collective-permute-start | bytes 147464 | tf_op jit(solution)/shard_map/ppermute | solution.py:19
  173.2 12.0 %collective-permute-start.41 = (f32[8,1536]{1,0:T(8,128)S(1)}, f32[8,1536]{1,0:T(8,128)S(1)}, u32[]{:S(2)}, u32[]{:S(2)}) collective-permute-start(f32[8,1536]{1,0:T(8,128)S(1)} %add_add_fusion.1), channel_id=1, source_target_pairs={{0,2},{1,3},{2,0},{3,1},{4,6},{5,7},{6,4},{7,5},{8,10},{9,11},{10,... | collective-permute-start | bytes 147464 | tf_op jit(solution)/shard_map/ppermute | solution.py:19
  178.7 8.0 %collective-permute-start.30 = (f32[48,384]{1,0:T(8,128)}, f32[48,384]{1,0:T(8,128)S(1)}, u32[]{:S(2)}, u32[]{:S(2)}) collective-permute-start(f32[48,384]{1,0:T(8,128)} %get-tuple-element.58), channel_id=1, source_target_pairs={{0,2},{1,3},{2,0},{3,1},{4,6},{5,7},{6,4},{7,5},{8,10},{9,11},{10,... | collective-permute-start | bytes 221192 | tf_op jit(solution)/shard_map/ppermute | solution.py:19
  179.6 9.8 %collective-permute-start.31 = (f32[48,384]{1,0:T(8,128)}, f32[48,384]{1,0:T(8,128)S(1)}, u32[]{:S(2)}, u32[]{:S(2)}) collective-permute-start(f32[48,384]{1,0:T(8,128)} %get-tuple-element.59), channel_id=1, source_target_pairs={{0,4},{1,5},{2,6},{3,7},{4,0},{5,1},{6,2},{7,3},{8,12},{9,13},{10,... | collective-permute-start | bytes 221192 | tf_op jit(solution)/shard_map/ppermute | solution.py:19
  182.7 8.0 %collective-permute-start.32 = (f32[48,384]{1,0:T(8,128)}, f32[48,384]{1,0:T(8,128)S(1)}, u32[]{:S(2)}, u32[]{:S(2)}) collective-permute-start(f32[48,384]{1,0:T(8,128)} %get-tuple-element.60), channel_id=1, source_target_pairs={{0,6},{1,7},{2,4},{3,5},{4,2},{5,3},{6,0},{7,1},{8,14},{9,15},{10,... | collective-permute-start | bytes 221192 | tf_op jit(solution)/shard_map/ppermute | solution.py:19
  185.3 6.5 %collective-permute-start.45 = (f32[8,48]{1,0:T(8,128)S(1)}, f32[8,48]{1,0:T(8,128)S(1)}, u32[]{:S(2)}, u32[]{:S(2)}) collective-permute-start(f32[8,48]{1,0:T(8,128)S(1)} %fusion), channel_id=1, source_target_pairs={{0,64},{32,96},{64,0},{96,32},{128,192},{160,224},{192,128},{224,1... | collective-permute-start | bytes 4616 | tf_op jit(solution)/shard_map/ppermute | solution.py:24
  185.9 5.9 %collective-permute-start.44 = (f32[8,48]{1,0:T(8,128)S(1)}, f32[8,48]{1,0:T(8,128)S(1)}, u32[]{:S(2)}, u32[]{:S(2)}) collective-permute-start(f32[8,48]{1,0:T(8,128)S(1)} %fusion), channel_id=1, source_target_pairs={{0,32},{32,0},{64,96},{96,64},{128,160},{160,128},{192,224},{224,1... | collective-permute-start | bytes 4616 | tf_op jit(solution)/shard_map/ppermute | solution.py:24
  186.7 5.1 %collective-permute-start.46 = (f32[8,48]{1,0:T(8,128)S(1)}, f32[8,48]{1,0:T(8,128)S(1)}, u32[]{:S(2)}, u32[]{:S(2)}) collective-permute-start(f32[8,48]{1,0:T(8,128)S(1)} %fusion), channel_id=1, source_target_pairs={{0,96},{32,64},{64,32},{96,0},{128,224},{160,192},{192,160},{224,1... | collective-permute-start | bytes 4616 | tf_op jit(solution)/shard_map/ppermute | solution.py:24
  191.6 4.4 %collective-permute-start.33 = (f32[48,384]{1,0:T(8,128)S(1)}, f32[48,384]{1,0:T(8,128)S(1)}, u32[]{:S(2)}, u32[]{:S(2)}) collective-permute-start(f32[48,384]{1,0:T(8,128)S(1)} %add_add_fusion), channel_id=1, source_target_pairs={{0,128},{32,160},{64,192},{96,224},{128,0},{160,32},{192,64},{224,... | collective-permute-start | bytes 221192 | tf_op jit(solution)/shard_map/ppermute | solution.py:24
  191.8 19.4 %collective-permute-start.47 = (f32[8,48]{1,0:T(8,128)S(1)}, f32[8,48]{1,0:T(8,128)S(1)}, u32[]{:S(2)}, u32[]{:S(2)}) collective-permute-start(f32[8,48]{1,0:T(8,128)S(1)} %add_add_fusion.3), channel_id=1, source_target_pairs={{0,128},{32,160},{64,192},{96,224},{128,0},{160,32},{192,64},{224,... | collective-permute-start | bytes 4616 | tf_op jit(solution)/shard_map/ppermute | solution.py:24
  196.1 15.8 %collective-permute-start.36 = (f32[48,384]{1,0:T(8,128)S(1)}, f32[48,384]{1,0:T(8,128)S(1)}, u32[]{:S(2)}, u32[]{:S(2)}) collective-permute-start(f32[48,384]{1,0:T(8,128)S(1)} %add.99.v0), channel_id=1, source_target_pairs={{0,96},{32,64},{64,32},{96,0},{128,224},{160,192},{192,160},{224,1... | collective-permute-start | bytes 221192 | tf_op jit(solution)/shard_map/ppermute | solution.py:24
  196.7 15.1 %collective-permute-start.35 = (f32[48,384]{1,0:T(8,128)S(1)}, f32[48,384]{1,0:T(8,128)S(1)}, u32[]{:S(2)}, u32[]{:S(2)}) collective-permute-start(f32[48,384]{1,0:T(8,128)S(1)} %add.99.v0), channel_id=1, source_target_pairs={{0,64},{32,96},{64,0},{96,32},{128,192},{160,224},{192,128},{224,1... | collective-permute-start | bytes 221192 | tf_op jit(solution)/shard_map/ppermute | solution.py:24
  198.7 13.2 %collective-permute-start.34 = (f32[48,384]{1,0:T(8,128)S(1)}, f32[48,384]{1,0:T(8,128)S(1)}, u32[]{:S(2)}, u32[]{:S(2)}) collective-permute-start(f32[48,384]{1,0:T(8,128)S(1)} %add.99.v0), channel_id=1, source_target_pairs={{0,32},{32,0},{64,96},{96,64},{128,160},{160,128},{192,224},{224,1... | collective-permute-start | bytes 221192 | tf_op jit(solution)/shard_map/ppermute | solution.py:24
  (23 other events, 166.6 us)

commit v2 on v1

v2 whole, which is shorter than its diff:
```python
import functools

import jax
import jax.numpy as jnp
from jax import lax
from jax.experimental import pallas as pl
from jax.experimental.pallas import tpu as pltpu
from jax.sharding import PartitionSpec as P

TAPS = 5
NX, NY, NZ = 4, 4, 4
F32, BF16 = jnp.float32, jnp.bfloat16
PAD = 8
HBM = pl.BlockSpec(memory_space=pl.ANY)
VMEM_LIMIT = 60 * 1024 * 1024


def fsdp_move(value, y=0, z=0, core=0):
    perm = [(i, i ^ (y * 8 + z * 2 + core)) for i in range(32)]
    return lax.ppermute(value, "fsdp", perm)


def dp_move(value, x=0, low=0):
    perm = [(i, i ^ (low * 4 + x)) for i in range(8)]
    return lax.ppermute(value, "dp", perm)


def params(micros):
    return dict(
        cost_estimate=pl.CostEstimate(flops=0, bytes_accessed=int(micros * 3.6e6), transcendentals=0),
    )


def compiler():
    return pltpu.CompilerParams(vmem_limit_bytes=VMEM_LIMIT)


def shifted(near, by, count):
    if by != 0:
        near = pltpu.roll(near, (-by) % near.shape[0], 0)
    return near[PAD : PAD + count]


def sds(shape, dtype):
    return jax.ShapeDtypeStruct(shape, dtype)


def whole(shape):
    return pl.BlockSpec(shape, lambda *_: (0,) * len(shape))


def forward_kernel(lens, par, glu, swished, normed, rstds, masked, *, rows, frames, chunk, unroll):
    step = pl.program_id(0)
    length = lens[0]
    width = glu.shape[1]

    @pl.when(step == 0)
    def _():
        masked[pl.ds(0, PAD), :] = jnp.zeros((PAD, width), F32)
        masked[pl.ds(PAD + frames, PAD), :] = jnp.zeros((PAD, width), F32)

        def fill(i, _):
            at = pl.multiple_of(i * 16, 16)
            ids = at + lax.broadcasted_iota(jnp.int32, (16, 1), 0)
            v = glu[pl.ds(at, 16), :].astype(F32)
            masked[pl.ds(pl.multiple_of(at + PAD, 8), 16), :] = jnp.where(ids < length, v, 0.0)
            return 0

        lax.fori_loop(0, frames // 16, fill, 0, unroll=4)

    def one(i, _):
        local = pl.multiple_of(i * chunk, chunk)
        base = step * rows + local
        near = masked[pl.ds(pl.multiple_of(base, 8), chunk + 2 * PAD), :]
        conv = par[0:1, :] * shifted(near, -2, chunk)
        for k in range(1, TAPS):
            conv = conv + par[k : k + 1, :] * shifted(near, k - 2, chunk)
        mean = jnp.sum(conv, axis=1, keepdims=True) * (1.0 / width)
        cent = conv - mean
        var = jnp.sum(cent * cent, axis=1, keepdims=True) * (1.0 / width)
        rstd = lax.rsqrt(var + 1e-05)
        norm = cent * rstd
        pre = norm * par[5:6, :] + par[6:7, :]
        sig = 0.5 * jnp.tanh(0.5 * pre) + 0.5
        ids = base + lax.broadcasted_iota(jnp.int32, (chunk, 1), 0)
        out = jnp.where(ids < length, pre * sig, 0.0)
        swished[pl.ds(local, chunk), :] = out.astype(BF16)
        normed[pl.ds(local, chunk), :] = norm
        rstds[pl.ds(local, chunk), :] = jnp.broadcast_to(rstd, (chunk, 128))
        return 0

    lax.fori_loop(0, rows // chunk, one, 0, unroll=unroll)


def forward(lens, par, glu, rows=128, chunk=16, unroll=8):
    frames, width = glu.shape
    block = lambda w: pl.BlockSpec((rows, w), lambda i, *_: (i, 0))
    return pl.pallas_call(
        functools.partial(forward_kernel, rows=rows, frames=frames, chunk=chunk, unroll=unroll),
        out_shape=(sds((frames, width), BF16), sds((frames, width), F32), sds((frames, 128), F32)),
        grid_spec=pltpu.PrefetchScalarGridSpec(
            num_scalar_prefetch=1,
            grid=(frames // rows,),
            in_specs=[whole((8, width)), whole((frames, width))],
            out_specs=(block(width), block(width), block(128)),
            scratch_shapes=[pltpu.VMEM((frames + 2 * PAD, width), F32)],
        ),
        compiler_params=compiler(),
        name="forward",
        **params(0.1),
    )(lens, par, glu)


def outer_kernel(core, sw, cot, h1, h2, h3, keep, send):
    res = lax.dot_general(
        sw[...], cot[...], (((0,), (0,)), ((), ())), preferred_element_type=F32
    )
    first = core[0] == 0
    for j in range(4):
        a = res[j * 96 : j * 96 + 48]
        b = res[j * 96 + 48 : j * 96 + 96]
        keep[j] = jnp.where(first, a, b)
        send[j] = jnp.where(first, b, a).astype(BF16)


def outer(core, sw, cot, held):
    frames, width = sw.shape
    return pl.pallas_call(
        outer_kernel,
        out_shape=(sds((16, 48, width), F32), sds((16, 48, width), BF16)),
        grid_spec=pltpu.PrefetchScalarGridSpec(
            num_scalar_prefetch=1,
            grid=(4,),
            in_specs=[
                pl.BlockSpec((frames, 384), lambda i, *_: (0, i)),
                whole((frames, width)),
                HBM,
                HBM,
                HBM,
            ],
            out_specs=(
                pl.BlockSpec((4, 48, width), lambda i, *_: (i, 0, 0)),
                pl.BlockSpec((4, 48, width), lambda i, *_: (i, 0, 0)),
            ),
        ),
        compiler_params=compiler(),
        name="outer",
        **params(0.1),
    )(core, sw, cot, *held)


def stage1_kernel(pos, keep, recv, a0, a1, a2, a3):
    j = pl.program_id(0)
    for n, out in enumerate((a0, a1, a2, a3)):

        @pl.when(j == n)
        def _(out=out):
            out[...] = (keep[0] + recv[0].astype(F32)).astype(out.dtype)


def stage1(pos, keep, recv):
    width = keep.shape[-1]
    keep = keep.reshape(4, 4, 48, width)
    recv = recv.reshape(4, 4, 48, width)
    src = pl.BlockSpec((1, 4, 48, width), lambda j, pos: (pos[0] ^ j, 0, 0, 0))
    return pl.pallas_call(
        stage1_kernel,
        out_shape=tuple(sds((4, 48, width), t) for t in (F32, BF16, BF16, BF16)),
        grid_spec=pltpu.PrefetchScalarGridSpec(
            num_scalar_prefetch=1,
            grid=(4,),
            in_specs=[src, src],
            out_specs=(whole((4, 48, width)),) * 4,
        ),
        compiler_params=compiler(),
        name="stage1",
        **params(0.1),
    )(pos, keep, recv)


def stage2_kernel(pos, a0, a1, a2, a3, held, o0, o1, o2, o3):
    j = pl.program_id(0)
    for n, out in enumerate((o0, o1, o2, o3)):

        @pl.when(j == n)
        def _(out=out):
            total = (a0[0] + a1[0].astype(F32)) + (a2[0].astype(F32) + a3[0].astype(F32))
            out[...] = total.astype(out.dtype)


def stage2(pos, a, held):
    width = a[0].shape[-1]
    src = pl.BlockSpec((1, 48, width), lambda j, pos: (pos[2] ^ j, 0, 0))
    return pl.pallas_call(
        stage2_kernel,
        out_shape=tuple(sds((48, width), t) for t in (F32, BF16, BF16, BF16)),
        grid_spec=pltpu.PrefetchScalarGridSpec(
            num_scalar_prefetch=1,
            grid=(4,),
            in_specs=[src] * 4 + [HBM],
            out_specs=(whole((48, width)),) * 4,
        ),
        compiler_params=compiler(),
        name="stage2",
        **params(3),
    )(pos, *a, held)


def stage3_kernel(pos, v0, v1, v2, v3, held, o0, o1, o2, o3, total):
    total[...] = (v0[...] + v1[...].astype(F32)) + (v2[...].astype(F32) + v3[...].astype(F32))
    for n, out in enumerate((o0, o1, o2, o3)):
        at = pl.multiple_of((pos[1] ^ n) * 384, 128)
        out[...] = total[:, pl.ds(at, 384)]


def stage3(pos, v, held):
    shape = v[0].shape
    part = (shape[0], 384)
    return pl.pallas_call(
        stage3_kernel,
        out_shape=(sds(part, F32),) * 4,
        grid_spec=pltpu.PrefetchScalarGridSpec(
            num_scalar_prefetch=1,
            grid=(1,),
            in_specs=[whole(shape)] * 4 + [HBM],
            out_specs=(whole(part),) * 4,
            scratch_shapes=[pltpu.VMEM(shape, F32)],
        ),
        compiler_params=compiler(),
        name="stage3",
        **params(2),
    )(pos, *v, held)


def join_kernel(pos, v0, v1, v2, v3, out):
    for n, v in enumerate((v0, v1, v2, v3)):
        at = pl.multiple_of((pos[1] ^ n) * 384, 128)
        out[:, pl.ds(at, 384)] = v[...]


def join(pos, parts):
    rows = parts[0].shape[0]
    return pl.pallas_call(
        join_kernel,
        out_shape=sds((rows, 1536), F32),
        grid_spec=pltpu.PrefetchScalarGridSpec(
            num_scalar_prefetch=1,
            grid=(1,),
            in_specs=[whole((rows, 384))] * 4,
            out_specs=whole((rows, 1536)),
        ),
        compiler_params=compiler(),
        name="join",
        **params(2),
    )(pos, *parts)


def gather_kernel(w0, w1, w2, w3, held, out):
    rows = w0.shape[0]
    for n, w in enumerate((w0, w1, w2, w3)):
        out[n * rows : n * rows + rows, :] = w[...]


def gather(w, held):
    rows, width = w[0].shape
    return pl.pallas_call(
        gather_kernel,
        out_shape=sds((4 * rows, width), BF16),
        grid=(1,),
        in_specs=[whole((rows, width))] * 4 + [HBM],
        out_specs=whole((4 * rows, width)),
        compiler_params=compiler(),
        name="gather",
        **params(0.1),
    )(*w, held)


def fetch_weight(pos, pieces, buf, sem):
    y, z, core = pos[0], pos[2], pos[3]
    copies = []
    for n, piece in enumerate(pieces):
        for j in range(16):
            index = ((y ^ (j // 4)) * 4 + (z ^ (j % 4))) * 2 + (core ^ n)
            at = pl.multiple_of(index * 48, 48)
            copies.append(
                pltpu.make_async_copy(
                    piece.at[pl.ds(j * 48, 48), :], buf.at[pl.ds(at, 48), :], sem.at[n * 16 + j]
                )
            )
    for c in copies:
        c.start()
    for c in copies:
        c.wait()


def project_kernel(pos, *refs):
    pieces, (sw, res, _, _, out, buf, sem) = refs[:2], refs[2:]

    @pl.when(pl.program_id(0) == 0)
    def _():
        fetch_weight(pos, pieces, buf, sem)

    prod = jnp.dot(sw[...], buf[...], preferred_element_type=F32)
    out[...] = (res[...].astype(F32) + prod).astype(BF16)


def project(pos, pieces, sw, res, held, rows=256):
    frames, width = sw.shape
    block = pl.BlockSpec((rows, width), lambda i, *_: (i, 0))
    return pl.pallas_call(
        project_kernel,
        out_shape=sds((frames, width), BF16),
        grid_spec=pltpu.PrefetchScalarGridSpec(
            num_scalar_prefetch=1,
            grid=(frames // rows,),
            in_specs=[HBM] * 2 + [block, block, HBM, HBM],
            out_specs=block,
            scratch_shapes=[pltpu.VMEM((width, width), BF16), pltpu.SemaphoreType.DMA((32,))],
        ),
        compiler_params=compiler(),
        name="project",
        **params(11),
    )(pos, *pieces, sw, res, *held)


def backward_kernel(pos, *refs, rows, chunk, unroll):
    pieces = refs[:2]
    par, cot, nrm, rst, _, gconv, sums, buf, sem, grad = refs[2:]
    step = pl.program_id(0)
    width = cot.shape[1]
    length = pos[4]

    @pl.when(step == 0)
    def _():
        fetch_weight(pos, pieces, buf, sem)
        sums[...] = jnp.zeros_like(sums)

    grad[...] = lax.dot_general(
        cot[...], buf[...], (((1,), (1,)), ((), ())), preferred_element_type=F32
    )

    def one(i, _):
        at = pl.multiple_of(i * chunk, chunk)
        gain = par[5:6, :]
        norm = nrm[pl.ds(at, chunk), :]
        pre = norm * gain + par[6:7, :]
        sig = 0.5 * jnp.tanh(0.5 * pre) + 0.5
        ids = step * rows + at + lax.broadcasted_iota(jnp.int32, (chunk, 1), 0)
        gs = jnp.where(ids < length, grad[pl.ds(at, chunk), :], 0.0)
        gpre = gs * (sig * (1.0 + pre * (1.0 - sig)))
        gn = gpre * norm
        for h in range(chunk // 8):
            sums[0] += gn[h * 8 : h * 8 + 8]
            sums[1] += gpre[h * 8 : h * 8 + 8]
        gnorm = gpre * gain
        m1 = jnp.sum(gnorm, axis=1, keepdims=True) * (1.0 / width)
        m2 = jnp.sum(gnorm * norm, axis=1, keepdims=True) * (1.0 / width)
        gconv[pl.ds(at, chunk), :] = rst[pl.ds(at, chunk), 0:1] * (gnorm - m1 - norm * m2)
        return 0

    lax.fori_loop(0, rows // chunk, one, 0, unroll=unroll)


def backward(pos, pieces, par, cot, nrm, rst, held, rows=256, chunk=16, unroll=4):
    frames, width = cot.shape
    block = lambda w: pl.BlockSpec((rows, w), lambda i, *_: (i, 0))
    return pl.pallas_call(
        functools.partial(backward_kernel, rows=rows, chunk=chunk, unroll=unroll),
        out_shape=(sds((frames, width), F32), sds((2, 8, width), F32)),
        grid_spec=pltpu.PrefetchScalarGridSpec(
            num_scalar_prefetch=1,
            grid=(frames // rows,),
            in_specs=[HBM] * 2
            + [whole((8, width)), block(width), block(width), block(128), HBM],
            out_specs=(block(width), whole((2, 8, width))),
            scratch_shapes=[
                pltpu.VMEM((width, width), BF16),
                pltpu.SemaphoreType.DMA((32,)),
                pltpu.VMEM((rows, width), F32),
            ],
        ),
        compiler_params=compiler(),
        name="backward",
        **params(21),
    )(pos, *pieces, par, cot, nrm, rst, held)


def taps_kernel(pos, par, glu, gconv, norm_sums, out, small, pad, sums, *, rows, frames, chunk, unroll, strip):
    step = pl.program_id(0)
    width = glu.shape[1]
    length = pos[4]

    @pl.when(step == 0)
    def _():
        sums[...] = jnp.zeros_like(sums)
        pad[pl.ds(0, PAD), :] = jnp.zeros((PAD, width), F32)
        pad[pl.ds(PAD + frames, PAD), :] = jnp.zeros((PAD, width), F32)

    @pl.when(step < frames // rows)
    def _():
        pad[pl.ds(pl.multiple_of(PAD + step * rows, 8), rows), :] = gconv[...]

    @pl.when(step > 0)
    def _():
        start = (step - 1) * rows
        for c in range(0, width, strip):
            cols = slice(c, c + strip)

            def one(i, acc, cols=cols):
                at = pl.multiple_of(i * chunk, chunk)
                base = pl.multiple_of(start + at, 8)
                live = base + lax.broadcasted_iota(jnp.int32, (chunk, 1), 0) < length
                mk = jnp.where(live, glu[pl.ds(at, chunk), cols].astype(F32), 0.0)
                near = pad[pl.ds(base, chunk + 2 * PAD), cols]
                grad, new = None, []
                for k in range(TAPS):
                    g = shifted(near, 2 - k, chunk)
                    term = par[k : k + 1, cols] * g
                    grad = term if grad is None else grad + term
                    p = mk * g
                    new.append(acc[k] + sum(p[h : h + 8] for h in range(0, chunk, 8)))
                out[pl.ds(at, chunk), cols] = jnp.where(live, grad, 0.0).astype(BF16)
                return tuple(new)

            zero = jnp.zeros((8, strip), F32)
            acc = lax.fori_loop(0, rows // chunk, one, (zero,) * TAPS, unroll=unroll)
            for k in range(TAPS):
                sums[k, :, cols] += acc[k]

    @pl.when(step == frames // rows)
    def _():
        for k in range(TAPS):
            small[k : k + 1, :] = jnp.sum(sums[k], axis=0, keepdims=True)
        for k in range(2):
            small[TAPS + k : TAPS + k + 1, :] = jnp.sum(norm_sums[k], axis=0, keepdims=True)
        small[TAPS + 2 :, :] = jnp.zeros((1, width), F32)


def taps(pos, par, glu, gconv, norm_sums, rows=128, chunk=32, unroll=2, strip=256):
    frames, width = glu.shape
    last = frames // rows - 1
    late = pl.BlockSpec((rows, width), lambda i, *_: (jnp.maximum(i - 1, 0), 0))
    return pl.pallas_call(
        functools.partial(taps_kernel, rows=rows, frames=frames, chunk=chunk, unroll=unroll, strip=strip),
        out_shape=(sds((frames, width), BF16), sds((8, width), F32)),
        grid_spec=pltpu.PrefetchScalarGridSpec(
            num_scalar_prefetch=1,
            grid=(frames // rows + 1,),
            in_specs=[
                whole((8, width)),
                late,
                pl.BlockSpec((rows, width), lambda i, *_: (jnp.minimum(i, last), 0)),
                whole((2, 8, width)),
            ],
            out_specs=(late, whole((8, width))),
            scratch_shapes=[pltpu.VMEM((frames + 2 * PAD, width), F32), pltpu.VMEM((TAPS, 8, width), F32)],
        ),
        compiler_params=compiler(),
        name="taps",
        **params(10),
    )(pos, par, glu, gconv, norm_sums)


def local(glu_out, residual_in, cotangent, lengths, conv_kernel, norm_gain, norm_bias, proj_weight):
    _, frames, width = glu_out.shape
    glu, res, cot = glu_out[0], residual_in[0], cotangent[0]
    f, d = lax.axis_index("fsdp"), lax.axis_index("dp")
    core, z, y = f % 2, (f // 2) % 4, f // 8
    x = d % 4
    pos = jnp.stack([y, x, z, core, lengths[0]]).astype(jnp.int32)

    own = jnp.concatenate([conv_kernel, norm_gain[None], norm_bias[None]], axis=0)
    own = jnp.pad(own, ((0, 1), (0, 0)))
    par = lax.dynamic_update_slice(jnp.zeros((8, width), BF16), own, (0, f * 48))
    par = par + fsdp_move(par, core=1)
    par = (par + fsdp_move(par, y=1)) + (fsdp_move(par, y=2) + fsdp_move(par, y=3))
    par = par + fsdp_move(par, z=1)
    par = par + fsdp_move(par, z=3)
    par = par.astype(F32)

    block = gather([proj_weight] + [fsdp_move(proj_weight, z=k) for k in (1, 2, 3)], own)
    near = [block] + [fsdp_move(block, y=k) for k in (1, 2, 3)]

    swished, normed, rstd = forward(lengths, par, glu)
    keep, send = outer(core[None].astype(jnp.int32), swished, cot, near[1:])
    recv = fsdp_move(send, core=1)
    a = stage1(pos, keep, recv)
    mine = gather(near, a[0])
    pieces = [mine, fsdp_move(mine, core=1)]
    gconv, sums = backward(pos, pieces, par, cot, normed, rstd, a[0])
    glu_grad, small = taps(pos, par, glu, gconv, sums)
    v = stage2(pos, [a[0]] + [fsdp_move(a[k], y=k) for k in (1, 2, 3)], glu_grad)
    small = small + fsdp_move(small, core=1)
    small = (small + fsdp_move(small, y=1)) + (fsdp_move(small, y=2) + fsdp_move(small, y=3))
    block_out = project(pos, pieces, swished, res, (v[0], small))
    v = stage3(pos, [v[0]] + [fsdp_move(v[k], z=k) for k in (1, 2, 3)], block_out)
    total = (v[0] + dp_move(v[1], x=1)) + (dp_move(v[2], x=2) + dp_move(v[3], x=3))
    total = total + dp_move(total, low=1)
    proj_grad = join(pos, [total] + [dp_move(total, x=k) for k in (1, 2, 3)])

    small = small + fsdp_move(small, z=1)
    small = small + fsdp_move(small, z=3)
    small = lax.dynamic_slice(small, (0, f * 48), (8, 48))
    small = (small + dp_move(small, x=1)) + (dp_move(small, x=2) + dp_move(small, x=3))
    small = small + dp_move(small, low=1)
    return (block_out[None], glu_grad[None], proj_grad, small[:TAPS], small[TAPS : TAPS + 2])


def solution(mesh):
    rows = P(("dp", "fsdp"), None, None)
    return jax.shard_map(
        local,
        mesh=mesh,
        in_specs=(rows, rows, rows, P(("dp", "fsdp")), P(None, "fsdp"), P("fsdp"), P("fsdp"), P("fsdp", None)),
        out_specs=(rows, rows, P("fsdp", None), P(None, "fsdp"), P(None, "fsdp")),
        check_vma=False,
    )
```

time: 216 us -> 179 us (0.83)
  waiting for transfers between devices: 53.7 us -> 32.7 us
  starting transfers between devices: 72.9 us -> 57 us
  Pallas kernels: 78 us -> 73.7 us
  local copies, waits for them, and re-layouts: 5.97 us -> 8.67 us
    ppermute x34 -> x26, waiting for transfers between devices: 51.4 us -> 29 us  [fsdp_move(): return lax.ppermute(value, 'fsdp', perm)]
    ppermute x34 -> x26, starting transfers between devices: 50.7 us -> 41.3 us  [fsdp_move(): return lax.ppermute(value, 'fsdp', perm)]
    ppermute x14 -> x11, starting transfers between devices: 22.2 us -> 15.7 us  [dp_move(): return lax.ppermute(value, 'dp', perm)]
    unnamed x49 -> x42, local copies, waits for them, and re-layouts: 4.49 us -> 7.22 us
    pallas_call x1, Pallas kernels: 11.9 us -> 9.59 us  [forward(): pl.pallas_call(functools.partial(forward_kernel, rows=rows, frames=frames...]
    pallas_call x5 -> x7, Pallas kernels: 36.6 us -> 36.1 us  [the longest x1 15.8 us: backward(): pl.pallas_call(functools.partial(backward_kernel, rows=rows, chunk=chunk,...]
  transfers between devices with their start and end apart: 48 -> 37, of which waited for: 12 -> 15; matrix products, arithmetic and copies ran while one was open for 1% -> 3% of each run, Pallas kernels for 24% -> 29%
where the time goes in v2:
time: 179 us; the launch traced here: 178 us
  Pallas kernels  73.7 us (41%)
  starting transfers between devices  57 us (32%)
  waiting for transfers between devices  32.7 us (18%)
  local copies, waits for them, and re-layouts  8.67 us (5%)
  other arithmetic  4.61 us (3%)
    ppermute x26, starting transfers between devices, fsdp_move(): return lax.ppermute(value, 'fsdp', perm)  41.3 us
    ppermute x26, waiting for transfers between devices, fsdp_move(): return lax.ppermute(value, 'fsdp', perm)  29 us
    pallas_call x1, Pallas kernels, backward(): pl.pallas_call(functools.partial(backward_kernel, rows=rows, chunk=chunk,...  15.8 us
    ppermute x11, starting transfers between devices, dp_move(): return lax.ppermute(value, 'dp', perm)  15.7 us
    pallas_call x1, Pallas kernels, project(): pl.pallas_call(project_kernel, out_shape=sds((frames, width), BF16), grid...  10 us
    pallas_call x1, Pallas kernels, taps(): pl.pallas_call(functools.partial(taps_kernel, rows=rows, frames=frames, c...  9.98 us
    pallas_call x1, Pallas kernels, forward(): pl.pallas_call(functools.partial(forward_kernel, rows=rows, frames=frames...  9.59 us
    pallas_call x1, Pallas kernels, outer(): pl.pallas_call(outer_kernel, out_shape=(sds((16, 48, width), F32), sds((1...  8.06 us
  transfers between devices with their start and end apart: 37, of which 15 were waited for; matrix products, arithmetic and copies ran while one was open for 3% of the time, Pallas kernels for 29%

profile of v2, /device:TPU:32, one launch (start us, length us, event | category | flops | bytes accessed | tf_op | source)
XLA Modules:
  0.0 178.2 jit_solution(13788121642106133262)
XLA Ops:
  0.6 6.4 %collective-permute-start.1 = (bf16[48,1536]{1,0:T(8,128)(2,1)}, bf16[48,1536]{1,0:T(8,128)(2,1)S(1)}, u32[]{:S(2)}, u32[]{:S(2)}) collective-permute-start(bf16[48,1536]{1,0:T(8,128)(2,1)} %w0.1), channel_id=1, source_target_pairs={{0,4},{1,5},{2,6},{3,7},{4,0},{5,1},{6,2},{7,3},{8,12},{9,13},{10,... | collective-permute-start | bytes 442376 | tf_op jit(solution)/shard_map/ppermute | solution.py:20
  8.0 1.6 collective-permute-start
  9.7 0.8 dynamic-slice_add_fusion.1
  10.6 3.1 %collective-permute-start.9 = (bf16[8,1536]{1,0:T(8,128)(2,1)S(1)}, bf16[8,1536]{1,0:T(8,128)(2,1)S(1)}, u32[]{:S(2)}, u32[]{:S(2)}) collective-permute-start(bf16[8,1536]{1,0:T(8,128)(2,1)S(1)} %add.83), channel_id=1, source_target_pairs={{0,24},{1,25},{2,26},{3,27},{4,28},{5,29},{6,30},{7,31},{8,16},{9,... | collective-permute-start | bytes 73736 | tf_op jit(solution)/shard_map/ppermute | solution.py:20
  15.0 1.6 collective-permute-start.7
  16.6 3.1 %collective-permute-done.w1 = bf16[48,1536]{1,0:T(8,128)(2,1)S(1)} collective-permute-done((bf16[48,1536]{1,0:T(8,128)(2,1)}, bf16[48,1536]{1,0:T(8,128)(2,1)S(1)}, u32[]{:S(2)}, u32[]{:S(2)}) %collective-permute-start) | collective-permute-done | bytes 147488 | tf_op jit(solution)/shard_map/ppermute | solution.py:20
  19.7 1.3 collective-permute-done.2.w3
  21.6 2.0 %gather.2.w0 = bf16[192,1536]{1,0:T(8,128)(2,1)} custom-call(bf16[48,1536]{1,0:T(8,128)(2,1)} %w0.1, bf16[48,1536]{1,0:T(8,128)(2,1)} %copy-done.13, bf16[48,1536]{1,0:T(8,128)(2,1)} %copy-done.10, bf16[48,1536]{1,0:T(8,128)(2,1)} %copy-done.15, bf16[8,48]{1,0:T(8,128)(2,1)} %copy-done.19), custom_call_target="tpu_custom_call" | custom-call | bytes 360000 | tf_op jit(solution)/shard_map/gather/pallas_call | solution.py:266
  23.6 3.0 %collective-permute-start.5 = (bf16[192,1536]{1,0:T(8,128)(2,1)}, bf16[192,1536]{1,0:T(8,128)(2,1)S(1)}, u32[]{:S(2)}, u32[]{:S(2)}) collective-permute-start(bf16[192,1536]{1,0:T(8,128)(2,1)} %gather.2.w0), channel_id=1, source_target_pairs={{0,24},{1,25},{2,26},{3,27},{4,28},{5,29},{6,30},{7,31},{8,16},{9,... | collective-permute-start | bytes 1769480 | tf_op jit(solution)/shard_map/ppermute | solution.py:20
  27.7 2.7 %collective-permute-start.10 = (bf16[8,1536]{1,0:T(8,128)(2,1)S(1)}, bf16[8,1536]{1,0:T(8,128)(2,1)S(1)}, u32[]{:S(2)}, u32[]{:S(2)}) collective-permute-start(bf16[8,1536]{1,0:T(8,128)(2,1)S(1)} %add_add_fusion.2), channel_id=1, source_target_pairs={{0,2},{1,3},{2,0},{3,1},{4,6},{5,7},{6,4},{7,5},{8,10},{9,11},{10,... | collective-permute-start | bytes 73736 | tf_op jit(solution)/shard_map/ppermute | solution.py:20
  30.4 2.1 %collective-permute-done.10 = bf16[8,1536]{1,0:T(8,128)(2,1)S(1)} collective-permute-done((bf16[8,1536]{1,0:T(8,128)(2,1)S(1)}, bf16[8,1536]{1,0:T(8,128)(2,1)S(1)}, u32[]{:S(2)}, u32[]{:S(2)}) %collective-permute-start.10) | collective-permute-done | bytes 24608 | tf_op jit(solution)/shard_map/ppermute | solution.py:20
  32.6 3.5 %collective-permute-start.11 = (bf16[8,1536]{1,0:T(8,128)(2,1)S(1)}, bf16[8,1536]{1,0:T(8,128)(2,1)S(1)}, u32[]{:S(2)}, u32[]{:S(2)}) collective-permute-start(bf16[8,1536]{1,0:T(8,128)(2,1)S(1)} %add.87), channel_id=1, source_target_pairs={{0,6},{1,7},{2,4},{3,5},{4,2},{5,3},{6,0},{7,1},{8,14},{9,15},{10,... | collective-permute-start | bytes 73736 | tf_op jit(solution)/shard_map/ppermute | solution.py:20
  36.7 1.9 %collective-permute-done.11 = bf16[8,1536]{1,0:T(8,128)(2,1)S(1)} collective-permute-done((bf16[8,1536]{1,0:T(8,128)(2,1)S(1)}, bf16[8,1536]{1,0:T(8,128)(2,1)S(1)}, u32[]{:S(2)}, u32[]{:S(2)}) %collective-permute-start.11) | collective-permute-done | bytes 24608 | tf_op jit(solution)/shard_map/ppermute | solution.py:20
  39.2 9.6 %forward.1 = (bf16[768,1536]{1,0:T(8,128)(2,1)}, f32[768,1536]{1,0:T(8,128)}, f32[768,128]{1,0:T(8,128)}) custom-call(s32[1]{0:T(128)S(6)} %copy.15.lens, f32[8,1536]{1,0:T(8,128)} %add_convert_fusion.par.refs_2_, bf16[768,1536]{1,0:T(8,128)(2,1)} %bitcast.14), custom_call_target="tpu_custom_call" | custom-call | bytes 360000 | tf_op jit(solution)/shard_map/forward/pallas_call | solution.py:98
  48.8 3.6 %collective-permute-done.5.h3.w3 = bf16[192,1536]{1,0:T(8,128)(2,1)S(1)} collective-permute-done((bf16[192,1536]{1,0:T(8,128)(2,1)}, bf16[192,1536]{1,0:T(8,128)(2,1)S(1)}, u32[]{:S(2)}, u32[]{:S(2)}) %collective-permute-start.5) | collective-permute-done | bytes 589856 | tf_op jit(solution)/shard_map/ppermute | solution.py:20
  53.9 8.1 %outer.1 = (f32[16,48,1536]{2,1,0:T(8,128)}, bf16[16,48,1536]{2,1,0:T(8,128)(2,1)}) custom-call(s32[1]{0:T(128)} %bitcast.3.core, bf16[768,1536]{1,0:T(8,128)(2,1)} %get-tuple-element.26.sw.refs_2_, bf16[768,1536]{1,0:T(8,128)(2,1)} %bitcast.16, bf16[192,1536]{1,0:T(8,128)(2,1)} %copy-done.3, bf16[192,1536]{1,0:T(8,128)(2,1)} %copy-done.2, ...), custom_call_target="tpu_custom_call" | custom-call | bytes 360000 | tf_op jit(solution)/shard_map/outer/pallas_call | solution.py:128
  62.6 4.1 %collective-permute-done.12 = bf16[16,48,1536]{2,1,0:T(8,128)(2,1)S(1)} collective-permute-done((bf16[16,48,1536]{2,1,0:T(8,128)(2,1)}, bf16[16,48,1536]{2,1,0:T(8,128)(2,1)S(1)}, u32[]{:S(2)}, u32[]{:S(2)}) %collective-permute-start.12) | collective-permute-done | bytes 2359328 | tf_op jit(solution)/shard_map/ppermute | solution.py:20
  66.7 1.4 copy-done.4
  68.1 6.0 %stage1.1 = (f32[4,48,1536]{2,1,0:T(8,128)}, bf16[4,48,1536]{2,1,0:T(8,128)(2,1)}, bf16[4,48,1536]{2,1,0:T(8,128)(2,1)}, bf16[4,48,1536]{2,1,0:T(8,128)(2,1)}) custom-call(s32[5]{0:T(128)} %stack.19.pos, f32[4,4,48,1536]{3,2,1,0:T(8,128)} %bitcast.19, bf16[4,4,48,1536]{3,2,1,0:T(8,128)(2,1)} %bitcast.20), custom_call_target="tpu_custom_call" | custom-call | bytes 360000 | tf_op jit(solution)/shard_map/stage1/pallas_call | solution.py:166
  74.1 3.1 %gather.3.refs_0_ = bf16[768,1536]{1,0:T(8,128)(2,1)} custom-call(bf16[192,1536]{1,0:T(8,128)(2,1)} %gather.2.w0, bf16[192,1536]{1,0:T(8,128)(2,1)} %copy-done.3, bf16[192,1536]{1,0:T(8,128)(2,1)} %copy-done.2, bf16[192,1536]{1,0:T(8,128)(2,1)} %copy-done.1, f32[4,48,1536]{2,1,0:T(8,128)} %get-tuple-element.29.held.refs_6_.a0), custom_call_target="tpu_custom_call" | custom-call | bytes 360000 | tf_op jit(solution)/shard_map/gather/pallas_call | solution.py:266
  77.4 1.6 collective-permute-start.14
  78.9 2.9 %collective-permute-start.15 = (bf16[4,48,1536]{2,1,0:T(8,128)(2,1)}, bf16[4,48,1536]{2,1,0:T(8,128)(2,1)S(1)}, u32[]{:S(2)}, u32[]{:S(2)}) collective-permute-start(bf16[4,48,1536]{2,1,0:T(8,128)(2,1)} %get-tuple-element.31), channel_id=1, source_target_pairs={{0,16},{1,17},{2,18},{3,19},{4,20},{5,21},{6,22},{7,23},{8,24},{9,... | collective-permute-start | bytes 1769480 | tf_op jit(solution)/shard_map/ppermute | solution.py:20
  82.1 1.4 copy-done
  83.4 15.8 %backward.1 = (f32[768,1536]{1,0:T(8,128)}, f32[2,8,1536]{2,1,0:T(8,128)}) custom-call(s32[5]{0:T(128)} %stack.19.pos, bf16[768,1536]{1,0:T(8,128)(2,1)} %gather.3.refs_0_, bf16[768,1536]{1,0:T(8,128)(2,1)} %copy-done, f32[8,1536]{1,0:T(8,128)} %add_convert_fusion.par.refs_2_, bf16[768,1536]{1,0:T(8,128)(2,1)} %bitcast.17, ...), custom_call_target="tpu_custom_call" | custom-call | bytes 75600000 | tf_op jit(solution)/shard_map/backward/pallas_call | solution.py:367
  99.2 10.0 %taps.1 = (bf16[768,1536]{1,0:T(8,128)(2,1)}, f32[8,1536]{1,0:T(8,128)}) custom-call(s32[5]{0:T(128)} %stack.19.pos, f32[8,1536]{1,0:T(8,128)} %add_convert_fusion.par.refs_2_, bf16[768,1536]{1,0:T(8,128)(2,1)} %bitcast.15, f32[768,1536]{1,0:T(8,128)} %get-tuple-element.35.gconv, f32[2,8,1536]{2,1,0:T(8,128)} %get-tuple-element.36.norm_sums), custom_call_target="tpu_custom_call" | custom-call | bytes 36000000 | tf_op jit(solution)/shard_map/taps/pallas_call | solution.py:443
  109.2 1.4 collective-permute-done.17
  110.6 0.8 add.89
  111.4 2.9 %collective-permute-start.20 = (f32[8,1536]{1,0:T(8,128)S(1)}, f32[8,1536]{1,0:T(8,128)S(1)}, u32[]{:S(2)}, u32[]{:S(2)}) collective-permute-start(f32[8,1536]{1,0:T(8,128)S(1)} %add.89), channel_id=1, source_target_pairs={{0,24},{1,25},{2,26},{3,27},{4,28},{5,29},{6,30},{7,31},{8,16},{9,... | collective-permute-start | bytes 147464 | tf_op jit(solution)/shard_map/ppermute | solution.py:20
  116.6 4.2 %stage2.1 = (f32[48,1536]{1,0:T(8,128)}, bf16[48,1536]{1,0:T(8,128)(2,1)}, bf16[48,1536]{1,0:T(8,128)(2,1)}, bf16[48,1536]{1,0:T(8,128)(2,1)}) custom-call(s32[5]{0:T(128)} %stack.19.pos, f32[4,48,1536]{2,1,0:T(8,128)} %get-tuple-element.29.held.refs_6_.a0, bf16[4,48,1536]{2,1,0:T(8,128)(2,1)} %copy-done.5, bf16[4,48,1536]{2,1,0:T(8,128)(2,1)} %copy-done.6, ...), custom_call_target="tpu_custom_call" | custom-call | bytes 10800000 | tf_op jit(solution)/shard_map/stage2/pallas_call | solution.py:194
  120.8 3.2 %collective-permute-start.21 = (bf16[48,1536]{1,0:T(8,128)(2,1)}, bf16[48,1536]{1,0:T(8,128)(2,1)S(1)}, u32[]{:S(2)}, u32[]{:S(2)}) collective-permute-start(bf16[48,1536]{1,0:T(8,128)(2,1)} %get-tuple-element.40), channel_id=1, source_target_pairs={{0,2},{1,3},{2,0},{3,1},{4,6},{5,7},{6,4},{7,5},{8,10},{9,11},{10,... | collective-permute-start | bytes 442376 | tf_op jit(solution)/shard_map/ppermute | solution.py:20
  124.0 2.2 %collective-permute-start.22 = (bf16[48,1536]{1,0:T(8,128)(2,1)}, bf16[48,1536]{1,0:T(8,128)(2,1)S(1)}, u32[]{:S(2)}, u32[]{:S(2)}) collective-permute-start(bf16[48,1536]{1,0:T(8,128)(2,1)} %get-tuple-element.41), channel_id=1, source_target_pairs={{0,4},{1,5},{2,6},{3,7},{4,0},{5,1},{6,2},{7,3},{8,12},{9,13},{10,... | collective-permute-start | bytes 442376 | tf_op jit(solution)/shard_map/ppermute | solution.py:20
  126.2 1.4 collective-permute-start.23
  128.3 10.0 %project.1.held = bf16[768,1536]{1,0:T(8,128)(2,1)} custom-call(s32[5]{0:T(128)} %stack.19.pos, bf16[768,1536]{1,0:T(8,128)(2,1)} %gather.3.refs_0_, bf16[768,1536]{1,0:T(8,128)(2,1)} %copy-done, bf16[768,1536]{1,0:T(8,128)(2,1)} %get-tuple-element.26.sw.refs_2_, bf16[768,1536]{1,0:T(8,128)(2,1)} %bitcast.21, f32[48,1536]{1,0:T(8,128)} %get-tuple-element.38.refs_4_.v0, ...), custom_call_target="tpu_custom_call" | custom-call | bytes 39600000 | tf_op jit(solution)/shard_map/project/pallas_call | solution.py:310
  138.4 3.3 %collective-permute-done.23.v3 = bf16[48,1536]{1,0:T(8,128)(2,1)S(1)} collective-permute-done((bf16[48,1536]{1,0:T(8,128)(2,1)}, bf16[48,1536]{1,0:T(8,128)(2,1)S(1)}, u32[]{:S(2)}, u32[]{:S(2)}) %collective-permute-start.23) | collective-permute-done | bytes 147488 | tf_op jit(solution)/shard_map/ppermute | solution.py:20
  142.3 2.6 %stage3.1 = (f32[48,384]{1,0:T(8,128)}, f32[48,384]{1,0:T(8,128)}, f32[48,384]{1,0:T(8,128)}, f32[48,384]{1,0:T(8,128)}) custom-call(s32[5]{0:T(128)} %stack.19.pos, f32[48,1536]{1,0:T(8,128)} %get-tuple-element.38.refs_4_.v0, bf16[48,1536]{1,0:T(8,128)(2,1)} %copy-done.11, bf16[48,1536]{1,0:T(8,128)(2,1)} %copy-done.12, bf16[48,1536]{1,0:T(8,128)(2,1)} %copy-done.14, ...), custom_call_target="tpu_custom_call" | custom-call | bytes 7200000 | tf_op jit(solution)/shard_map/stage3/pallas_call | solution.py:219
  144.9 1.5 collective-permute-start.24
  146.4 2.7 %collective-permute-start.25 = (f32[48,384]{1,0:T(8,128)}, f32[48,384]{1,0:T(8,128)S(1)}, u32[]{:S(2)}, u32[]{:S(2)}) collective-permute-start(f32[48,384]{1,0:T(8,128)} %get-tuple-element.45), channel_id=1, source_target_pairs={{0,64},{32,96},{64,0},{96,32},{128,192},{160,224},{192,128},{224,1... | collective-permute-start | bytes 221192 | tf_op jit(solution)/shard_map/ppermute | solution.py:25
  149.9 4.7 %collective-permute-done.31 = f32[8,1536]{1,0:T(8,128)S(1)} collective-permute-done((f32[8,1536]{1,0:T(8,128)S(1)}, f32[8,1536]{1,0:T(8,128)S(1)}, u32[]{:S(2)}, u32[]{:S(2)}) %collective-permute-start.31) | collective-permute-done | bytes 49184 | tf_op jit(solution)/shard_map/ppermute | solution.py:20
  154.6 1.5 collective-permute-start.32
  156.2 0.9 add_add_fusion
  157.1 2.2 %collective-permute-start.27 = (f32[48,384]{1,0:T(8,128)S(1)}, f32[48,384]{1,0:T(8,128)S(1)}, u32[]{:S(2)}, u32[]{:S(2)}) collective-permute-start(f32[48,384]{1,0:T(8,128)S(1)} %add_add_fusion), channel_id=1, source_target_pairs={{0,128},{32,160},{64,192},{96,224},{128,0},{160,32},{192,64},{224,... | collective-permute-start | bytes 221192 | tf_op jit(solution)/shard_map/ppermute | solution.py:25
  159.3 2.1 %collective-permute-done.32 = f32[8,1536]{1,0:T(8,128)S(1)} collective-permute-done((f32[8,1536]{1,0:T(8,128)S(1)}, f32[8,1536]{1,0:T(8,128)S(1)}, u32[]{:S(2)}, u32[]{:S(2)}) %collective-permute-start.32) | collective-permute-done | bytes 49184 | tf_op jit(solution)/shard_map/ppermute | solution.py:20
  161.4 2.1 %collective-permute-start.34 = (f32[8,48]{1,0:T(8,128)S(1)}, f32[8,48]{1,0:T(8,128)S(1)}, u32[]{:S(2)}, u32[]{:S(2)}) collective-permute-start(f32[8,48]{1,0:T(8,128)S(1)} %dynamic-slice_add_fusion), channel_id=1, source_target_pairs={{0,64},{32,96},{64,0},{96,32},{128,192},{160,224},{192,128},{224,1... | collective-permute-start | bytes 4616 | tf_op jit(solution)/shard_map/ppermute | solution.py:25
  163.5 1.8 %collective-permute-start.33 = (f32[8,48]{1,0:T(8,128)S(1)}, f32[8,48]{1,0:T(8,128)S(1)}, u32[]{:S(2)}, u32[]{:S(2)}) collective-permute-start(f32[8,48]{1,0:T(8,128)S(1)} %dynamic-slice_add_fusion), channel_id=1, source_target_pairs={{0,32},{32,0},{64,96},{96,64},{128,160},{160,128},{192,224},{224,1... | collective-permute-start | bytes 4616 | tf_op jit(solution)/shard_map/ppermute | solution.py:25
  165.8 2.9 %collective-permute-start.30 = (f32[48,384]{1,0:T(8,128)S(1)}, f32[48,384]{1,0:T(8,128)S(1)}, u32[]{:S(2)}, u32[]{:S(2)}) collective-permute-start(f32[48,384]{1,0:T(8,128)S(1)} %add.96.v0), channel_id=1, source_target_pairs={{0,96},{32,64},{64,32},{96,0},{128,224},{160,192},{192,160},{224,1... | collective-permute-start | bytes 221192 | tf_op jit(solution)/shard_map/ppermute | solution.py:25
  168.7 1.3 collective-permute-start.28
  170.4 3.4 %collective-permute-done.36 = f32[8,48]{1,0:T(8,128)S(1)} collective-permute-done((f32[8,48]{1,0:T(8,128)S(1)}, f32[8,48]{1,0:T(8,128)S(1)}, u32[]{:S(2)}, u32[]{:S(2)}) %collective-permute-start.36) | collective-permute-done | bytes 1568 | tf_op jit(solution)/shard_map/ppermute | solution.py:25
  175.8 2.4 %join.1 = f32[48,1536]{1,0:T(8,128)} custom-call(s32[5]{0:T(128)} %stack.19.pos, f32[48,384]{1,0:T(8,128)} %copy-done.9, f32[48,384]{1,0:T(8,128)} %copy-done.18, f32[48,384]{1,0:T(8,128)} %copy-done.17, f32[48,384]{1,0:T(8,128)} %copy-done.16), custom_call_target="tpu_custom_call" | custom-call | bytes 7200000 | tf_op jit(solution)/shard_map/join/pallas_call | solution.py:243
  (97 shorter events, 14.6 us)
Async XLA Ops:
  0.6 14.4 %collective-permute-start.1 = (bf16[48,1536]{1,0:T(8,128)(2,1)}, bf16[48,1536]{1,0:T(8,128)(2,1)S(1)}, u32[]{:S(2)}, u32[]{:S(2)}) collective-permute-start(bf16[48,1536]{1,0:T(8,128)(2,1)} %w0.1), channel_id=1, source_target_pairs={{0,4},{1,5},{2,6},{3,7},{4,0},{5,1},{6,2},{7,3},{8,12},{9,13},{10,... | collective-permute-start | bytes 442376 | tf_op jit(solution)/shard_map/ppermute | solution.py:20
  7.7 13.2 %copy-start.19 = (bf16[8,48]{1,0:T(8,128)(2,1)}, bf16[8,48]{1,0:T(8,128)(2,1)S(1)}, u32[]{:S(2)}) copy-start(bf16[8,48]{1,0:T(8,128)(2,1)S(1)} %fusion.4.held) | copy-start | bytes 2308
  7.9 1.7 collective-permute-start.6
  8.0 11.6 %collective-permute-start = (bf16[48,1536]{1,0:T(8,128)(2,1)}, bf16[48,1536]{1,0:T(8,128)(2,1)S(1)}, u32[]{:S(2)}, u32[]{:S(2)}) collective-permute-start(bf16[48,1536]{1,0:T(8,128)(2,1)} %w0.1), channel_id=1, source_target_pairs={{0,2},{1,3},{2,0},{3,1},{4,6},{5,7},{6,4},{7,5},{8,10},{9,11},{10,... | collective-permute-start | bytes 442376 | tf_op jit(solution)/shard_map/ppermute | solution.py:20
  9.7 11.3 %collective-permute-start.2 = (bf16[48,1536]{1,0:T(8,128)(2,1)}, bf16[48,1536]{1,0:T(8,128)(2,1)S(1)}, u32[]{:S(2)}, u32[]{:S(2)}) collective-permute-start(bf16[48,1536]{1,0:T(8,128)(2,1)} %w0.1), channel_id=1, source_target_pairs={{0,6},{1,7},{2,4},{3,5},{4,2},{5,3},{6,0},{7,1},{8,14},{9,15},{10,... | collective-permute-start | bytes 442376 | tf_op jit(solution)/shard_map/ppermute | solution.py:20
  10.6 16.7 %collective-permute-start.9 = (bf16[8,1536]{1,0:T(8,128)(2,1)S(1)}, bf16[8,1536]{1,0:T(8,128)(2,1)S(1)}, u32[]{:S(2)}, u32[]{:S(2)}) collective-permute-start(bf16[8,1536]{1,0:T(8,128)(2,1)S(1)} %add.83), channel_id=1, source_target_pairs={{0,24},{1,25},{2,26},{3,27},{4,28},{5,29},{6,30},{7,31},{8,16},{9,... | collective-permute-start | bytes 73736 | tf_op jit(solution)/shard_map/ppermute | solution.py:20
  13.7 14.1 %collective-permute-start.8 = (bf16[8,1536]{1,0:T(8,128)(2,1)S(1)}, bf16[8,1536]{1,0:T(8,128)(2,1)S(1)}, u32[]{:S(2)}, u32[]{:S(2)}) collective-permute-start(bf16[8,1536]{1,0:T(8,128)(2,1)S(1)} %add.83), channel_id=1, source_target_pairs={{0,16},{1,17},{2,18},{3,19},{4,20},{5,21},{6,22},{7,23},{8,24},{9,... | collective-permute-start | bytes 73736 | tf_op jit(solution)/shard_map/ppermute | solution.py:20
  15.0 6.0 %copy-start.10 = (bf16[48,1536]{1,0:T(8,128)(2,1)}, bf16[48,1536]{1,0:T(8,128)(2,1)S(1)}, u32[]{:S(2)}) copy-start(bf16[48,1536]{1,0:T(8,128)(2,1)S(1)} %collective-permute-done.1.w2) | copy-start | bytes 442372
  15.0 12.7 %collective-permute-start.7 = (bf16[8,1536]{1,0:T(8,128)(2,1)S(1)}, bf16[8,1536]{1,0:T(8,128)(2,1)S(1)}, u32[]{:S(2)}, u32[]{:S(2)}) collective-permute-start(bf16[8,1536]{1,0:T(8,128)(2,1)S(1)} %add.83), channel_id=1, source_target_pairs={{0,8},{1,9},{2,10},{3,11},{4,12},{5,13},{6,14},{7,15},{8,0},{9,1},... | collective-permute-start | bytes 73736 | tf_op jit(solution)/shard_map/ppermute | solution.py:20
  19.7 1.3 copy-start.13
  23.6 28.8 %collective-permute-start.5 = (bf16[192,1536]{1,0:T(8,128)(2,1)}, bf16[192,1536]{1,0:T(8,128)(2,1)S(1)}, u32[]{:S(2)}, u32[]{:S(2)}) collective-permute-start(bf16[192,1536]{1,0:T(8,128)(2,1)} %gather.2.w0), channel_id=1, source_target_pairs={{0,24},{1,25},{2,26},{3,27},{4,28},{5,29},{6,30},{7,31},{8,16},{9,... | collective-permute-start | bytes 1769480 | tf_op jit(solution)/shard_map/ppermute | solution.py:20
  26.6 25.8 %collective-permute-start.4 = (bf16[192,1536]{1,0:T(8,128)(2,1)}, bf16[192,1536]{1,0:T(8,128)(2,1)S(1)}, u32[]{:S(2)}, u32[]{:S(2)}) collective-permute-start(bf16[192,1536]{1,0:T(8,128)(2,1)} %gather.2.w0), channel_id=1, source_target_pairs={{0,16},{1,17},{2,18},{3,19},{4,20},{5,21},{6,22},{7,23},{8,24},{9,... | collective-permute-start | bytes 1769480 | tf_op jit(solution)/shard_map/ppermute | solution.py:20
  27.3 25.8 %collective-permute-start.3 = (bf16[192,1536]{1,0:T(8,128)(2,1)}, bf16[192,1536]{1,0:T(8,128)(2,1)S(1)}, u32[]{:S(2)}, u32[]{:S(2)}) collective-permute-start(bf16[192,1536]{1,0:T(8,128)(2,1)} %gather.2.w0), channel_id=1, source_target_pairs={{0,8},{1,9},{2,10},{3,11},{4,12},{5,13},{6,14},{7,15},{8,0},{9,1},... | collective-permute-start | bytes 1769480 | tf_op jit(solution)/shard_map/ppermute | solution.py:20
  27.7 4.8 %collective-permute-start.10 = (bf16[8,1536]{1,0:T(8,128)(2,1)S(1)}, bf16[8,1536]{1,0:T(8,128)(2,1)S(1)}, u32[]{:S(2)}, u32[]{:S(2)}) collective-permute-start(bf16[8,1536]{1,0:T(8,128)(2,1)S(1)} %add_add_fusion.2), channel_id=1, source_target_pairs={{0,2},{1,3},{2,0},{3,1},{4,6},{5,7},{6,4},{7,5},{8,10},{9,11},{10,... | collective-permute-start | bytes 73736 | tf_op jit(solution)/shard_map/ppermute | solution.py:20
  32.6 6.0 %collective-permute-start.11 = (bf16[8,1536]{1,0:T(8,128)(2,1)S(1)}, bf16[8,1536]{1,0:T(8,128)(2,1)S(1)}, u32[]{:S(2)}, u32[]{:S(2)}) collective-permute-start(bf16[8,1536]{1,0:T(8,128)(2,1)S(1)} %add.87), channel_id=1, source_target_pairs={{0,6},{1,7},{2,4},{3,5},{4,2},{5,3},{6,0},{7,1},{8,14},{9,15},{10,... | collective-permute-start | bytes 73736 | tf_op jit(solution)/shard_map/ppermute | solution.py:20
  52.4 1.0 copy-start.2
  62.0 4.7 %collective-permute-start.12 = (bf16[16,48,1536]{2,1,0:T(8,128)(2,1)}, bf16[16,48,1536]{2,1,0:T(8,128)(2,1)S(1)}, u32[]{:S(2)}, u32[]{:S(2)}) collective-permute-start(bf16[16,48,1536]{2,1,0:T(8,128)(2,1)} %get-tuple-element.28), channel_id=1, source_target_pairs={{0,1},{1,0},{2,3},{3,2},{4,5},{5,4},{6,7},{7,6},{8,9},{9,8},{10,11... | collective-permute-start | bytes 7077896 | tf_op jit(solution)/shard_map/ppermute | solution.py:20
  66.7 1.4 copy-start.4
  77.2 4.9 %collective-permute-start.13 = (bf16[768,1536]{1,0:T(8,128)(2,1)}, bf16[768,1536]{1,0:T(8,128)(2,1)S(1)}, u32[]{:S(2)}, u32[]{:S(2)}) collective-permute-start(bf16[768,1536]{1,0:T(8,128)(2,1)} %gather.3.refs_0_), channel_id=1, source_target_pairs={{0,1},{1,0},{2,3},{3,2},{4,5},{5,4},{6,7},{7,6},{8,9},{9,8},{10,11... | collective-permute-start | bytes 7077896 | tf_op jit(solution)/shard_map/ppermute | solution.py:20
  77.4 37.6 %collective-permute-start.14 = (bf16[4,48,1536]{2,1,0:T(8,128)(2,1)}, bf16[4,48,1536]{2,1,0:T(8,128)(2,1)S(1)}, u32[]{:S(2)}, u32[]{:S(2)}) collective-permute-start(bf16[4,48,1536]{2,1,0:T(8,128)(2,1)} %get-tuple-element.30), channel_id=1, source_target_pairs={{0,8},{1,9},{2,10},{3,11},{4,12},{5,13},{6,14},{7,15},{8,0},{9,1},... | collective-permute-start | bytes 1769480 | tf_op jit(solution)/shard_map/ppermute | solution.py:20
  78.9 36.6 %collective-permute-start.15 = (bf16[4,48,1536]{2,1,0:T(8,128)(2,1)}, bf16[4,48,1536]{2,1,0:T(8,128)(2,1)S(1)}, u32[]{:S(2)}, u32[]{:S(2)}) collective-permute-start(bf16[4,48,1536]{2,1,0:T(8,128)(2,1)} %get-tuple-element.31), channel_id=1, source_target_pairs={{0,16},{1,17},{2,18},{3,19},{4,20},{5,21},{6,22},{7,23},{8,24},{9,... | collective-permute-start | bytes 1769480 | tf_op jit(solution)/shard_map/ppermute | solution.py:20
  81.8 33.8 %collective-permute-start.16 = (bf16[4,48,1536]{2,1,0:T(8,128)(2,1)}, bf16[4,48,1536]{2,1,0:T(8,128)(2,1)S(1)}, u32[]{:S(2)}, u32[]{:S(2)}) collective-permute-start(bf16[4,48,1536]{2,1,0:T(8,128)(2,1)} %get-tuple-element.32), channel_id=1, source_target_pairs={{0,24},{1,25},{2,26},{3,27},{4,28},{5,29},{6,30},{7,31},{8,16},{9,... | collective-permute-start | bytes 1769480 | tf_op jit(solution)/shard_map/ppermute | solution.py:20
  82.1 1.4 copy-start
  109.2 1.4 collective-permute-start.17
  111.4 14.8 %collective-permute-start.20 = (f32[8,1536]{1,0:T(8,128)S(1)}, f32[8,1536]{1,0:T(8,128)S(1)}, u32[]{:S(2)}, u32[]{:S(2)}) collective-permute-start(f32[8,1536]{1,0:T(8,128)S(1)} %add.89), channel_id=1, source_target_pairs={{0,24},{1,25},{2,26},{3,27},{4,28},{5,29},{6,30},{7,31},{8,16},{9,... | collective-permute-start | bytes 147464 | tf_op jit(solution)/shard_map/ppermute | solution.py:20
  114.4 13.3 %collective-permute-start.19 = (f32[8,1536]{1,0:T(8,128)S(1)}, f32[8,1536]{1,0:T(8,128)S(1)}, u32[]{:S(2)}, u32[]{:S(2)}) collective-permute-start(f32[8,1536]{1,0:T(8,128)S(1)} %add.89), channel_id=1, source_target_pairs={{0,16},{1,17},{2,18},{3,19},{4,20},{5,21},{6,22},{7,23},{8,24},{9,... | collective-permute-start | bytes 147464 | tf_op jit(solution)/shard_map/ppermute | solution.py:20
  115.0 12.7 %collective-permute-start.18 = (f32[8,1536]{1,0:T(8,128)S(1)}, f32[8,1536]{1,0:T(8,128)S(1)}, u32[]{:S(2)}, u32[]{:S(2)}) collective-permute-start(f32[8,1536]{1,0:T(8,128)S(1)} %add.89), channel_id=1, source_target_pairs={{0,8},{1,9},{2,10},{3,11},{4,12},{5,13},{6,14},{7,15},{8,0},{9,1},... | collective-permute-start | bytes 147464 | tf_op jit(solution)/shard_map/ppermute | solution.py:20
  120.8 17.6 %collective-permute-start.21 = (bf16[48,1536]{1,0:T(8,128)(2,1)}, bf16[48,1536]{1,0:T(8,128)(2,1)S(1)}, u32[]{:S(2)}, u32[]{:S(2)}) collective-permute-start(bf16[48,1536]{1,0:T(8,128)(2,1)} %get-tuple-element.40), channel_id=1, source_target_pairs={{0,2},{1,3},{2,0},{3,1},{4,6},{5,7},{6,4},{7,5},{8,10},{9,11},{10,... | collective-permute-start | bytes 442376 | tf_op jit(solution)/shard_map/ppermute | solution.py:20
  124.0 14.4 %collective-permute-start.22 = (bf16[48,1536]{1,0:T(8,128)(2,1)}, bf16[48,1536]{1,0:T(8,128)(2,1)S(1)}, u32[]{:S(2)}, u32[]{:S(2)}) collective-permute-start(bf16[48,1536]{1,0:T(8,128)(2,1)} %get-tuple-element.41), channel_id=1, source_target_pairs={{0,4},{1,5},{2,6},{3,7},{4,0},{5,1},{6,2},{7,3},{8,12},{9,13},{10,... | collective-permute-start | bytes 442376 | tf_op jit(solution)/shard_map/ppermute | solution.py:20
  126.2 15.4 %collective-permute-start.23 = (bf16[48,1536]{1,0:T(8,128)(2,1)}, bf16[48,1536]{1,0:T(8,128)(2,1)S(1)}, u32[]{:S(2)}, u32[]{:S(2)}) collective-permute-start(bf16[48,1536]{1,0:T(8,128)(2,1)} %get-tuple-element.42), channel_id=1, source_target_pairs={{0,6},{1,7},{2,4},{3,5},{4,2},{5,3},{6,0},{7,1},{8,14},{9,15},{10,... | collective-permute-start | bytes 442376 | tf_op jit(solution)/shard_map/ppermute | solution.py:20
  138.3 11.3 %copy-start.8 = (f32[8,1536]{1,0:T(8,128)S(1)}, f32[8,1536]{1,0:T(8,128)}, u32[]{:S(2)}) copy-start(f32[8,1536]{1,0:T(8,128)} %add_add_fusion.1.refs_5_) | copy-start | bytes 147460
  138.3 3.3 %copy-start.11 = (bf16[48,1536]{1,0:T(8,128)(2,1)}, bf16[48,1536]{1,0:T(8,128)(2,1)S(1)}, u32[]{:S(2)}) copy-start(bf16[48,1536]{1,0:T(8,128)(2,1)S(1)} %collective-permute-done.21.v1) | copy-start | bytes 442372
  138.4 3.3 %copy-start.12 = (bf16[48,1536]{1,0:T(8,128)(2,1)}, bf16[48,1536]{1,0:T(8,128)(2,1)S(1)}, u32[]{:S(2)}) copy-start(bf16[48,1536]{1,0:T(8,128)(2,1)S(1)} %collective-permute-done.22.v2) | copy-start | bytes 442372
  144.9 11.2 %collective-permute-start.24 = (f32[48,384]{1,0:T(8,128)}, f32[48,384]{1,0:T(8,128)S(1)}, u32[]{:S(2)}, u32[]{:S(2)}) collective-permute-start(f32[48,384]{1,0:T(8,128)} %get-tuple-element.44), channel_id=1, source_target_pairs={{0,32},{32,0},{64,96},{96,64},{128,160},{160,128},{192,224},{224,1... | collective-permute-start | bytes 221192 | tf_op jit(solution)/shard_map/ppermute | solution.py:25
  146.4 9.7 %collective-permute-start.25 = (f32[48,384]{1,0:T(8,128)}, f32[48,384]{1,0:T(8,128)S(1)}, u32[]{:S(2)}, u32[]{:S(2)}) collective-permute-start(f32[48,384]{1,0:T(8,128)} %get-tuple-element.45), channel_id=1, source_target_pairs={{0,64},{32,96},{64,0},{96,32},{128,192},{160,224},{192,128},{224,1... | collective-permute-start | bytes 221192 | tf_op jit(solution)/shard_map/ppermute | solution.py:25
  149.2 7.0 %collective-permute-start.26 = (f32[48,384]{1,0:T(8,128)}, f32[48,384]{1,0:T(8,128)S(1)}, u32[]{:S(2)}, u32[]{:S(2)}) collective-permute-start(f32[48,384]{1,0:T(8,128)} %get-tuple-element.46), channel_id=1, source_target_pairs={{0,96},{32,64},{64,32},{96,0},{128,224},{160,192},{192,160},{224,1... | collective-permute-start | bytes 221192 | tf_op jit(solution)/shard_map/ppermute | solution.py:25
  149.6 5.0 %collective-permute-start.31 = (f32[8,1536]{1,0:T(8,128)S(1)}, f32[8,1536]{1,0:T(8,128)S(1)}, u32[]{:S(2)}, u32[]{:S(2)}) collective-permute-start(f32[8,1536]{1,0:T(8,128)S(1)} %copy-done.8), channel_id=1, source_target_pairs={{0,2},{1,3},{2,0},{3,1},{4,6},{5,7},{6,4},{7,5},{8,10},{9,11},{10,... | collective-permute-start | bytes 147464 | tf_op jit(solution)/shard_map/ppermute | solution.py:20
  154.6 6.7 %collective-permute-start.32 = (f32[8,1536]{1,0:T(8,128)S(1)}, f32[8,1536]{1,0:T(8,128)S(1)}, u32[]{:S(2)}, u32[]{:S(2)}) collective-permute-start(f32[8,1536]{1,0:T(8,128)S(1)} %add.97), channel_id=1, source_target_pairs={{0,6},{1,7},{2,4},{3,5},{4,2},{5,3},{6,0},{7,1},{8,14},{9,15},{10,... | collective-permute-start | bytes 147464 | tf_op jit(solution)/shard_map/ppermute | solution.py:20
  157.1 8.7 %collective-permute-start.27 = (f32[48,384]{1,0:T(8,128)S(1)}, f32[48,384]{1,0:T(8,128)S(1)}, u32[]{:S(2)}, u32[]{:S(2)}) collective-permute-start(f32[48,384]{1,0:T(8,128)S(1)} %add_add_fusion), channel_id=1, source_target_pairs={{0,128},{32,160},{64,192},{96,224},{128,0},{160,32},{192,64},{224,... | collective-permute-start | bytes 221192 | tf_op jit(solution)/shard_map/ppermute | solution.py:25
  161.4 7.3 %collective-permute-start.34 = (f32[8,48]{1,0:T(8,128)S(1)}, f32[8,48]{1,0:T(8,128)S(1)}, u32[]{:S(2)}, u32[]{:S(2)}) collective-permute-start(f32[8,48]{1,0:T(8,128)S(1)} %dynamic-slice_add_fusion), channel_id=1, source_target_pairs={{0,64},{32,96},{64,0},{96,32},{128,192},{160,224},{192,128},{224,1... | collective-permute-start | bytes 4616 | tf_op jit(solution)/shard_map/ppermute | solution.py:25
  163.5 6.5 %collective-permute-start.33 = (f32[8,48]{1,0:T(8,128)S(1)}, f32[8,48]{1,0:T(8,128)S(1)}, u32[]{:S(2)}, u32[]{:S(2)}) collective-permute-start(f32[8,48]{1,0:T(8,128)S(1)} %dynamic-slice_add_fusion), channel_id=1, source_target_pairs={{0,32},{32,0},{64,96},{96,64},{128,160},{160,128},{192,224},{224,1... | collective-permute-start | bytes 4616 | tf_op jit(solution)/shard_map/ppermute | solution.py:25
  165.3 4.8 %collective-permute-start.35 = (f32[8,48]{1,0:T(8,128)S(1)}, f32[8,48]{1,0:T(8,128)S(1)}, u32[]{:S(2)}, u32[]{:S(2)}) collective-permute-start(f32[8,48]{1,0:T(8,128)S(1)} %dynamic-slice_add_fusion), channel_id=1, source_target_pairs={{0,96},{32,64},{64,32},{96,0},{128,224},{160,192},{192,160},{224,1... | collective-permute-start | bytes 4616 | tf_op jit(solution)/shard_map/ppermute | solution.py:25
  165.8 8.8 %copy-start.9 = (f32[48,384]{1,0:T(8,128)}, f32[48,384]{1,0:T(8,128)S(1)}, u32[]{:S(2)}) copy-start(f32[48,384]{1,0:T(8,128)S(1)} %add.96.v0) | copy-start | bytes 221188
  165.8 8.5 %collective-permute-start.30 = (f32[48,384]{1,0:T(8,128)S(1)}, f32[48,384]{1,0:T(8,128)S(1)}, u32[]{:S(2)}, u32[]{:S(2)}) collective-permute-start(f32[48,384]{1,0:T(8,128)S(1)} %add.96.v0), channel_id=1, source_target_pairs={{0,96},{32,64},{64,32},{96,0},{128,224},{160,192},{192,160},{224,1... | collective-permute-start | bytes 221192 | tf_op jit(solution)/shard_map/ppermute | solution.py:25
  168.7 5.9 %collective-permute-start.29 = (f32[48,384]{1,0:T(8,128)S(1)}, f32[48,384]{1,0:T(8,128)S(1)}, u32[]{:S(2)}, u32[]{:S(2)}) collective-permute-start(f32[48,384]{1,0:T(8,128)S(1)} %add.96.v0), channel_id=1, source_target_pairs={{0,64},{32,96},{64,0},{96,32},{128,192},{160,224},{192,128},{224,1... | collective-permute-start | bytes 221192 | tf_op jit(solution)/shard_map/ppermute | solution.py:25
  168.7 5.9 %collective-permute-start.28 = (f32[48,384]{1,0:T(8,128)S(1)}, f32[48,384]{1,0:T(8,128)S(1)}, u32[]{:S(2)}, u32[]{:S(2)}) collective-permute-start(f32[48,384]{1,0:T(8,128)S(1)} %add.96.v0), channel_id=1, source_target_pairs={{0,32},{32,0},{64,96},{96,64},{128,160},{160,128},{192,224},{224,1... | collective-permute-start | bytes 221192 | tf_op jit(solution)/shard_map/ppermute | solution.py:25
  170.2 3.6 %collective-permute-start.36 = (f32[8,48]{1,0:T(8,128)S(1)}, f32[8,48]{1,0:T(8,128)S(1)}, u32[]{:S(2)}, u32[]{:S(2)}) collective-permute-start(f32[8,48]{1,0:T(8,128)S(1)} %add_add_fusion.3), channel_id=1, source_target_pairs={{0,128},{32,160},{64,192},{96,224},{128,0},{160,32},{192,64},{224,... | collective-permute-start | bytes 4616 | tf_op jit(solution)/shard_map/ppermute | solution.py:25
  173.8 4.4 %copy-start.20 = (f32[8,48]{1,0:T(8,128)}, f32[8,48]{1,0:T(8,128)S(1)}, u32[]{:S(2)}) copy-start(f32[8,48]{1,0:T(8,128)S(1)} %add.102) | copy-start | bytes 4612
  (10 other events, 7.5 us)

commit v3 on v2

--- a/solution.py
+++ b/solution.py
@@ -178,8 +178,9 @@
     )(pos, keep, recv)
 
 
-def stage2_kernel(pos, a0, a1, a2, a3, held, o0, o1, o2, o3):
+def stage2_kernel(pos, a0, a1, a2, a3, small, o0, o1, o2, o3, same):
     j = pl.program_id(0)
+    same[...] = small[...]
     for n, out in enumerate((o0, o1, o2, o3)):
 
         @pl.when(j == n)
@@ -188,65 +189,66 @@
             out[...] = total.astype(out.dtype)
 
 
-def stage2(pos, a, held):
+def stage2(pos, a, small):
     width = a[0].shape[-1]
     src = pl.BlockSpec((1, 48, width), lambda j, pos: (pos[2] ^ j, 0, 0))
     return pl.pallas_call(
         stage2_kernel,
-        out_shape=tuple(sds((48, width), t) for t in (F32, BF16, BF16, BF16)),
+        out_shape=tuple(sds((48, width), t) for t in (F32, BF16, BF16, BF16)) + (sds(small.shape, F32),),
         grid_spec=pltpu.PrefetchScalarGridSpec(
             num_scalar_prefetch=1,
             grid=(4,),
-            in_specs=[src] * 4 + [HBM],
-            out_specs=(whole((48, width)),) * 4,
+            in_specs=[src] * 4 + [whole(small.shape)],
+            out_specs=(whole((48, width)),) * 4 + (whole(small.shape),),
         ),
         compiler_params=compiler(),
         name="stage2",
         **params(3),
-    )(pos, *a, held)
-
-
-def stage3_kernel(pos, v0, v1, v2, v3, held, o0, o1, o2, o3, total):
+    )(pos, *a, small)
+
+
+def stage3_kernel(pos, v0, v1, v2, v3, small, o0, o1, o2, o3, total):
     total[...] = (v0[...] + v1[...].astype(F32)) + (v2[...].astype(F32) + v3[...].astype(F32))
     for n, out in enumerate((o0, o1, o2, o3)):
         at = pl.multiple_of((pos[1] ^ n) * 384, 128)
-        out[...] = total[:, pl.ds(at, 384)]
-
-
-def stage3(pos, v, held):
+        out[0:48, :] = total[:, pl.ds(at, 384)]
+        out[48:56, :] = small[...]
+
+
+def stage3(pos, v, small):
     shape = v[0].shape
-    part = (shape[0], 384)
+    part = (shape[0] + 8, 384)
     return pl.pallas_call(
         stage3_kernel,
         out_shape=(sds(part, F32),) * 4,
         grid_spec=pltpu.PrefetchScalarGridSpec(
             num_scalar_prefetch=1,
             grid=(1,),
-            in_specs=[whole(shape)] * 4 + [HBM],
+            in_specs=[whole(shape)] * 4 + [whole(small.shape)],
             out_specs=(whole(part),) * 4,
             scratch_shapes=[pltpu.VMEM(shape, F32)],
         ),
         compiler_params=compiler(),
         name="stage3",
         **params(2),
-    )(pos, *v, held)
+    )(pos, *v, small)
 
 
 def join_kernel(pos, v0, v1, v2, v3, out):
     for n, v in enumerate((v0, v1, v2, v3)):
         at = pl.multiple_of((pos[1] ^ n) * 384, 128)
-        out[:, pl.ds(at, 384)] = v[...]
+        out[:, pl.ds(at, 384)] = v[0:48, :]
 
 
 def join(pos, parts):
-    rows = parts[0].shape[0]
+    rows = parts[0].shape[0] - 8
     return pl.pallas_call(
         join_kernel,
         out_shape=sds((rows, 1536), F32),
         grid_spec=pltpu.PrefetchScalarGridSpec(
             num_scalar_prefetch=1,
             grid=(1,),
-            in_specs=[whole((rows, 384))] * 4,
+            in_specs=[whole((rows + 8, 384))] * 4,
             out_specs=whole((rows, 1536)),
         ),
         compiler_params=compiler(),
@@ -279,12 +281,13 @@
     y, z, core = pos[0], pos[2], pos[3]
     copies = []
     for n, piece in enumerate(pieces):
-        for j in range(16):
-            index = ((y ^ (j // 4)) * 4 + (z ^ (j % 4))) * 2 + (core ^ n)
+        dc, dy = n // 4, n % 4
+        for dz in range(4):
+            index = ((y ^ dy) * 4 + (z ^ dz)) * 2 + (core ^ dc)
             at = pl.multiple_of(index * 48, 48)
             copies.append(
                 pltpu.make_async_copy(
-                    piece.at[pl.ds(j * 48, 48), :], buf.at[pl.ds(at, 48), :], sem.at[n * 16 + j]
+                    piece.at[pl.ds(dz * 48, 48), :], buf.at[pl.ds(at, 48), :], sem.at[n * 4 + dz]
                 )
             )
     for c in copies:
@@ -294,7 +297,7 @@
 
 
 def project_kernel(pos, *refs):
-    pieces, (sw, res, _, _, out, buf, sem) = refs[:2], refs[2:]
+    pieces, (sw, res, _, _, out, buf, sem) = refs[:8], refs[8:]
 
     @pl.when(pl.program_id(0) == 0)
     def _():
@@ -313,7 +316,7 @@
         grid_spec=pltpu.PrefetchScalarGridSpec(
             num_scalar_prefetch=1,
             grid=(frames // rows,),
-            in_specs=[HBM] * 2 + [block, block, HBM, HBM],
+            in_specs=[HBM] * 8 + [block, block, HBM, HBM],
             out_specs=block,
             scratch_shapes=[pltpu.VMEM((width, width), BF16), pltpu.SemaphoreType.DMA((32,))],
         ),
@@ -324,8 +327,8 @@
 
 
 def backward_kernel(pos, *refs, rows, chunk, unroll):
-    pieces = refs[:2]
-    par, cot, nrm, rst, _, gconv, sums, buf, sem, grad = refs[2:]
+    pieces = refs[:8]
+    par, cot, nrm, rst, _, gconv, sums, buf, sem, grad = refs[8:]
     step = pl.program_id(0)
     width = cot.shape[1]
     length = pos[4]
@@ -370,7 +373,7 @@
         grid_spec=pltpu.PrefetchScalarGridSpec(
             num_scalar_prefetch=1,
             grid=(frames // rows,),
-            in_specs=[HBM] * 2
+            in_specs=[HBM] * 8
             + [whole((8, width)), block(width), block(width), block(128), HBM],
             out_specs=(block(width), whole((2, 8, width))),
             scratch_shapes=[
@@ -381,7 +384,7 @@
         ),
         compiler_params=compiler(),
         name="backward",
-        **params(21),
+        **params(0.1),
     )(pos, *pieces, par, cot, nrm, rst, held)
 
 
@@ -461,6 +464,102 @@
     )(pos, par, glu, gconv, norm_sums)
 
 
+def finish_kernel(pos, *refs, rows, frames, chunk, strip):
+    pieces = refs[:8]
+    par, glu, gconv, norm_sums, sw, res, grad, out, small, buf, sem, pad, sums = refs[8:]
+    step = pl.program_id(0)
+    width = glu.shape[1]
+    length = pos[4]
+    last = frames // rows
+
+    @pl.when(step == 0)
+    def _():
+        fetch_weight(pos, pieces, buf, sem)
+        pad[pl.ds(0, PAD), :] = jnp.zeros((PAD, width), F32)
+        pad[pl.ds(PAD + frames, PAD), :] = jnp.zeros((PAD, width), F32)
+
+    @pl.when(step < 2)
+    def _():
+        sums[...] = jnp.zeros_like(sums)
+
+    @pl.when(step < last)
+    def _():
+        pad[pl.ds(pl.multiple_of(PAD + step * rows, 8), rows), :] = gconv[...]
+
+    start = jnp.maximum(step - 1, 0) * rows
+    for c in range(0, width, strip):
+        cols = slice(c, c + strip)
+        prod = jnp.dot(sw[...], buf[:, cols], preferred_element_type=F32)
+        out[:, cols] = (res[:, cols].astype(F32) + prod).astype(BF16)
+        acc = [jnp.zeros((8, strip), F32)] * TAPS
+        for at in range(0, rows, chunk):
+            base = pl.multiple_of(start + at, 8)
+            live = base + lax.broadcasted_iota(jnp.int32, (chunk, 1), 0) < length
+            mk = jnp.where(live, glu[pl.ds(at, chunk), cols].astype(F32), 0.0)
+            near = pad[pl.ds(base, chunk + 2 * PAD), cols]
+            total = None
+            for k in range(TAPS):
+                g = shifted(near, 2 - k, chunk)
+                term = par[k : k + 1, cols] * g
+                total = term if total is None else total + term
+                p = mk * g
+                acc[k] = acc[k] + sum(p[h : h + 8] for h in range(0, chunk, 8))
+            grad[pl.ds(at, chunk), cols] = jnp.where(live, total, 0.0).astype(BF16)
+        for k in range(TAPS):
+            sums[k, :, cols] += acc[k]
+
+    @pl.when(step == last)
+    def _():
+        for k in range(TAPS):
+            small[k : k + 1, :] = jnp.sum(sums[k], axis=0, keepdims=True)
+        for k in range(2):
+            small[TAPS + k : TAPS + k + 1, :] = jnp.sum(norm_sums[k], axis=0, keepdims=True)
+        small[TAPS + 2 :, :] = jnp.zeros((1, width), F32)
+
+
+def finish(pos, pieces, par, glu, gconv, norm_sums, sw, res, rows=256, chunk=32, strip=256):
+    frames, width = glu.shape
+    last = frames // rows - 1
+    late = pl.BlockSpec((rows, width), lambda i, *_: (jnp.maximum(i - 1, 0), 0))
+    soon = pl.BlockSpec((rows, width), lambda i, *_: (jnp.minimum(i, last), 0))
+    return pl.pallas_call(
+        functools.partial(finish_kernel, rows=rows, frames=frames, chunk=chunk, strip=strip),
+        out_shape=(sds((frames, width), BF16), sds((frames, width), BF16), sds((8, width), F32)),
+        grid_spec=pltpu.PrefetchScalarGridSpec(
+            num_scalar_prefetch=1,
+            grid=(frames // rows + 1,),
+            in_specs=[HBM] * 8 + [whole((8, width)), late, soon, whole((2, 8, width)), soon, soon],
+            out_specs=(late, soon, whole((8, width))),
+            scratch_shapes=[
+                pltpu.VMEM((width, width), BF16),
+                pltpu.SemaphoreType.DMA((32,)),
+                pltpu.VMEM((frames + 2 * PAD, width), F32),
+                pltpu.VMEM((TAPS, 8, width), F32),
+            ],
+        ),
+        compiler_params=compiler(),
+        name="finish",
+        **params(0.1),
+    )(pos, *pieces, par, glu, gconv, norm_sums, sw, res)
+
+
+def hold_kernel(a, b, h1, h2, h3, out):
+    out[...] = a[...] + b[...]
+
+
+def hold_add(a, b, held):
+    return pl.pallas_call(
+        hold_kernel,
+        out_shape=sds(a.shape, a.dtype),
+        grid=(1,),
+        in_specs=[whole(a.shape)] * 2 + [HBM] * 3,
+        out_specs=whole(a.shape),
+        compiler_params=compiler(),
+        name="hold_add",
+        **params(1),
+    )(a, b, *held)
+
+
 def local(glu_out, residual_in, cotangent, lengths, conv_kernel, norm_gain, norm_bias, proj_weight):
     _, frames, width = glu_out.shape
     glu, res, cot = glu_out[0], residual_in[0], cotangent[0]
@@ -480,29 +579,26 @@
 
     block = gather([proj_weight] + [fsdp_move(proj_weight, z=k) for k in (1, 2, 3)], own)
     near = [block] + [fsdp_move(block, y=k) for k in (1, 2, 3)]
+    pieces = near + [fsdp_move(p, core=1) for p in near]
 
     swished, normed, rstd = forward(lengths, par, glu)
     keep, send = outer(core[None].astype(jnp.int32), swished, cot, near[1:])
     recv = fsdp_move(send, core=1)
     a = stage1(pos, keep, recv)
-    mine = gather(near, a[0])
-    pieces = [mine, fsdp_move(mine, core=1)]
     gconv, sums = backward(pos, pieces, par, cot, normed, rstd, a[0])
-    glu_grad, small = taps(pos, par, glu, gconv, sums)
-    v = stage2(pos, [a[0]] + [fsdp_move(a[k], y=k) for k in (1, 2, 3)], glu_grad)
+    glu_grad, block_out, small = finish(pos, pieces, par, glu, gconv, sums, swished, res)
+    *v, small = stage2(pos, [a[0]] + [fsdp_move(a[k], y=k) for k in (1, 2, 3)], small)
     small = small + fsdp_move(small, core=1)
     small = (small + fsdp_move(small, y=1)) + (fsdp_move(small, y=2) + fsdp_move(small, y=3))
-    block_out = project(pos, pieces, swished, res, (v[0], small))
-    v = stage3(pos, [v[0]] + [fsdp_move(v[k], z=k) for k in (1, 2, 3)], block_out)
+    v = [v[0]] + [fsdp_move(v[k], z=k) for k in (1, 2, 3)]
+    small = hold_add(small, fsdp_move(small, z=1), v[1:])
+    small = small + fsdp_move(small, z=3)
+    small = jnp.pad(lax.dynamic_slice(small, (0, f * 48), (8, 48)), ((0, 0), (0, 336)))
+    v = stage3(pos, v, small)
     total = (v[0] + dp_move(v[1], x=1)) + (dp_move(v[2], x=2) + dp_move(v[3], x=3))
     total = total + dp_move(total, low=1)
     proj_grad = join(pos, [total] + [dp_move(total, x=k) for k in (1, 2, 3)])
-
-    small = small + fsdp_move(small, z=1)
-    small = small + fsdp_move(small, z=3)
-    small = lax.dynamic_slice(small, (0, f * 48), (8, 48))
-    small = (small + dp_move(small, x=1)) + (dp_move(small, x=2) + dp_move(small, x=3))
-    small = small + dp_move(small, low=1)
+    small = total[48:, :48]
     return (block_out[None], glu_grad[None], proj_grad, small[:TAPS], small[TAPS : TAPS + 2])
 
 

time: 179 us -> 193 us (1.078)
  waiting for transfers between devices: 32.7 us -> 52.2 us
  Pallas kernels: 73.7 us -> 69.8 us
    ppermute x26 -> x29, waiting for transfers between devices: 29 us -> 40.1 us  [fsdp_move(): return lax.ppermute(value, 'fsdp', perm)]
    ppermute x11 -> x7, waiting for transfers between devices: 3.74 us -> 12.1 us  [dp_move(): return lax.ppermute(value, 'dp', perm)]
    ppermute x11 -> x7, starting transfers between devices: 15.7 us -> 9.57 us  [dp_move(): return lax.ppermute(value, 'dp', perm)]
    ppermute x26 -> x29, starting transfers between devices: 41.3 us -> 46.8 us  [fsdp_move(): return lax.ppermute(value, 'fsdp', perm)]
    pallas_call x2 -> x1, Pallas kernels: 5.11 us -> 1.98 us  [gather(): pl.pallas_call(gather_kernel, out_shape=sds((4 * rows, width), BF16), gri...]
    unnamed x42 -> x46, local copies, waits for them, and re-layouts: 7.22 us -> 4.83 us
  transfers between devices with their start and end apart: 37 -> 36, of which waited for: 15 -> 16; matrix products, arithmetic and copies ran while one was open for 3% -> 2% of each run, Pallas kernels for 29% -> 27%
where the time goes in v3:
time: 193 us; the launch traced here: 192 us
  Pallas kernels  69.8 us (36%)
  starting transfers between devices  56.3 us (29%)
  waiting for transfers between devices  52.2 us (27%)
  local copies, waits for them, and re-layouts  7.51 us (4%)
  other arithmetic  4.66 us (2%)
    ppermute x29, starting transfers between devices, fsdp_move(): return lax.ppermute(value, 'fsdp', perm)  46.8 us
    ppermute x29, waiting for transfers between devices, fsdp_move(): return lax.ppermute(value, 'fsdp', perm)  40.1 us
    pallas_call x1, Pallas kernels, finish(): pl.pallas_call(functools.partial(finish_kernel, rows=rows, frames=frames,...  17.7 us
    pallas_call x1, Pallas kernels, backward(): pl.pallas_call(functools.partial(backward_kernel, rows=rows, chunk=chunk,...  15.7 us
    ppermute x7, waiting for transfers between devices, dp_move(): return lax.ppermute(value, 'dp', perm)  12.1 us
    pallas_call x1, Pallas kernels, forward(): pl.pallas_call(functools.partial(forward_kernel, rows=rows, frames=frames...  9.57 us
    ppermute x7, starting transfers between devices, dp_move(): return lax.ppermute(value, 'dp', perm)  9.57 us
    pallas_call x1, Pallas kernels, outer(): pl.pallas_call(outer_kernel, out_shape=(sds((16, 48, width), F32), sds((1...  8.11 us
  transfers between devices with their start and end apart: 36, of which 16 were waited for; matrix products, arithmetic and copies ran while one was open for 2% of the time, Pallas kernels for 27%

profile of v3, /device:TPU:32, one launch (start us, length us, event | category | flops | bytes accessed | tf_op | source)
XLA Modules:
  0.0 192.0 jit_solution(7456658637617533160)
XLA Ops:
  0.6 3.4 %collective-permute-start = (bf16[48,1536]{1,0:T(8,128)(2,1)}, bf16[48,1536]{1,0:T(8,128)(2,1)S(1)}, u32[]{:S(2)}, u32[]{:S(2)}) collective-permute-start(bf16[48,1536]{1,0:T(8,128)(2,1)} %w0.1), channel_id=1, source_target_pairs={{0,2},{1,3},{2,0},{3,1},{4,6},{5,7},{6,4},{7,5},{8,10},{9,11},{10,... | collective-permute-start | bytes 442376 | tf_op jit(solution)/shard_map/ppermute | solution.py:20
  5.0 4.6 %collective-permute-start.1 = (bf16[48,1536]{1,0:T(8,128)(2,1)}, bf16[48,1536]{1,0:T(8,128)(2,1)S(1)}, u32[]{:S(2)}, u32[]{:S(2)}) collective-permute-start(bf16[48,1536]{1,0:T(8,128)(2,1)} %w0.1), channel_id=1, source_target_pairs={{0,4},{1,5},{2,6},{3,7},{4,0},{5,1},{6,2},{7,3},{8,12},{9,13},{10,... | collective-permute-start | bytes 442376 | tf_op jit(solution)/shard_map/ppermute | solution.py:20
  10.6 1.7 collective-permute-start.11
  12.2 2.9 %collective-permute-start.12 = (bf16[8,1536]{1,0:T(8,128)(2,1)S(1)}, bf16[8,1536]{1,0:T(8,128)(2,1)S(1)}, u32[]{:S(2)}, u32[]{:S(2)}) collective-permute-start(bf16[8,1536]{1,0:T(8,128)(2,1)S(1)} %add.70), channel_id=1, source_target_pairs={{0,16},{1,17},{2,18},{3,19},{4,20},{5,21},{6,22},{7,23},{8,24},{9,... | collective-permute-start | bytes 73736 | tf_op jit(solution)/shard_map/ppermute | solution.py:20
  15.1 3.2 %collective-permute-start.13 = (bf16[8,1536]{1,0:T(8,128)(2,1)S(1)}, bf16[8,1536]{1,0:T(8,128)(2,1)S(1)}, u32[]{:S(2)}, u32[]{:S(2)}) collective-permute-start(bf16[8,1536]{1,0:T(8,128)(2,1)S(1)} %add.70), channel_id=1, source_target_pairs={{0,24},{1,25},{2,26},{3,27},{4,28},{5,29},{6,30},{7,31},{8,16},{9,... | collective-permute-start | bytes 73736 | tf_op jit(solution)/shard_map/ppermute | solution.py:20
  18.4 3.0 %collective-permute-done.1.w2 = bf16[48,1536]{1,0:T(8,128)(2,1)S(1)} collective-permute-done((bf16[48,1536]{1,0:T(8,128)(2,1)}, bf16[48,1536]{1,0:T(8,128)(2,1)S(1)}, u32[]{:S(2)}, u32[]{:S(2)}) %collective-permute-start.1) | collective-permute-done | bytes 147488 | tf_op jit(solution)/shard_map/ppermute | solution.py:20
  21.4 2.1 %collective-permute-done.2.w3 = bf16[48,1536]{1,0:T(8,128)(2,1)S(1)} collective-permute-done((bf16[48,1536]{1,0:T(8,128)(2,1)}, bf16[48,1536]{1,0:T(8,128)(2,1)S(1)}, u32[]{:S(2)}, u32[]{:S(2)}) %collective-permute-start.2) | collective-permute-done | bytes 147488 | tf_op jit(solution)/shard_map/ppermute | solution.py:20
  24.2 2.0 %gather.1.refs_0_ = bf16[192,1536]{1,0:T(8,128)(2,1)} custom-call(bf16[48,1536]{1,0:T(8,128)(2,1)} %w0.1, bf16[48,1536]{1,0:T(8,128)(2,1)} %copy-done.15, bf16[48,1536]{1,0:T(8,128)(2,1)} %copy-done.16, bf16[48,1536]{1,0:T(8,128)(2,1)} %copy-done.17, bf16[8,48]{1,0:T(8,128)(2,1)} %copy-done.22), custom_call_target="tpu_custom_call" | custom-call | bytes 360000 | tf_op jit(solution)/shard_map/gather/pallas_call | solution.py:268
  26.2 1.4 collective-permute-start.3
  27.5 2.9 %collective-permute-start.4 = (bf16[192,1536]{1,0:T(8,128)(2,1)}, bf16[192,1536]{1,0:T(8,128)(2,1)S(1)}, u32[]{:S(2)}, u32[]{:S(2)}) collective-permute-start(bf16[192,1536]{1,0:T(8,128)(2,1)} %gather.1.refs_0_), channel_id=1, source_target_pairs={{0,16},{1,17},{2,18},{3,19},{4,20},{5,21},{6,22},{7,23},{8,24},{9,... | collective-permute-start | bytes 1769480 | tf_op jit(solution)/shard_map/ppermute | solution.py:20
  30.9 1.4 collective-permute-start.14
  32.3 3.4 %collective-permute-done.14 = bf16[8,1536]{1,0:T(8,128)(2,1)S(1)} collective-permute-done((bf16[8,1536]{1,0:T(8,128)(2,1)S(1)}, bf16[8,1536]{1,0:T(8,128)(2,1)S(1)}, u32[]{:S(2)}, u32[]{:S(2)}) %collective-permute-start.14) | collective-permute-done | bytes 24608 | tf_op jit(solution)/shard_map/ppermute | solution.py:20
  35.7 3.0 %collective-permute-start.15 = (bf16[8,1536]{1,0:T(8,128)(2,1)S(1)}, bf16[8,1536]{1,0:T(8,128)(2,1)S(1)}, u32[]{:S(2)}, u32[]{:S(2)}) collective-permute-start(bf16[8,1536]{1,0:T(8,128)(2,1)S(1)} %add.74), channel_id=1, source_target_pairs={{0,6},{1,7},{2,4},{3,5},{4,2},{5,3},{6,0},{7,1},{8,14},{9,15},{10,... | collective-permute-start | bytes 73736 | tf_op jit(solution)/shard_map/ppermute | solution.py:20
  39.3 2.4 %collective-permute-done.15 = bf16[8,1536]{1,0:T(8,128)(2,1)S(1)} collective-permute-done((bf16[8,1536]{1,0:T(8,128)(2,1)S(1)}, bf16[8,1536]{1,0:T(8,128)(2,1)S(1)}, u32[]{:S(2)}, u32[]{:S(2)}) %collective-permute-start.15) | collective-permute-done | bytes 24608 | tf_op jit(solution)/shard_map/ppermute | solution.py:20
  42.4 9.6 %forward.1 = (bf16[768,1536]{1,0:T(8,128)(2,1)}, f32[768,1536]{1,0:T(8,128)}, f32[768,128]{1,0:T(8,128)}) custom-call(s32[1]{0:T(128)S(6)} %copy.15.lens, f32[8,1536]{1,0:T(8,128)} %add_convert_fusion.par.refs_8_, bf16[768,1536]{1,0:T(8,128)(2,1)} %bitcast.15), custom_call_target="tpu_custom_call" | custom-call | bytes 360000 | tf_op jit(solution)/shard_map/forward/pallas_call | solution.py:98
  51.9 4.7 %collective-permute-done.4.h2.refs_2_ = bf16[192,1536]{1,0:T(8,128)(2,1)S(1)} collective-permute-done((bf16[192,1536]{1,0:T(8,128)(2,1)}, bf16[192,1536]{1,0:T(8,128)(2,1)S(1)}, u32[]{:S(2)}, u32[]{:S(2)}) %collective-permute-start.4) | collective-permute-done | bytes 589856 | tf_op jit(solution)/shard_map/ppermute | solution.py:20
  56.6 2.6 %collective-permute-done.5.h3.refs_3_ = bf16[192,1536]{1,0:T(8,128)(2,1)S(1)} collective-permute-done((bf16[192,1536]{1,0:T(8,128)(2,1)}, bf16[192,1536]{1,0:T(8,128)(2,1)S(1)}, u32[]{:S(2)}, u32[]{:S(2)}) %collective-permute-start.5) | collective-permute-done | bytes 589856 | tf_op jit(solution)/shard_map/ppermute | solution.py:20
  60.0 8.1 %outer.1 = (f32[16,48,1536]{2,1,0:T(8,128)}, bf16[16,48,1536]{2,1,0:T(8,128)(2,1)}) custom-call(s32[1]{0:T(128)} %bitcast.3.core, bf16[768,1536]{1,0:T(8,128)(2,1)} %get-tuple-element.30.sw.refs_12_, bf16[768,1536]{1,0:T(8,128)(2,1)} %bitcast.13, bf16[192,1536]{1,0:T(8,128)(2,1)} %copy-done, bf16[192,1536]{1,0:T(8,128)(2,1)} %copy-done.1, ...), custom_call_target="tpu_custom_call" | custom-call | bytes 360000 | tf_op jit(solution)/shard_map/outer/pallas_call | solution.py:128
  69.9 5.5 %collective-permute-done.16 = bf16[16,48,1536]{2,1,0:T(8,128)(2,1)} collective-permute-done((bf16[16,48,1536]{2,1,0:T(8,128)(2,1)}, bf16[16,48,1536]{2,1,0:T(8,128)(2,1)}, u32[]{:S(2)}, u32[]{:S(2)}) %collective-permute-start.16) | collective-permute-done | bytes 2359328 | tf_op jit(solution)/shard_map/ppermute | solution.py:20
  75.4 6.0 %stage1.1 = (f32[4,48,1536]{2,1,0:T(8,128)}, bf16[4,48,1536]{2,1,0:T(8,128)(2,1)}, bf16[4,48,1536]{2,1,0:T(8,128)(2,1)}, bf16[4,48,1536]{2,1,0:T(8,128)(2,1)}) custom-call(s32[5]{0:T(128)} %stack.19.pos, f32[4,4,48,1536]{3,2,1,0:T(8,128)} %bitcast.17, bf16[4,4,48,1536]{3,2,1,0:T(8,128)(2,1)} %bitcast.9.recv), custom_call_target="tpu_custom_call" | custom-call | bytes 360000 | tf_op jit(solution)/shard_map/stage1/pallas_call | solution.py:166
  81.4 1.9 collective-permute-start.18
  83.3 2.8 %collective-permute-start.19 = (bf16[4,48,1536]{2,1,0:T(8,128)(2,1)}, bf16[4,48,1536]{2,1,0:T(8,128)(2,1)}, u32[]{:S(2)}, u32[]{:S(2)}) collective-permute-start(bf16[4,48,1536]{2,1,0:T(8,128)(2,1)} %get-tuple-element.40), channel_id=1, source_target_pairs={{0,24},{1,25},{2,26},{3,27},{4,28},{5,29},{6,30},{7,31},{8,16},{9,... | collective-permute-start | bytes 1769480 | tf_op jit(solution)/shard_map/ppermute | solution.py:20
  87.2 15.7 %backward.1 = (f32[768,1536]{1,0:T(8,128)}, f32[2,8,1536]{2,1,0:T(8,128)}) custom-call(s32[5]{0:T(128)} %stack.19.pos, bf16[192,1536]{1,0:T(8,128)(2,1)} %gather.1.refs_0_, bf16[192,1536]{1,0:T(8,128)(2,1)} %copy-done, bf16[192,1536]{1,0:T(8,128)(2,1)} %copy-done.1, bf16[192,1536]{1,0:T(8,128)(2,1)} %copy-done.2, bf16[192,1536]{1,0:T(8,128)(2,1)} %copy-done.4, ...), custom_call_target="tpu_custom_call" | custom-call | bytes 360000 | tf_op jit(solution)/shard_map/backward/pallas_call | solution.py:370
  102.9 17.7 %finish.1 = (bf16[768,1536]{1,0:T(8,128)(2,1)}, bf16[768,1536]{1,0:T(8,128)(2,1)}, f32[8,1536]{1,0:T(8,128)}) custom-call(s32[5]{0:T(128)} %stack.19.pos, bf16[192,1536]{1,0:T(8,128)(2,1)} %gather.1.refs_0_, bf16[192,1536]{1,0:T(8,128)(2,1)} %copy-done, bf16[192,1536]{1,0:T(8,128)(2,1)} %copy-done.1, bf16[192,1536]{1,0:T(8,128)(2,1)} %copy-done.2, ...), custom_call_target="tpu_custom_call" | custom-call | bytes 360000 | tf_op jit(solution)/shard_map/finish/pallas_call | solution.py:525
  121.6 4.2 %stage2.1 = (f32[48,1536]{1,0:T(8,128)}, bf16[48,1536]{1,0:T(8,128)(2,1)}, bf16[48,1536]{1,0:T(8,128)(2,1)}, bf16[48,1536]{1,0:T(8,128)(2,1)}, f32[8,1536]{1,0:T(8,128)}) custom-call(s32[5]{0:T(128)} %stack.19.pos, f32[4,48,1536]{2,1,0:T(8,128)} %get-tuple-element.33.refs_12_.a0, bf16[4,48,1536]{2,1,0:T(8,128)(2,1)} %copy-done.8, ...), custom_call_target="tpu_custom_call" | custom-call | bytes 10800000 | tf_op jit(solution)/shard_map/stage2/pallas_call | solution.py:195
  125.9 1.4 collective-permute-done.23
  128.2 1.9 collective-permute-start.25
  130.1 2.8 %collective-permute-start.26 = (f32[8,1536]{1,0:T(8,128)S(1)}, f32[8,1536]{1,0:T(8,128)S(1)}, u32[]{:S(2)}, u32[]{:S(2)}) collective-permute-start(f32[8,1536]{1,0:T(8,128)S(1)} %add.76), channel_id=1, source_target_pairs={{0,24},{1,25},{2,26},{3,27},{4,28},{5,29},{6,30},{7,31},{8,16},{9,... | collective-permute-start | bytes 147464 | tf_op jit(solution)/shard_map/ppermute | solution.py:20
  132.9 1.3 collective-permute-start.20
  134.2 3.9 %collective-permute-start.21 = (bf16[48,1536]{1,0:T(8,128)(2,1)}, bf16[48,1536]{1,0:T(8,128)(2,1)S(1)}, u32[]{:S(2)}, u32[]{:S(2)}) collective-permute-start(bf16[48,1536]{1,0:T(8,128)(2,1)} %get-tuple-element.44), channel_id=1, source_target_pairs={{0,4},{1,5},{2,6},{3,7},{4,0},{5,1},{6,2},{7,3},{8,12},{9,13},{10,... | collective-permute-start | bytes 442376 | tf_op jit(solution)/shard_map/ppermute | solution.py:20
  138.1 1.3 collective-permute-start.22
  139.4 1.7 collective-permute-start.27
  141.1 9.0 %collective-permute-done.27.b = f32[8,1536]{1,0:T(8,128)S(1)} collective-permute-done((f32[8,1536]{1,0:T(8,128)S(1)}, f32[8,1536]{1,0:T(8,128)S(1)}, u32[]{:S(2)}, u32[]{:S(2)}) %collective-permute-start.27) | collective-permute-done | bytes 49184 | tf_op jit(solution)/shard_map/ppermute | solution.py:20
  150.2 2.3 %collective-permute-done.22.h3.v3 = bf16[48,1536]{1,0:T(8,128)(2,1)S(1)} collective-permute-done((bf16[48,1536]{1,0:T(8,128)(2,1)}, bf16[48,1536]{1,0:T(8,128)(2,1)S(1)}, u32[]{:S(2)}, u32[]{:S(2)}) %collective-permute-start.22) | collective-permute-done | bytes 147488 | tf_op jit(solution)/shard_map/ppermute | solution.py:20
  153.2 1.4 hold_add.1
  154.6 3.0 %collective-permute-start.28 = (f32[8,1536]{1,0:T(8,128)}, f32[8,1536]{1,0:T(8,128)S(1)}, u32[]{:S(2)}, u32[]{:S(2)}) collective-permute-start(f32[8,1536]{1,0:T(8,128)} %hold_add.1), channel_id=1, source_target_pairs={{0,6},{1,7},{2,4},{3,5},{4,2},{5,3},{6,0},{7,1},{8,14},{9,15},{10,... | collective-permute-start | bytes 147464 | tf_op jit(solution)/shard_map/ppermute | solution.py:20
  157.6 3.5 %collective-permute-done.28 = f32[8,1536]{1,0:T(8,128)S(1)} collective-permute-done((f32[8,1536]{1,0:T(8,128)}, f32[8,1536]{1,0:T(8,128)S(1)}, u32[]{:S(2)}, u32[]{:S(2)}) %collective-permute-start.28) | collective-permute-done | bytes 49184 | tf_op jit(solution)/shard_map/ppermute | solution.py:20
  162.5 2.6 %stage3.1 = (f32[56,384]{1,0:T(8,128)}, f32[56,384]{1,0:T(8,128)}, f32[56,384]{1,0:T(8,128)}, f32[56,384]{1,0:T(8,128)}) custom-call(s32[5]{0:T(128)} %stack.19.pos, f32[48,1536]{1,0:T(8,128)} %get-tuple-element.42.v0, bf16[48,1536]{1,0:T(8,128)(2,1)} %copy-done.10, bf16[48,1536]{1,0:T(8,128)(2,1)} %copy-done.11, bf16[48,1536]{1,0:T(8,128)(2,1)} %copy-done.12, ...), custom_call_target="tpu_custom_call" | custom-call | bytes 7200000 | tf_op jit(solution)/shard_map/stage3/pallas_call | solution.py:221
  165.2 1.5 collective-permute-start.29
  166.7 2.7 %collective-permute-start.30 = (f32[56,384]{1,0:T(8,128)}, f32[56,384]{1,0:T(8,128)S(1)}, u32[]{:S(2)}, u32[]{:S(2)}) collective-permute-start(f32[56,384]{1,0:T(8,128)} %get-tuple-element.49), channel_id=1, source_target_pairs={{0,64},{32,96},{64,0},{96,32},{128,192},{160,224},{192,128},{224,1... | collective-permute-start | bytes 258056 | tf_op jit(solution)/shard_map/ppermute | solution.py:25
  169.9 3.7 %collective-permute-done.30 = f32[56,384]{1,0:T(8,128)S(1)} collective-permute-done((f32[56,384]{1,0:T(8,128)}, f32[56,384]{1,0:T(8,128)S(1)}, u32[]{:S(2)}, u32[]{:S(2)}) %collective-permute-start.30) | collective-permute-done | bytes 86048 | tf_op jit(solution)/shard_map/ppermute | solution.py:25
  173.7 1.7 collective-permute-done.31
  175.3 0.9 add_add_fusion
  176.3 4.5 %collective-permute-done.32 = f32[56,384]{1,0:T(8,128)S(1)} collective-permute-done((f32[56,384]{1,0:T(8,128)S(1)}, f32[56,384]{1,0:T(8,128)S(1)}, u32[]{:S(2)}, u32[]{:S(2)}) %collective-permute-start.32) | collective-permute-done | bytes 86048 | tf_op jit(solution)/shard_map/ppermute | solution.py:25
  180.9 2.4 %collective-permute-start.34 = (f32[56,384]{1,0:T(8,128)S(1)}, f32[56,384]{1,0:T(8,128)S(1)}, u32[]{:S(2)}, u32[]{:S(2)}) collective-permute-start(f32[56,384]{1,0:T(8,128)S(1)} %add.84.v0), channel_id=1, source_target_pairs={{0,64},{32,96},{64,0},{96,32},{128,192},{160,224},{192,128},{224,1... | collective-permute-start | bytes 258056 | tf_op jit(solution)/shard_map/ppermute | solution.py:25
  183.3 2.3 %collective-permute-start.35 = (f32[56,384]{1,0:T(8,128)S(1)}, f32[56,384]{1,0:T(8,128)S(1)}, u32[]{:S(2)}, u32[]{:S(2)}) collective-permute-start(f32[56,384]{1,0:T(8,128)S(1)} %add.84.v0), channel_id=1, source_target_pairs={{0,96},{32,64},{64,32},{96,0},{128,224},{160,192},{192,160},{224,1... | collective-permute-start | bytes 258056 | tf_op jit(solution)/shard_map/ppermute | solution.py:25
  187.0 2.0 %collective-permute-done.35.v3 = f32[56,384]{1,0:T(8,128)S(1)} collective-permute-done((f32[56,384]{1,0:T(8,128)S(1)}, f32[56,384]{1,0:T(8,128)S(1)}, u32[]{:S(2)}, u32[]{:S(2)}) %collective-permute-start.35) | collective-permute-done | bytes 86048 | tf_op jit(solution)/shard_map/ppermute | solution.py:25
  189.6 2.4 %join.1 = f32[48,1536]{1,0:T(8,128)} custom-call(s32[5]{0:T(128)} %stack.19.pos, f32[56,384]{1,0:T(8,128)} %copy-done.13, f32[56,384]{1,0:T(8,128)} %copy-done.18, f32[56,384]{1,0:T(8,128)} %copy-done.19, f32[56,384]{1,0:T(8,128)} %copy-done.20), custom_call_target="tpu_custom_call" | custom-call | bytes 7200000 | tf_op jit(solution)/shard_map/join/pallas_call | solution.py:245
  (97 shorter events, 14.0 us)
Async XLA Ops:
  0.6 14.5 %collective-permute-start = (bf16[48,1536]{1,0:T(8,128)(2,1)}, bf16[48,1536]{1,0:T(8,128)(2,1)S(1)}, u32[]{:S(2)}, u32[]{:S(2)}) collective-permute-start(bf16[48,1536]{1,0:T(8,128)(2,1)} %w0.1), channel_id=1, source_target_pairs={{0,2},{1,3},{2,0},{3,1},{4,6},{5,7},{6,4},{7,5},{8,10},{9,11},{10,... | collective-permute-start | bytes 442376 | tf_op jit(solution)/shard_map/ppermute | solution.py:20
  4.7 18.8 %copy-start.22 = (bf16[8,48]{1,0:T(8,128)(2,1)}, bf16[8,48]{1,0:T(8,128)(2,1)S(1)}, u32[]{:S(2)}) copy-start(bf16[8,48]{1,0:T(8,128)(2,1)S(1)} %fusion.4.held) | copy-start | bytes 2308
  4.9 4.7 %collective-permute-start.10 = (bf16[8,1536]{1,0:T(8,128)(2,1)S(1)}, bf16[8,1536]{1,0:T(8,128)(2,1)S(1)}, u32[]{:S(2)}, u32[]{:S(2)}) collective-permute-start(bf16[8,1536]{1,0:T(8,128)(2,1)S(1)} %dynamic_update_slice.5), channel_id=1, source_target_pairs={{0,1},{1,0},{2,3},{3,2},{4,5},{5,4},{6,7},{7,6},{8,9},{9,8},{10,11... | collective-permute-start | bytes 73736 | tf_op jit(solution)/shard_map/ppermute | solution.py:20
  5.0 16.4 %collective-permute-start.1 = (bf16[48,1536]{1,0:T(8,128)(2,1)}, bf16[48,1536]{1,0:T(8,128)(2,1)S(1)}, u32[]{:S(2)}, u32[]{:S(2)}) collective-permute-start(bf16[48,1536]{1,0:T(8,128)(2,1)} %w0.1), channel_id=1, source_target_pairs={{0,4},{1,5},{2,6},{3,7},{4,0},{5,1},{6,2},{7,3},{8,12},{9,13},{10,... | collective-permute-start | bytes 442376 | tf_op jit(solution)/shard_map/ppermute | solution.py:20
  9.7 13.9 %collective-permute-start.2 = (bf16[48,1536]{1,0:T(8,128)(2,1)}, bf16[48,1536]{1,0:T(8,128)(2,1)S(1)}, u32[]{:S(2)}, u32[]{:S(2)}) collective-permute-start(bf16[48,1536]{1,0:T(8,128)(2,1)} %w0.1), channel_id=1, source_target_pairs={{0,6},{1,7},{2,4},{3,5},{4,2},{5,3},{6,0},{7,1},{8,14},{9,15},{10,... | collective-permute-start | bytes 442376 | tf_op jit(solution)/shard_map/ppermute | solution.py:20
  10.6 19.9 %collective-permute-start.11 = (bf16[8,1536]{1,0:T(8,128)(2,1)S(1)}, bf16[8,1536]{1,0:T(8,128)(2,1)S(1)}, u32[]{:S(2)}, u32[]{:S(2)}) collective-permute-start(bf16[8,1536]{1,0:T(8,128)(2,1)S(1)} %add.70), channel_id=1, source_target_pairs={{0,8},{1,9},{2,10},{3,11},{4,12},{5,13},{6,14},{7,15},{8,0},{9,1},... | collective-permute-start | bytes 73736 | tf_op jit(solution)/shard_map/ppermute | solution.py:20
  12.2 18.7 %collective-permute-start.12 = (bf16[8,1536]{1,0:T(8,128)(2,1)S(1)}, bf16[8,1536]{1,0:T(8,128)(2,1)S(1)}, u32[]{:S(2)}, u32[]{:S(2)}) collective-permute-start(bf16[8,1536]{1,0:T(8,128)(2,1)S(1)} %add.70), channel_id=1, source_target_pairs={{0,16},{1,17},{2,18},{3,19},{4,20},{5,21},{6,22},{7,23},{8,24},{9,... | collective-permute-start | bytes 73736 | tf_op jit(solution)/shard_map/ppermute | solution.py:20
  15.1 8.4 %copy-start.15 = (bf16[48,1536]{1,0:T(8,128)(2,1)}, bf16[48,1536]{1,0:T(8,128)(2,1)S(1)}, u32[]{:S(2)}) copy-start(bf16[48,1536]{1,0:T(8,128)(2,1)S(1)} %collective-permute-done.w1) | copy-start | bytes 442372
  15.1 15.8 %collective-permute-start.13 = (bf16[8,1536]{1,0:T(8,128)(2,1)S(1)}, bf16[8,1536]{1,0:T(8,128)(2,1)S(1)}, u32[]{:S(2)}, u32[]{:S(2)}) collective-permute-start(bf16[8,1536]{1,0:T(8,128)(2,1)S(1)} %add.70), channel_id=1, source_target_pairs={{0,24},{1,25},{2,26},{3,27},{4,28},{5,29},{6,30},{7,31},{8,16},{9,... | collective-permute-start | bytes 73736 | tf_op jit(solution)/shard_map/ppermute | solution.py:20
  26.2 25.8 %collective-permute-start.3 = (bf16[192,1536]{1,0:T(8,128)(2,1)}, bf16[192,1536]{1,0:T(8,128)(2,1)S(1)}, u32[]{:S(2)}, u32[]{:S(2)}) collective-permute-start(bf16[192,1536]{1,0:T(8,128)(2,1)} %gather.1.refs_0_), channel_id=1, source_target_pairs={{0,8},{1,9},{2,10},{3,11},{4,12},{5,13},{6,14},{7,15},{8,0},{9,1},... | collective-permute-start | bytes 1769480 | tf_op jit(solution)/shard_map/ppermute | solution.py:20
  27.5 29.1 %collective-permute-start.4 = (bf16[192,1536]{1,0:T(8,128)(2,1)}, bf16[192,1536]{1,0:T(8,128)(2,1)S(1)}, u32[]{:S(2)}, u32[]{:S(2)}) collective-permute-start(bf16[192,1536]{1,0:T(8,128)(2,1)} %gather.1.refs_0_), channel_id=1, source_target_pairs={{0,16},{1,17},{2,18},{3,19},{4,20},{5,21},{6,22},{7,23},{8,24},{9,... | collective-permute-start | bytes 1769480 | tf_op jit(solution)/shard_map/ppermute | solution.py:20
  30.4 28.8 %collective-permute-start.5 = (bf16[192,1536]{1,0:T(8,128)(2,1)}, bf16[192,1536]{1,0:T(8,128)(2,1)S(1)}, u32[]{:S(2)}, u32[]{:S(2)}) collective-permute-start(bf16[192,1536]{1,0:T(8,128)(2,1)} %gather.1.refs_0_), channel_id=1, source_target_pairs={{0,24},{1,25},{2,26},{3,27},{4,28},{5,29},{6,30},{7,31},{8,16},{9,... | collective-permute-start | bytes 1769480 | tf_op jit(solution)/shard_map/ppermute | solution.py:20
  30.9 4.8 %collective-permute-start.14 = (bf16[8,1536]{1,0:T(8,128)(2,1)S(1)}, bf16[8,1536]{1,0:T(8,128)(2,1)S(1)}, u32[]{:S(2)}, u32[]{:S(2)}) collective-permute-start(bf16[8,1536]{1,0:T(8,128)(2,1)S(1)} %add_add_fusion.2), channel_id=1, source_target_pairs={{0,2},{1,3},{2,0},{3,1},{4,6},{5,7},{6,4},{7,5},{8,10},{9,11},{10,... | collective-permute-start | bytes 73736 | tf_op jit(solution)/shard_map/ppermute | solution.py:20
  35.7 6.0 %collective-permute-start.15 = (bf16[8,1536]{1,0:T(8,128)(2,1)S(1)}, bf16[8,1536]{1,0:T(8,128)(2,1)S(1)}, u32[]{:S(2)}, u32[]{:S(2)}) collective-permute-start(bf16[8,1536]{1,0:T(8,128)(2,1)S(1)} %add.74), channel_id=1, source_target_pairs={{0,6},{1,7},{2,4},{3,5},{4,2},{5,3},{6,0},{7,1},{8,14},{9,15},{10,... | collective-permute-start | bytes 73736 | tf_op jit(solution)/shard_map/ppermute | solution.py:20
  51.9 7.3 %copy-start = (bf16[192,1536]{1,0:T(8,128)(2,1)}, bf16[192,1536]{1,0:T(8,128)(2,1)S(1)}, u32[]{:S(2)}) copy-start(bf16[192,1536]{1,0:T(8,128)(2,1)S(1)} %collective-permute-done.3.h1.refs_1_) | copy-start | bytes 1769476
  56.6 2.6 %copy-start.1 = (bf16[192,1536]{1,0:T(8,128)(2,1)}, bf16[192,1536]{1,0:T(8,128)(2,1)S(1)}, u32[]{:S(2)}) copy-start(bf16[192,1536]{1,0:T(8,128)(2,1)S(1)} %collective-permute-done.4.h2.refs_2_) | copy-start | bytes 1769476
  60.0 8.1 %copy-start.3 = (bf16[192,1536]{1,0:T(8,128)(2,1)S(1)}, bf16[192,1536]{1,0:T(8,128)(2,1)}, u32[]{:S(2)}) copy-start(bf16[192,1536]{1,0:T(8,128)(2,1)} %gather.1.refs_0_) | copy-start | bytes 1769476
  68.1 7.3 %collective-permute-start.16 = (bf16[16,48,1536]{2,1,0:T(8,128)(2,1)}, bf16[16,48,1536]{2,1,0:T(8,128)(2,1)}, u32[]{:S(2)}, u32[]{:S(2)}) collective-permute-start(bf16[16,48,1536]{2,1,0:T(8,128)(2,1)} %get-tuple-element.32), channel_id=1, source_target_pairs={{0,1},{1,0},{2,3},{3,2},{4,5},{5,4},{6,7},{7,6},{8,9},{9,8},{10,11... | collective-permute-start | bytes 7077896 | tf_op jit(solution)/shard_map/ppermute | solution.py:20
  68.1 13.3 %collective-permute-start.6 = (bf16[192,1536]{1,0:T(8,128)(2,1)S(1)}, bf16[192,1536]{1,0:T(8,128)(2,1)S(1)}, u32[]{:S(2)}, u32[]{:S(2)}) collective-permute-start(bf16[192,1536]{1,0:T(8,128)(2,1)S(1)} %copy-done.3), channel_id=1, source_target_pairs={{0,1},{1,0},{2,3},{3,2},{4,5},{5,4},{6,7},{7,6},{8,9},{9,8},{10,11... | collective-permute-start | bytes 1769480 | tf_op jit(solution)/shard_map/ppermute | solution.py:20
  68.6 14.7 %collective-permute-start.7 = (bf16[192,1536]{1,0:T(8,128)(2,1)}, bf16[192,1536]{1,0:T(8,128)(2,1)S(1)}, u32[]{:S(2)}, u32[]{:S(2)}) collective-permute-start(bf16[192,1536]{1,0:T(8,128)(2,1)} %copy-done), channel_id=1, source_target_pairs={{0,1},{1,0},{2,3},{3,2},{4,5},{5,4},{6,7},{7,6},{8,9},{9,8},{10,11... | collective-permute-start | bytes 1769480 | tf_op jit(solution)/shard_map/ppermute | solution.py:20
  69.4 16.7 %collective-permute-start.8 = (bf16[192,1536]{1,0:T(8,128)(2,1)}, bf16[192,1536]{1,0:T(8,128)(2,1)S(1)}, u32[]{:S(2)}, u32[]{:S(2)}) collective-permute-start(bf16[192,1536]{1,0:T(8,128)(2,1)} %copy-done.1), channel_id=1, source_target_pairs={{0,1},{1,0},{2,3},{3,2},{4,5},{5,4},{6,7},{7,6},{8,9},{9,8},{10,11... | collective-permute-start | bytes 1769480 | tf_op jit(solution)/shard_map/ppermute | solution.py:20
  69.8 16.3 %collective-permute-start.9 = (bf16[192,1536]{1,0:T(8,128)(2,1)}, bf16[192,1536]{1,0:T(8,128)(2,1)S(1)}, u32[]{:S(2)}, u32[]{:S(2)}) collective-permute-start(bf16[192,1536]{1,0:T(8,128)(2,1)} %copy-done.2), channel_id=1, source_target_pairs={{0,1},{1,0},{2,3},{3,2},{4,5},{5,4},{6,7},{7,6},{8,9},{9,8},{10,11... | collective-permute-start | bytes 1769480 | tf_op jit(solution)/shard_map/ppermute | solution.py:20
  81.4 39.2 %collective-permute-start.17 = (bf16[4,48,1536]{2,1,0:T(8,128)(2,1)}, bf16[4,48,1536]{2,1,0:T(8,128)(2,1)S(1)}, u32[]{:S(2)}, u32[]{:S(2)}) collective-permute-start(bf16[4,48,1536]{2,1,0:T(8,128)(2,1)} %get-tuple-element.38), channel_id=1, source_target_pairs={{0,8},{1,9},{2,10},{3,11},{4,12},{5,13},{6,14},{7,15},{8,0},{9,1},... | collective-permute-start | bytes 1769480 | tf_op jit(solution)/shard_map/ppermute | solution.py:20
  81.4 4.7 %copy-start.4 = (bf16[192,1536]{1,0:T(8,128)(2,1)}, bf16[192,1536]{1,0:T(8,128)(2,1)S(1)}, u32[]{:S(2)}) copy-start(bf16[192,1536]{1,0:T(8,128)(2,1)S(1)} %collective-permute-done.6.refs_4_) | copy-start | bytes 1769476
  81.4 39.2 %collective-permute-start.18 = (bf16[4,48,1536]{2,1,0:T(8,128)(2,1)}, bf16[4,48,1536]{2,1,0:T(8,128)(2,1)S(1)}, u32[]{:S(2)}, u32[]{:S(2)}) collective-permute-start(bf16[4,48,1536]{2,1,0:T(8,128)(2,1)} %get-tuple-element.39), channel_id=1, source_target_pairs={{0,16},{1,17},{2,18},{3,19},{4,20},{5,21},{6,22},{7,23},{8,24},{9,... | collective-permute-start | bytes 1769480 | tf_op jit(solution)/shard_map/ppermute | solution.py:20
  83.3 2.8 %copy-start.5 = (bf16[192,1536]{1,0:T(8,128)(2,1)}, bf16[192,1536]{1,0:T(8,128)(2,1)S(1)}, u32[]{:S(2)}) copy-start(bf16[192,1536]{1,0:T(8,128)(2,1)S(1)} %collective-permute-done.7.refs_5_) | copy-start | bytes 1769476
  83.3 37.3 %collective-permute-start.19 = (bf16[4,48,1536]{2,1,0:T(8,128)(2,1)}, bf16[4,48,1536]{2,1,0:T(8,128)(2,1)}, u32[]{:S(2)}, u32[]{:S(2)}) collective-permute-start(bf16[4,48,1536]{2,1,0:T(8,128)(2,1)} %get-tuple-element.40), channel_id=1, source_target_pairs={{0,24},{1,25},{2,26},{3,27},{4,28},{5,29},{6,30},{7,31},{8,16},{9,... | collective-permute-start | bytes 1769480 | tf_op jit(solution)/shard_map/ppermute | solution.py:20
  125.9 1.5 collective-permute-start.23
  128.2 9.9 %collective-permute-start.24 = (f32[8,1536]{1,0:T(8,128)S(1)}, f32[8,1536]{1,0:T(8,128)S(1)}, u32[]{:S(2)}, u32[]{:S(2)}) collective-permute-start(f32[8,1536]{1,0:T(8,128)S(1)} %add.76), channel_id=1, source_target_pairs={{0,8},{1,9},{2,10},{3,11},{4,12},{5,13},{6,14},{7,15},{8,0},{9,1},... | collective-permute-start | bytes 147464 | tf_op jit(solution)/shard_map/ppermute | solution.py:20
  128.2 11.2 %collective-permute-start.25 = (f32[8,1536]{1,0:T(8,128)S(1)}, f32[8,1536]{1,0:T(8,128)S(1)}, u32[]{:S(2)}, u32[]{:S(2)}) collective-permute-start(f32[8,1536]{1,0:T(8,128)S(1)} %add.76), channel_id=1, source_target_pairs={{0,16},{1,17},{2,18},{3,19},{4,20},{5,21},{6,22},{7,23},{8,24},{9,... | collective-permute-start | bytes 147464 | tf_op jit(solution)/shard_map/ppermute | solution.py:20
  130.1 9.3 %collective-permute-start.26 = (f32[8,1536]{1,0:T(8,128)S(1)}, f32[8,1536]{1,0:T(8,128)S(1)}, u32[]{:S(2)}, u32[]{:S(2)}) collective-permute-start(f32[8,1536]{1,0:T(8,128)S(1)} %add.76), channel_id=1, source_target_pairs={{0,24},{1,25},{2,26},{3,27},{4,28},{5,29},{6,30},{7,31},{8,16},{9,... | collective-permute-start | bytes 147464 | tf_op jit(solution)/shard_map/ppermute | solution.py:20
  132.9 17.3 %collective-permute-start.20 = (bf16[48,1536]{1,0:T(8,128)(2,1)}, bf16[48,1536]{1,0:T(8,128)(2,1)S(1)}, u32[]{:S(2)}, u32[]{:S(2)}) collective-permute-start(bf16[48,1536]{1,0:T(8,128)(2,1)} %get-tuple-element.43), channel_id=1, source_target_pairs={{0,2},{1,3},{2,0},{3,1},{4,6},{5,7},{6,4},{7,5},{8,10},{9,11},{10,... | collective-permute-start | bytes 442376 | tf_op jit(solution)/shard_map/ppermute | solution.py:20
  134.2 16.0 %collective-permute-start.21 = (bf16[48,1536]{1,0:T(8,128)(2,1)}, bf16[48,1536]{1,0:T(8,128)(2,1)S(1)}, u32[]{:S(2)}, u32[]{:S(2)}) collective-permute-start(bf16[48,1536]{1,0:T(8,128)(2,1)} %get-tuple-element.44), channel_id=1, source_target_pairs={{0,4},{1,5},{2,6},{3,7},{4,0},{5,1},{6,2},{7,3},{8,12},{9,13},{10,... | collective-permute-start | bytes 442376 | tf_op jit(solution)/shard_map/ppermute | solution.py:20
  138.1 14.4 %collective-permute-start.22 = (bf16[48,1536]{1,0:T(8,128)(2,1)}, bf16[48,1536]{1,0:T(8,128)(2,1)S(1)}, u32[]{:S(2)}, u32[]{:S(2)}) collective-permute-start(bf16[48,1536]{1,0:T(8,128)(2,1)} %get-tuple-element.45), channel_id=1, source_target_pairs={{0,6},{1,7},{2,4},{3,5},{4,2},{5,3},{6,0},{7,1},{8,14},{9,15},{10,... | collective-permute-start | bytes 442376 | tf_op jit(solution)/shard_map/ppermute | solution.py:20
  139.4 13.1 %copy-start.14 = (f32[8,1536]{1,0:T(8,128)}, f32[8,1536]{1,0:T(8,128)S(1)}, u32[]{:S(2)}) copy-start(f32[8,1536]{1,0:T(8,128)S(1)} %add_add_fusion.1.a) | copy-start | bytes 147460
  139.4 10.8 %collective-permute-start.27 = (f32[8,1536]{1,0:T(8,128)S(1)}, f32[8,1536]{1,0:T(8,128)S(1)}, u32[]{:S(2)}, u32[]{:S(2)}) collective-permute-start(f32[8,1536]{1,0:T(8,128)S(1)} %add_add_fusion.1.a), channel_id=1, source_target_pairs={{0,2},{1,3},{2,0},{3,1},{4,6},{5,7},{6,4},{7,5},{8,10},{9,11},{10,... | collective-permute-start | bytes 147464 | tf_op jit(solution)/shard_map/ppermute | solution.py:20
  150.2 2.3 %copy-start.21 = (f32[8,1536]{1,0:T(8,128)}, f32[8,1536]{1,0:T(8,128)S(1)}, u32[]{:S(2)}) copy-start(f32[8,1536]{1,0:T(8,128)S(1)} %collective-permute-done.27.b) | copy-start | bytes 147460
  150.2 2.3 %copy-start.10 = (bf16[48,1536]{1,0:T(8,128)(2,1)}, bf16[48,1536]{1,0:T(8,128)(2,1)S(1)}, u32[]{:S(2)}) copy-start(bf16[48,1536]{1,0:T(8,128)(2,1)S(1)} %collective-permute-done.20.h1.v1) | copy-start | bytes 442372
  150.2 2.3 %copy-start.11 = (bf16[48,1536]{1,0:T(8,128)(2,1)}, bf16[48,1536]{1,0:T(8,128)(2,1)S(1)}, u32[]{:S(2)}) copy-start(bf16[48,1536]{1,0:T(8,128)(2,1)S(1)} %collective-permute-done.21.h2.v2) | copy-start | bytes 442372
  154.6 6.5 %collective-permute-start.28 = (f32[8,1536]{1,0:T(8,128)}, f32[8,1536]{1,0:T(8,128)S(1)}, u32[]{:S(2)}, u32[]{:S(2)}) collective-permute-start(f32[8,1536]{1,0:T(8,128)} %hold_add.1), channel_id=1, source_target_pairs={{0,6},{1,7},{2,4},{3,5},{4,2},{5,3},{6,0},{7,1},{8,14},{9,15},{10,... | collective-permute-start | bytes 147464 | tf_op jit(solution)/shard_map/ppermute | solution.py:20
  165.2 4.7 %collective-permute-start.29 = (f32[56,384]{1,0:T(8,128)}, f32[56,384]{1,0:T(8,128)S(1)}, u32[]{:S(2)}, u32[]{:S(2)}) collective-permute-start(f32[56,384]{1,0:T(8,128)} %get-tuple-element.48), channel_id=1, source_target_pairs={{0,32},{32,0},{64,96},{96,64},{128,160},{160,128},{192,224},{224,1... | collective-permute-start | bytes 258056 | tf_op jit(solution)/shard_map/ppermute | solution.py:25
  166.7 7.0 %collective-permute-start.30 = (f32[56,384]{1,0:T(8,128)}, f32[56,384]{1,0:T(8,128)S(1)}, u32[]{:S(2)}, u32[]{:S(2)}) collective-permute-start(f32[56,384]{1,0:T(8,128)} %get-tuple-element.49), channel_id=1, source_target_pairs={{0,64},{32,96},{64,0},{96,32},{128,192},{160,224},{192,128},{224,1... | collective-permute-start | bytes 258056 | tf_op jit(solution)/shard_map/ppermute | solution.py:25
  169.4 5.9 %collective-permute-start.31 = (f32[56,384]{1,0:T(8,128)}, f32[56,384]{1,0:T(8,128)S(1)}, u32[]{:S(2)}, u32[]{:S(2)}) collective-permute-start(f32[56,384]{1,0:T(8,128)} %get-tuple-element.50), channel_id=1, source_target_pairs={{0,96},{32,64},{64,32},{96,0},{128,224},{160,192},{192,160},{224,1... | collective-permute-start | bytes 258056 | tf_op jit(solution)/shard_map/ppermute | solution.py:25
  176.2 4.6 %collective-permute-start.32 = (f32[56,384]{1,0:T(8,128)S(1)}, f32[56,384]{1,0:T(8,128)S(1)}, u32[]{:S(2)}, u32[]{:S(2)}) collective-permute-start(f32[56,384]{1,0:T(8,128)S(1)} %add_add_fusion), channel_id=1, source_target_pairs={{0,128},{32,160},{64,192},{96,224},{128,0},{160,32},{192,64},{224,... | collective-permute-start | bytes 258056 | tf_op jit(solution)/shard_map/ppermute | solution.py:25
  180.8 8.2 %copy-start.13 = (f32[56,384]{1,0:T(8,128)}, f32[56,384]{1,0:T(8,128)S(1)}, u32[]{:S(2)}) copy-start(f32[56,384]{1,0:T(8,128)S(1)} %add.84.v0) | copy-start | bytes 258052
  180.8 5.9 %collective-permute-start.33 = (f32[56,384]{1,0:T(8,128)S(1)}, f32[56,384]{1,0:T(8,128)S(1)}, u32[]{:S(2)}, u32[]{:S(2)}) collective-permute-start(f32[56,384]{1,0:T(8,128)S(1)} %add.84.v0), channel_id=1, source_target_pairs={{0,32},{32,0},{64,96},{96,64},{128,160},{160,128},{192,224},{224,1... | collective-permute-start | bytes 258056 | tf_op jit(solution)/shard_map/ppermute | solution.py:25
  180.9 6.1 %collective-permute-start.34 = (f32[56,384]{1,0:T(8,128)S(1)}, f32[56,384]{1,0:T(8,128)S(1)}, u32[]{:S(2)}, u32[]{:S(2)}) collective-permute-start(f32[56,384]{1,0:T(8,128)S(1)} %add.84.v0), channel_id=1, source_target_pairs={{0,64},{32,96},{64,0},{96,32},{128,192},{160,224},{192,128},{224,1... | collective-permute-start | bytes 258056 | tf_op jit(solution)/shard_map/ppermute | solution.py:25
  183.3 5.7 %collective-permute-start.35 = (f32[56,384]{1,0:T(8,128)S(1)}, f32[56,384]{1,0:T(8,128)S(1)}, u32[]{:S(2)}, u32[]{:S(2)}) collective-permute-start(f32[56,384]{1,0:T(8,128)S(1)} %add.84.v0), channel_id=1, source_target_pairs={{0,96},{32,64},{64,32},{96,0},{128,224},{160,192},{192,160},{224,1... | collective-permute-start | bytes 258056 | tf_op jit(solution)/shard_map/ppermute | solution.py:25
  (11 other events, 12.8 us)

commit v4 on v2

--- a/solution.py
+++ b/solution.py
@@ -206,7 +206,7 @@
     )(pos, *a, held)
 
 
-def stage3_kernel(pos, v0, v1, v2, v3, held, o0, o1, o2, o3, total):
+def stage3_kernel(pos, v0, v1, v2, v3, h1, h2, o0, o1, o2, o3, total):
     total[...] = (v0[...] + v1[...].astype(F32)) + (v2[...].astype(F32) + v3[...].astype(F32))
     for n, out in enumerate((o0, o1, o2, o3)):
         at = pl.multiple_of((pos[1] ^ n) * 384, 128)
@@ -222,32 +222,52 @@
         grid_spec=pltpu.PrefetchScalarGridSpec(
             num_scalar_prefetch=1,
             grid=(1,),
-            in_specs=[whole(shape)] * 4 + [HBM],
+            in_specs=[whole(shape)] * 4 + [HBM] * 2,
             out_specs=(whole(part),) * 4,
             scratch_shapes=[pltpu.VMEM(shape, F32)],
         ),
         compiler_params=compiler(),
         name="stage3",
         **params(2),
-    )(pos, *v, held)
-
-
-def join_kernel(pos, v0, v1, v2, v3, out):
+    )(pos, *v, *held)
+
+
+def pack_kernel(v0, v1, v2, v3, small, out):
+    out[0:48, :] = (v0[...] + v1[...]) + (v2[...] + v3[...])
+    out[48:56, :] = small[...]
+
+
+def pack(v, small):
+    rows, width = v[0].shape
+    return pl.pallas_call(
+        pack_kernel,
+        out_shape=sds((rows + 8, width), F32),
+        grid=(1,),
+        in_specs=[whole((rows, width))] * 4 + [whole((8, width))],
+        out_specs=whole((rows + 8, width)),
+        compiler_params=compiler(),
+        name="pack",
+        **params(1),
+    )(*v, small)
+
+
+def join_kernel(pos, v0, v1, v2, v3, out, small):
     for n, v in enumerate((v0, v1, v2, v3)):
         at = pl.multiple_of((pos[1] ^ n) * 384, 128)
-        out[:, pl.ds(at, 384)] = v[...]
+        out[:, pl.ds(at, 384)] = v[0:48, :]
+    small[...] = (v0[48:56, :] + v1[48:56, :]) + (v2[48:56, :] + v3[48:56, :])
 
 
 def join(pos, parts):
-    rows = parts[0].shape[0]
+    rows = parts[0].shape[0] - 8
     return pl.pallas_call(
         join_kernel,
-        out_shape=sds((rows, 1536), F32),
+        out_shape=(sds((rows, 1536), F32), sds((8, 384), F32)),
         grid_spec=pltpu.PrefetchScalarGridSpec(
             num_scalar_prefetch=1,
             grid=(1,),
-            in_specs=[whole((rows, 384))] * 4,
-            out_specs=whole((rows, 1536)),
+            in_specs=[whole((rows + 8, 384))] * 4,
+            out_specs=(whole((rows, 1536)), whole((8, 384))),
         ),
         compiler_params=compiler(),
         name="join",
@@ -279,12 +299,13 @@
     y, z, core = pos[0], pos[2], pos[3]
     copies = []
     for n, piece in enumerate(pieces):
-        for j in range(16):
-            index = ((y ^ (j // 4)) * 4 + (z ^ (j % 4))) * 2 + (core ^ n)
+        dc, dy = n // 4, n % 4
+        for dz in range(4):
+            index = ((y ^ dy) * 4 + (z ^ dz)) * 2 + (core ^ dc)
             at = pl.multiple_of(index * 48, 48)
             copies.append(
                 pltpu.make_async_copy(
-                    piece.at[pl.ds(j * 48, 48), :], buf.at[pl.ds(at, 48), :], sem.at[n * 16 + j]
+                    piece.at[pl.ds(dz * 48, 48), :], buf.at[pl.ds(at, 48), :], sem.at[n * 4 + dz]
                 )
             )
     for c in copies:
@@ -294,7 +315,7 @@
 
 
 def project_kernel(pos, *refs):
-    pieces, (sw, res, _, _, out, buf, sem) = refs[:2], refs[2:]
+    pieces, (sw, res, _, _, out, buf, sem) = refs[:8], refs[8:]
 
     @pl.when(pl.program_id(0) == 0)
     def _():
@@ -313,7 +334,7 @@
         grid_spec=pltpu.PrefetchScalarGridSpec(
             num_scalar_prefetch=1,
             grid=(frames // rows,),
-            in_specs=[HBM] * 2 + [block, block, HBM, HBM],
+            in_specs=[HBM] * 8 + [block, block, HBM, HBM],
             out_specs=block,
             scratch_shapes=[pltpu.VMEM((width, width), BF16), pltpu.SemaphoreType.DMA((32,))],
         ),
@@ -324,8 +345,8 @@
 
 
 def backward_kernel(pos, *refs, rows, chunk, unroll):
-    pieces = refs[:2]
-    par, cot, nrm, rst, _, gconv, sums, buf, sem, grad = refs[2:]
+    pieces = refs[:8]
+    par, cot, nrm, rst, _, gconv, sums, buf, sem, grad = refs[8:]
     step = pl.program_id(0)
     width = cot.shape[1]
     length = pos[4]
@@ -370,7 +391,7 @@
         grid_spec=pltpu.PrefetchScalarGridSpec(
             num_scalar_prefetch=1,
             grid=(frames // rows,),
-            in_specs=[HBM] * 2
+            in_specs=[HBM] * 8
             + [whole((8, width)), block(width), block(width), block(128), HBM],
             out_specs=(block(width), whole((2, 8, width))),
             scratch_shapes=[
@@ -381,7 +402,7 @@
         ),
         compiler_params=compiler(),
         name="backward",
-        **params(21),
+        **params(0.1),
     )(pos, *pieces, par, cot, nrm, rst, held)
 
 
@@ -457,7 +478,7 @@
         ),
         compiler_params=compiler(),
         name="taps",
-        **params(10),
+        **params(0.1),
     )(pos, par, glu, gconv, norm_sums)
 
 
@@ -480,30 +501,26 @@
 
     block = gather([proj_weight] + [fsdp_move(proj_weight, z=k) for k in (1, 2, 3)], own)
     near = [block] + [fsdp_move(block, y=k) for k in (1, 2, 3)]
+    pieces = near + [fsdp_move(p, core=1) for p in near]
 
     swished, normed, rstd = forward(lengths, par, glu)
     keep, send = outer(core[None].astype(jnp.int32), swished, cot, near[1:])
     recv = fsdp_move(send, core=1)
     a = stage1(pos, keep, recv)
-    mine = gather(near, a[0])
-    pieces = [mine, fsdp_move(mine, core=1)]
     gconv, sums = backward(pos, pieces, par, cot, normed, rstd, a[0])
     glu_grad, small = taps(pos, par, glu, gconv, sums)
     v = stage2(pos, [a[0]] + [fsdp_move(a[k], y=k) for k in (1, 2, 3)], glu_grad)
     small = small + fsdp_move(small, core=1)
     small = (small + fsdp_move(small, y=1)) + (fsdp_move(small, y=2) + fsdp_move(small, y=3))
     block_out = project(pos, pieces, swished, res, (v[0], small))
-    v = stage3(pos, [v[0]] + [fsdp_move(v[k], z=k) for k in (1, 2, 3)], block_out)
-    total = (v[0] + dp_move(v[1], x=1)) + (dp_move(v[2], x=2) + dp_move(v[3], x=3))
+    small = small + fsdp_move(small, z=1)
+    v = stage3(pos, [v[0]] + [fsdp_move(v[k], z=k) for k in (1, 2, 3)], (block_out, small))
+    small = small + fsdp_move(small, z=3)
+    small = jnp.pad(lax.dynamic_slice(small, (0, f * 48), (8, 48)), ((0, 0), (0, 336)))
+    total = pack([v[0]] + [dp_move(v[k], x=k) for k in (1, 2, 3)], small)
     total = total + dp_move(total, low=1)
-    proj_grad = join(pos, [total] + [dp_move(total, x=k) for k in (1, 2, 3)])
-
-    small = small + fsdp_move(small, z=1)
-    small = small + fsdp_move(small, z=3)
-    small = lax.dynamic_slice(small, (0, f * 48), (8, 48))
-    small = (small + dp_move(small, x=1)) + (dp_move(small, x=2) + dp_move(small, x=3))
-    small = small + dp_move(small, low=1)
-    return (block_out[None], glu_grad[None], proj_grad, small[:TAPS], small[TAPS : TAPS + 2])
+    proj_grad, small = join(pos, [total] + [dp_move(total, x=k) for k in (1, 2, 3)])
+    return (block_out[None], glu_grad[None], proj_grad, small[:TAPS, :48], small[TAPS : TAPS + 2, :48])
 
 
 def solution(mesh):

time: 179 us -> 192 us (1.073)
  waiting for transfers between devices: 32.7 us -> 45.8 us
    ppermute x11 -> x7, waiting for transfers between devices: 3.74 us -> 11.5 us  [dp_move(): return lax.ppermute(value, 'dp', perm)]
    ppermute x11 -> x7, starting transfers between devices: 15.7 us -> 9.48 us  [dp_move(): return lax.ppermute(value, 'dp', perm)]
    ppermute x26 -> x29, starting transfers between devices: 41.3 us -> 47.5 us  [fsdp_move(): return lax.ppermute(value, 'fsdp', perm)]
    ppermute x26 -> x29, waiting for transfers between devices: 29 us -> 34.3 us  [fsdp_move(): return lax.ppermute(value, 'fsdp', perm)]
    pallas_call x2 -> x1, Pallas kernels: 5.11 us -> 1.98 us  [gather(): pl.pallas_call(gather_kernel, out_shape=sds((4 * rows, width), BF16), gri...]
    slice x1 -> x2, local copies, waits for them, and re-layouts: 0.57 us -> 2.51 us  [the longest x1 1.27 us: local(): small[:TAPS, :48]]
    pallas_call x1 -> x2, Pallas kernels: 2.39 us -> 4.06 us  [the longest x1 2.41 us: join(): pl.pallas_call(join_kernel, out_shape=(sds((rows, 1536), F32), sds((8, 38...]
    unnamed x42 -> x52, local copies, waits for them, and re-layouts: 7.22 us -> 5.95 us
  transfers between devices with their start and end apart: 37 -> 36, of which waited for: 15 -> 14; matrix products, arithmetic and copies ran while one was open for 3% -> 3% of each run, Pallas kernels for 29% -> 31%
where the time goes in v4:
time: 192 us; the launch traced here: 191 us
  Pallas kernels  72.3 us (38%)
  starting transfers between devices  57 us (30%)
  waiting for transfers between devices  45.8 us (24%)
  local copies, waits for them, and re-layouts  9.9 us (5%)
  other arithmetic  4.65 us (2%)
    ppermute x29, starting transfers between devices, fsdp_move(): return lax.ppermute(value, 'fsdp', perm)  47.5 us
    ppermute x29, waiting for transfers between devices, fsdp_move(): return lax.ppermute(value, 'fsdp', perm)  34.3 us
    pallas_call x1, Pallas kernels, backward(): pl.pallas_call(functools.partial(backward_kernel, rows=rows, chunk=chunk,...  15.7 us
    ppermute x7, waiting for transfers between devices, dp_move(): return lax.ppermute(value, 'dp', perm)  11.5 us
    pallas_call x1, Pallas kernels, project(): pl.pallas_call(project_kernel, out_shape=sds((frames, width), BF16), grid...  10 us
    pallas_call x1, Pallas kernels, taps(): pl.pallas_call(functools.partial(taps_kernel, rows=rows, frames=frames, c...  9.98 us
    pallas_call x1, Pallas kernels, forward(): pl.pallas_call(functools.partial(forward_kernel, rows=rows, frames=frames...  9.58 us
    ppermute x7, starting transfers between devices, dp_move(): return lax.ppermute(value, 'dp', perm)  9.48 us
  transfers between devices with their start and end apart: 36, of which 14 were waited for; matrix products, arithmetic and copies ran while one was open for 3% of the time, Pallas kernels for 31%

profile of v4, /device:TPU:32, one launch (start us, length us, event | category | flops | bytes accessed | tf_op | source)
XLA Modules:
  0.0 191.2 jit_solution(5039638476661381289)
XLA Ops:
  0.6 3.4 %collective-permute-start = (bf16[48,1536]{1,0:T(8,128)(2,1)}, bf16[48,1536]{1,0:T(8,128)(2,1)S(1)}, u32[]{:S(2)}, u32[]{:S(2)}) collective-permute-start(bf16[48,1536]{1,0:T(8,128)(2,1)} %w0.1), channel_id=1, source_target_pairs={{0,2},{1,3},{2,0},{3,1},{4,6},{5,7},{6,4},{7,5},{8,10},{9,11},{10,... | collective-permute-start | bytes 442376 | tf_op jit(solution)/shard_map/ppermute | solution.py:20
  5.0 4.6 %collective-permute-start.1 = (bf16[48,1536]{1,0:T(8,128)(2,1)}, bf16[48,1536]{1,0:T(8,128)(2,1)S(1)}, u32[]{:S(2)}, u32[]{:S(2)}) collective-permute-start(bf16[48,1536]{1,0:T(8,128)(2,1)} %w0.1), channel_id=1, source_target_pairs={{0,4},{1,5},{2,6},{3,7},{4,0},{5,1},{6,2},{7,3},{8,12},{9,13},{10,... | collective-permute-start | bytes 442376 | tf_op jit(solution)/shard_map/ppermute | solution.py:20
  10.6 1.7 collective-permute-start.11
  12.2 2.9 %collective-permute-start.12 = (bf16[8,1536]{1,0:T(8,128)(2,1)S(1)}, bf16[8,1536]{1,0:T(8,128)(2,1)S(1)}, u32[]{:S(2)}, u32[]{:S(2)}) collective-permute-start(bf16[8,1536]{1,0:T(8,128)(2,1)S(1)} %add.64), channel_id=1, source_target_pairs={{0,16},{1,17},{2,18},{3,19},{4,20},{5,21},{6,22},{7,23},{8,24},{9,... | collective-permute-start | bytes 73736 | tf_op jit(solution)/shard_map/ppermute | solution.py:20
  15.1 3.2 %collective-permute-start.13 = (bf16[8,1536]{1,0:T(8,128)(2,1)S(1)}, bf16[8,1536]{1,0:T(8,128)(2,1)S(1)}, u32[]{:S(2)}, u32[]{:S(2)}) collective-permute-start(bf16[8,1536]{1,0:T(8,128)(2,1)S(1)} %add.64), channel_id=1, source_target_pairs={{0,24},{1,25},{2,26},{3,27},{4,28},{5,29},{6,30},{7,31},{8,16},{9,... | collective-permute-start | bytes 73736 | tf_op jit(solution)/shard_map/ppermute | solution.py:20
  18.4 3.0 %collective-permute-done.1.w2 = bf16[48,1536]{1,0:T(8,128)(2,1)S(1)} collective-permute-done((bf16[48,1536]{1,0:T(8,128)(2,1)}, bf16[48,1536]{1,0:T(8,128)(2,1)S(1)}, u32[]{:S(2)}, u32[]{:S(2)}) %collective-permute-start.1) | collective-permute-done | bytes 147488 | tf_op jit(solution)/shard_map/ppermute | solution.py:20
  21.4 2.1 %collective-permute-done.2.w3 = bf16[48,1536]{1,0:T(8,128)(2,1)S(1)} collective-permute-done((bf16[48,1536]{1,0:T(8,128)(2,1)}, bf16[48,1536]{1,0:T(8,128)(2,1)S(1)}, u32[]{:S(2)}, u32[]{:S(2)}) %collective-permute-start.2) | collective-permute-done | bytes 147488 | tf_op jit(solution)/shard_map/ppermute | solution.py:20
  24.2 2.0 %gather.1.refs_0_ = bf16[192,1536]{1,0:T(8,128)(2,1)} custom-call(bf16[48,1536]{1,0:T(8,128)(2,1)} %w0.1, bf16[48,1536]{1,0:T(8,128)(2,1)} %copy-done.13, bf16[48,1536]{1,0:T(8,128)(2,1)} %copy-done.14, bf16[48,1536]{1,0:T(8,128)(2,1)} %copy-done.15, bf16[8,48]{1,0:T(8,128)(2,1)} %copy-done.25), custom_call_target="tpu_custom_call" | custom-call | bytes 360000 | tf_op jit(solution)/shard_map/gather/pallas_call | solution.py:286
  26.2 1.4 collective-permute-start.3
  27.5 2.9 %collective-permute-start.4 = (bf16[192,1536]{1,0:T(8,128)(2,1)}, bf16[192,1536]{1,0:T(8,128)(2,1)S(1)}, u32[]{:S(2)}, u32[]{:S(2)}) collective-permute-start(bf16[192,1536]{1,0:T(8,128)(2,1)} %gather.1.refs_0_), channel_id=1, source_target_pairs={{0,16},{1,17},{2,18},{3,19},{4,20},{5,21},{6,22},{7,23},{8,24},{9,... | collective-permute-start | bytes 1769480 | tf_op jit(solution)/shard_map/ppermute | solution.py:20
  30.9 1.4 collective-permute-start.14
  32.3 3.4 %collective-permute-done.14 = bf16[8,1536]{1,0:T(8,128)(2,1)S(1)} collective-permute-done((bf16[8,1536]{1,0:T(8,128)(2,1)S(1)}, bf16[8,1536]{1,0:T(8,128)(2,1)S(1)}, u32[]{:S(2)}, u32[]{:S(2)}) %collective-permute-start.14) | collective-permute-done | bytes 24608 | tf_op jit(solution)/shard_map/ppermute | solution.py:20
  35.7 3.0 %collective-permute-start.15 = (bf16[8,1536]{1,0:T(8,128)(2,1)S(1)}, bf16[8,1536]{1,0:T(8,128)(2,1)S(1)}, u32[]{:S(2)}, u32[]{:S(2)}) collective-permute-start(bf16[8,1536]{1,0:T(8,128)(2,1)S(1)} %add.68), channel_id=1, source_target_pairs={{0,6},{1,7},{2,4},{3,5},{4,2},{5,3},{6,0},{7,1},{8,14},{9,15},{10,... | collective-permute-start | bytes 73736 | tf_op jit(solution)/shard_map/ppermute | solution.py:20
  39.3 2.4 %collective-permute-done.15 = bf16[8,1536]{1,0:T(8,128)(2,1)S(1)} collective-permute-done((bf16[8,1536]{1,0:T(8,128)(2,1)S(1)}, bf16[8,1536]{1,0:T(8,128)(2,1)S(1)}, u32[]{:S(2)}, u32[]{:S(2)}) %collective-permute-start.15) | collective-permute-done | bytes 24608 | tf_op jit(solution)/shard_map/ppermute | solution.py:20
  42.4 9.6 %forward.1 = (bf16[768,1536]{1,0:T(8,128)(2,1)}, f32[768,1536]{1,0:T(8,128)}, f32[768,128]{1,0:T(8,128)}) custom-call(s32[1]{0:T(128)S(6)} %copy.15.lens, f32[8,1536]{1,0:T(8,128)} %add_convert_fusion.par.refs_8_, bf16[768,1536]{1,0:T(8,128)(2,1)} %bitcast.13), custom_call_target="tpu_custom_call" | custom-call | bytes 360000 | tf_op jit(solution)/shard_map/forward/pallas_call | solution.py:98
  52.0 4.7 %collective-permute-done.4.h2.refs_2_ = bf16[192,1536]{1,0:T(8,128)(2,1)S(1)} collective-permute-done((bf16[192,1536]{1,0:T(8,128)(2,1)}, bf16[192,1536]{1,0:T(8,128)(2,1)S(1)}, u32[]{:S(2)}, u32[]{:S(2)}) %collective-permute-start.4) | collective-permute-done | bytes 589856 | tf_op jit(solution)/shard_map/ppermute | solution.py:20
  56.6 2.6 %collective-permute-done.5.h3.refs_3_ = bf16[192,1536]{1,0:T(8,128)(2,1)S(1)} collective-permute-done((bf16[192,1536]{1,0:T(8,128)(2,1)}, bf16[192,1536]{1,0:T(8,128)(2,1)S(1)}, u32[]{:S(2)}, u32[]{:S(2)}) %collective-permute-start.5) | collective-permute-done | bytes 589856 | tf_op jit(solution)/shard_map/ppermute | solution.py:20
  60.0 8.1 %outer.1 = (f32[16,48,1536]{2,1,0:T(8,128)}, bf16[16,48,1536]{2,1,0:T(8,128)(2,1)}) custom-call(s32[1]{0:T(128)} %bitcast.3.core, bf16[768,1536]{1,0:T(8,128)(2,1)} %get-tuple-element.28.sw.refs_8_, bf16[768,1536]{1,0:T(8,128)(2,1)} %bitcast.15, bf16[192,1536]{1,0:T(8,128)(2,1)} %copy-done, bf16[192,1536]{1,0:T(8,128)(2,1)} %copy-done.1, ...), custom_call_target="tpu_custom_call" | custom-call | bytes 360000 | tf_op jit(solution)/shard_map/outer/pallas_call | solution.py:128
  69.8 5.6 %collective-permute-done.16 = bf16[16,48,1536]{2,1,0:T(8,128)(2,1)} collective-permute-done((bf16[16,48,1536]{2,1,0:T(8,128)(2,1)}, bf16[16,48,1536]{2,1,0:T(8,128)(2,1)}, u32[]{:S(2)}, u32[]{:S(2)}) %collective-permute-start.16) | collective-permute-done | bytes 2359328 | tf_op jit(solution)/shard_map/ppermute | solution.py:20
  75.4 6.0 %stage1.1 = (f32[4,48,1536]{2,1,0:T(8,128)}, bf16[4,48,1536]{2,1,0:T(8,128)(2,1)}, bf16[4,48,1536]{2,1,0:T(8,128)(2,1)}, bf16[4,48,1536]{2,1,0:T(8,128)(2,1)}) custom-call(s32[5]{0:T(128)} %stack.19.pos, f32[4,4,48,1536]{3,2,1,0:T(8,128)} %bitcast.18, bf16[4,4,48,1536]{3,2,1,0:T(8,128)(2,1)} %bitcast.10.recv), custom_call_target="tpu_custom_call" | custom-call | bytes 360000 | tf_op jit(solution)/shard_map/stage1/pallas_call | solution.py:166
  81.4 1.9 collective-permute-start.18
  83.3 2.8 %collective-permute-start.19 = (bf16[4,48,1536]{2,1,0:T(8,128)(2,1)}, bf16[4,48,1536]{2,1,0:T(8,128)(2,1)}, u32[]{:S(2)}, u32[]{:S(2)}) collective-permute-start(bf16[4,48,1536]{2,1,0:T(8,128)(2,1)} %get-tuple-element.34), channel_id=1, source_target_pairs={{0,24},{1,25},{2,26},{3,27},{4,28},{5,29},{6,30},{7,31},{8,16},{9,... | collective-permute-start | bytes 1769480 | tf_op jit(solution)/shard_map/ppermute | solution.py:20
  87.1 15.7 %backward.1 = (f32[768,1536]{1,0:T(8,128)}, f32[2,8,1536]{2,1,0:T(8,128)}) custom-call(s32[5]{0:T(128)} %stack.19.pos, bf16[192,1536]{1,0:T(8,128)(2,1)} %gather.1.refs_0_, bf16[192,1536]{1,0:T(8,128)(2,1)} %copy-done, bf16[192,1536]{1,0:T(8,128)(2,1)} %copy-done.1, bf16[192,1536]{1,0:T(8,128)(2,1)} %copy-done.2, bf16[192,1536]{1,0:T(8,128)(2,1)} %copy-done.4, ...), custom_call_target="tpu_custom_call" | custom-call | bytes 360000 | tf_op jit(solution)/shard_map/backward/pallas_call | solution.py:388
  102.9 10.0 %taps.1 = (bf16[768,1536]{1,0:T(8,128)(2,1)}, f32[8,1536]{1,0:T(8,128)}) custom-call(s32[5]{0:T(128)} %stack.19.pos, f32[8,1536]{1,0:T(8,128)} %add_convert_fusion.par.refs_8_, bf16[768,1536]{1,0:T(8,128)(2,1)} %bitcast.14, f32[768,1536]{1,0:T(8,128)} %get-tuple-element.37.gconv, f32[2,8,1536]{2,1,0:T(8,128)} %get-tuple-element.38.norm_sums), custom_call_target="tpu_custom_call" | custom-call | bytes 360000 | tf_op jit(solution)/shard_map/taps/pallas_call | solution.py:464
  112.9 1.4 collective-permute-done.20
  115.1 1.9 collective-permute-start.22
  117.0 2.8 %collective-permute-start.23 = (f32[8,1536]{1,0:T(8,128)S(1)}, f32[8,1536]{1,0:T(8,128)S(1)}, u32[]{:S(2)}, u32[]{:S(2)}) collective-permute-start(f32[8,1536]{1,0:T(8,128)S(1)} %add.70), channel_id=1, source_target_pairs={{0,24},{1,25},{2,26},{3,27},{4,28},{5,29},{6,30},{7,31},{8,16},{9,... | collective-permute-start | bytes 147464 | tf_op jit(solution)/shard_map/ppermute | solution.py:20
  120.7 4.2 %stage2.1 = (f32[48,1536]{1,0:T(8,128)}, bf16[48,1536]{1,0:T(8,128)(2,1)}, bf16[48,1536]{1,0:T(8,128)(2,1)}, bf16[48,1536]{1,0:T(8,128)(2,1)}) custom-call(s32[5]{0:T(128)} %stack.19.pos, f32[4,48,1536]{2,1,0:T(8,128)} %get-tuple-element.31.refs_12_.a0, bf16[4,48,1536]{2,1,0:T(8,128)(2,1)} %copy-done.8, bf16[4,48,1536]{2,1,0:T(8,128)(2,1)} %copy-done.9, ...), custom_call_target="tpu_custom_call" | custom-call | bytes 10800000 | tf_op jit(solution)/shard_map/stage2/pallas_call | solution.py:194
  124.9 1.4 collective-permute-start.24
  126.3 3.9 %collective-permute-start.25 = (bf16[48,1536]{1,0:T(8,128)(2,1)}, bf16[48,1536]{1,0:T(8,128)(2,1)S(1)}, u32[]{:S(2)}, u32[]{:S(2)}) collective-permute-start(bf16[48,1536]{1,0:T(8,128)(2,1)} %get-tuple-element.43), channel_id=1, source_target_pairs={{0,4},{1,5},{2,6},{3,7},{4,0},{5,1},{6,2},{7,3},{8,12},{9,13},{10,... | collective-permute-start | bytes 442376 | tf_op jit(solution)/shard_map/ppermute | solution.py:20
  131.4 1.8 collective-permute-start.27
  133.2 9.0 %collective-permute-done.27 = f32[8,1536]{1,0:T(8,128)S(1)} collective-permute-done((f32[8,1536]{1,0:T(8,128)S(1)}, f32[8,1536]{1,0:T(8,128)S(1)}, u32[]{:S(2)}, u32[]{:S(2)}) %collective-permute-start.27) | collective-permute-done | bytes 49184 | tf_op jit(solution)/shard_map/ppermute | solution.py:20
  142.2 3.8 %collective-permute-start.31 = (f32[8,1536]{1,0:T(8,128)S(1)}, f32[8,1536]{1,0:T(8,128)S(1)}, u32[]{:S(2)}, u32[]{:S(2)}) collective-permute-start(f32[8,1536]{1,0:T(8,128)S(1)} %add.74.h2), channel_id=1, source_target_pairs={{0,6},{1,7},{2,4},{3,5},{4,2},{5,3},{6,0},{7,1},{8,14},{9,15},{10,... | collective-permute-start | bytes 147464 | tf_op jit(solution)/shard_map/ppermute | solution.py:20
  146.0 10.0 %project.1.h1 = bf16[768,1536]{1,0:T(8,128)(2,1)} custom-call(s32[5]{0:T(128)} %stack.19.pos, bf16[192,1536]{1,0:T(8,128)(2,1)} %gather.1.refs_0_, bf16[192,1536]{1,0:T(8,128)(2,1)} %copy-done, bf16[192,1536]{1,0:T(8,128)(2,1)} %copy-done.1, bf16[192,1536]{1,0:T(8,128)(2,1)} %copy-done.2, bf16[192,1536]{1,0:T(8,128)(2,1)} %copy-done.4, ...), custom_call_target="tpu_custom_call" | custom-call | bytes 39600000 | tf_op jit(solution)/shard_map/project/pallas_call | solution.py:331
  157.4 2.6 %stage3.1 = (f32[48,384]{1,0:T(8,128)}, f32[48,384]{1,0:T(8,128)}, f32[48,384]{1,0:T(8,128)}, f32[48,384]{1,0:T(8,128)}) custom-call(s32[5]{0:T(128)} %stack.19.pos, f32[48,1536]{1,0:T(8,128)} %get-tuple-element.40.refs_10_.v0, bf16[48,1536]{1,0:T(8,128)(2,1)} %copy-done.16, bf16[48,1536]{1,0:T(8,128)(2,1)} %copy-done.17, bf16[48,1536]{1,0:T(8,128)(2,1)} %copy-done.18, ...), custom_call_target="tpu_custom_call" | custom-call | bytes 7200000 | tf_op jit(solution)/shard_map/stage3/pallas_call | solution.py:219
  160.1 1.5 collective-permute-start.28
  161.6 2.7 %collective-permute-start.29 = (f32[48,384]{1,0:T(8,128)}, f32[48,384]{1,0:T(8,128)S(1)}, u32[]{:S(2)}, u32[]{:S(2)}) collective-permute-start(f32[48,384]{1,0:T(8,128)} %get-tuple-element.47), channel_id=1, source_target_pairs={{0,64},{32,96},{64,0},{96,32},{128,192},{160,224},{192,128},{224,1... | collective-permute-start | bytes 221192 | tf_op jit(solution)/shard_map/ppermute | solution.py:25
  166.2 1.5 collective-permute-done.29.v2
  167.7 2.4 %collective-permute-done.30.v3 = f32[48,384]{1,0:T(8,128)S(1)} collective-permute-done((f32[48,384]{1,0:T(8,128)}, f32[48,384]{1,0:T(8,128)S(1)}, u32[]{:S(2)}, u32[]{:S(2)}) %collective-permute-start.30) | collective-permute-done | bytes 73760 | tf_op jit(solution)/shard_map/ppermute | solution.py:25
  170.7 1.6 pack.1
  172.3 4.7 %collective-permute-done.32 = f32[56,384]{1,0:T(8,128)S(1)} collective-permute-done((f32[56,384]{1,0:T(8,128)}, f32[56,384]{1,0:T(8,128)S(1)}, u32[]{:S(2)}, u32[]{:S(2)}) %collective-permute-start.32) | collective-permute-done | bytes 86048 | tf_op jit(solution)/shard_map/ppermute | solution.py:25
  178.1 1.9 %collective-permute-start.34 = (f32[56,384]{1,0:T(8,128)S(1)}, f32[56,384]{1,0:T(8,128)S(1)}, u32[]{:S(2)}, u32[]{:S(2)}) collective-permute-start(f32[56,384]{1,0:T(8,128)S(1)} %add.76.v0), channel_id=1, source_target_pairs={{0,64},{32,96},{64,0},{96,32},{128,192},{160,224},{192,128},{224,1... | collective-permute-start | bytes 258056 | tf_op jit(solution)/shard_map/ppermute | solution.py:25
  180.0 2.8 %collective-permute-start.35 = (f32[56,384]{1,0:T(8,128)S(1)}, f32[56,384]{1,0:T(8,128)S(1)}, u32[]{:S(2)}, u32[]{:S(2)}) collective-permute-start(f32[56,384]{1,0:T(8,128)S(1)} %add.76.v0), channel_id=1, source_target_pairs={{0,96},{32,64},{64,32},{96,0},{128,224},{160,192},{192,160},{224,1... | collective-permute-start | bytes 258056 | tf_op jit(solution)/shard_map/ppermute | solution.py:25
  182.7 1.4 collective-permute-done.34.v2
  184.1 1.5 collective-permute-done.35.v3
  186.3 2.4 %join.1 = (f32[48,1536]{1,0:T(8,128)}, f32[8,384]{1,0:T(8,128)}) custom-call(s32[5]{0:T(128)} %stack.19.pos, f32[56,384]{1,0:T(8,128)} %copy-done.11, f32[56,384]{1,0:T(8,128)} %copy-done.19, f32[56,384]{1,0:T(8,128)} %copy-done.20, f32[56,384]{1,0:T(8,128)} %copy-done.21), custom_call_target="tpu_custom_call" | custom-call | bytes 7200000 | tf_op jit(solution)/shard_map/join/pallas_call | solution.py:263
  188.7 1.3 slice.6
  190.0 1.2 slice.7
  (104 shorter events, 15.6 us)
Async XLA Ops:
  0.6 14.5 %collective-permute-start = (bf16[48,1536]{1,0:T(8,128)(2,1)}, bf16[48,1536]{1,0:T(8,128)(2,1)S(1)}, u32[]{:S(2)}, u32[]{:S(2)}) collective-permute-start(bf16[48,1536]{1,0:T(8,128)(2,1)} %w0.1), channel_id=1, source_target_pairs={{0,2},{1,3},{2,0},{3,1},{4,6},{5,7},{6,4},{7,5},{8,10},{9,11},{10,... | collective-permute-start | bytes 442376 | tf_op jit(solution)/shard_map/ppermute | solution.py:20
  4.7 18.8 %copy-start.25 = (bf16[8,48]{1,0:T(8,128)(2,1)}, bf16[8,48]{1,0:T(8,128)(2,1)S(1)}, u32[]{:S(2)}) copy-start(bf16[8,48]{1,0:T(8,128)(2,1)S(1)} %fusion.4.held) | copy-start | bytes 2308
  4.9 4.7 %collective-permute-start.10 = (bf16[8,1536]{1,0:T(8,128)(2,1)S(1)}, bf16[8,1536]{1,0:T(8,128)(2,1)S(1)}, u32[]{:S(2)}, u32[]{:S(2)}) collective-permute-start(bf16[8,1536]{1,0:T(8,128)(2,1)S(1)} %dynamic_update_slice.5), channel_id=1, source_target_pairs={{0,1},{1,0},{2,3},{3,2},{4,5},{5,4},{6,7},{7,6},{8,9},{9,8},{10,11... | collective-permute-start | bytes 73736 | tf_op jit(solution)/shard_map/ppermute | solution.py:20
  5.0 16.4 %collective-permute-start.1 = (bf16[48,1536]{1,0:T(8,128)(2,1)}, bf16[48,1536]{1,0:T(8,128)(2,1)S(1)}, u32[]{:S(2)}, u32[]{:S(2)}) collective-permute-start(bf16[48,1536]{1,0:T(8,128)(2,1)} %w0.1), channel_id=1, source_target_pairs={{0,4},{1,5},{2,6},{3,7},{4,0},{5,1},{6,2},{7,3},{8,12},{9,13},{10,... | collective-permute-start | bytes 442376 | tf_op jit(solution)/shard_map/ppermute | solution.py:20
  9.7 13.9 %collective-permute-start.2 = (bf16[48,1536]{1,0:T(8,128)(2,1)}, bf16[48,1536]{1,0:T(8,128)(2,1)S(1)}, u32[]{:S(2)}, u32[]{:S(2)}) collective-permute-start(bf16[48,1536]{1,0:T(8,128)(2,1)} %w0.1), channel_id=1, source_target_pairs={{0,6},{1,7},{2,4},{3,5},{4,2},{5,3},{6,0},{7,1},{8,14},{9,15},{10,... | collective-permute-start | bytes 442376 | tf_op jit(solution)/shard_map/ppermute | solution.py:20
  10.6 19.9 %collective-permute-start.11 = (bf16[8,1536]{1,0:T(8,128)(2,1)S(1)}, bf16[8,1536]{1,0:T(8,128)(2,1)S(1)}, u32[]{:S(2)}, u32[]{:S(2)}) collective-permute-start(bf16[8,1536]{1,0:T(8,128)(2,1)S(1)} %add.64), channel_id=1, source_target_pairs={{0,8},{1,9},{2,10},{3,11},{4,12},{5,13},{6,14},{7,15},{8,0},{9,1},... | collective-permute-start | bytes 73736 | tf_op jit(solution)/shard_map/ppermute | solution.py:20
  12.2 18.7 %collective-permute-start.12 = (bf16[8,1536]{1,0:T(8,128)(2,1)S(1)}, bf16[8,1536]{1,0:T(8,128)(2,1)S(1)}, u32[]{:S(2)}, u32[]{:S(2)}) collective-permute-start(bf16[8,1536]{1,0:T(8,128)(2,1)S(1)} %add.64), channel_id=1, source_target_pairs={{0,16},{1,17},{2,18},{3,19},{4,20},{5,21},{6,22},{7,23},{8,24},{9,... | collective-permute-start | bytes 73736 | tf_op jit(solution)/shard_map/ppermute | solution.py:20
  15.1 8.4 %copy-start.13 = (bf16[48,1536]{1,0:T(8,128)(2,1)}, bf16[48,1536]{1,0:T(8,128)(2,1)S(1)}, u32[]{:S(2)}) copy-start(bf16[48,1536]{1,0:T(8,128)(2,1)S(1)} %collective-permute-done.w1) | copy-start | bytes 442372
  15.1 15.8 %collective-permute-start.13 = (bf16[8,1536]{1,0:T(8,128)(2,1)S(1)}, bf16[8,1536]{1,0:T(8,128)(2,1)S(1)}, u32[]{:S(2)}, u32[]{:S(2)}) collective-permute-start(bf16[8,1536]{1,0:T(8,128)(2,1)S(1)} %add.64), channel_id=1, source_target_pairs={{0,24},{1,25},{2,26},{3,27},{4,28},{5,29},{6,30},{7,31},{8,16},{9,... | collective-permute-start | bytes 73736 | tf_op jit(solution)/shard_map/ppermute | solution.py:20
  26.2 25.8 %collective-permute-start.3 = (bf16[192,1536]{1,0:T(8,128)(2,1)}, bf16[192,1536]{1,0:T(8,128)(2,1)S(1)}, u32[]{:S(2)}, u32[]{:S(2)}) collective-permute-start(bf16[192,1536]{1,0:T(8,128)(2,1)} %gather.1.refs_0_), channel_id=1, source_target_pairs={{0,8},{1,9},{2,10},{3,11},{4,12},{5,13},{6,14},{7,15},{8,0},{9,1},... | collective-permute-start | bytes 1769480 | tf_op jit(solution)/shard_map/ppermute | solution.py:20
  27.5 29.1 %collective-permute-start.4 = (bf16[192,1536]{1,0:T(8,128)(2,1)}, bf16[192,1536]{1,0:T(8,128)(2,1)S(1)}, u32[]{:S(2)}, u32[]{:S(2)}) collective-permute-start(bf16[192,1536]{1,0:T(8,128)(2,1)} %gather.1.refs_0_), channel_id=1, source_target_pairs={{0,16},{1,17},{2,18},{3,19},{4,20},{5,21},{6,22},{7,23},{8,24},{9,... | collective-permute-start | bytes 1769480 | tf_op jit(solution)/shard_map/ppermute | solution.py:20
  30.4 28.8 %collective-permute-start.5 = (bf16[192,1536]{1,0:T(8,128)(2,1)}, bf16[192,1536]{1,0:T(8,128)(2,1)S(1)}, u32[]{:S(2)}, u32[]{:S(2)}) collective-permute-start(bf16[192,1536]{1,0:T(8,128)(2,1)} %gather.1.refs_0_), channel_id=1, source_target_pairs={{0,24},{1,25},{2,26},{3,27},{4,28},{5,29},{6,30},{7,31},{8,16},{9,... | collective-permute-start | bytes 1769480 | tf_op jit(solution)/shard_map/ppermute | solution.py:20
  30.9 4.8 %collective-permute-start.14 = (bf16[8,1536]{1,0:T(8,128)(2,1)S(1)}, bf16[8,1536]{1,0:T(8,128)(2,1)S(1)}, u32[]{:S(2)}, u32[]{:S(2)}) collective-permute-start(bf16[8,1536]{1,0:T(8,128)(2,1)S(1)} %add_add_fusion.1), channel_id=1, source_target_pairs={{0,2},{1,3},{2,0},{3,1},{4,6},{5,7},{6,4},{7,5},{8,10},{9,11},{10,... | collective-permute-start | bytes 73736 | tf_op jit(solution)/shard_map/ppermute | solution.py:20
  35.7 6.0 %collective-permute-start.15 = (bf16[8,1536]{1,0:T(8,128)(2,1)S(1)}, bf16[8,1536]{1,0:T(8,128)(2,1)S(1)}, u32[]{:S(2)}, u32[]{:S(2)}) collective-permute-start(bf16[8,1536]{1,0:T(8,128)(2,1)S(1)} %add.68), channel_id=1, source_target_pairs={{0,6},{1,7},{2,4},{3,5},{4,2},{5,3},{6,0},{7,1},{8,14},{9,15},{10,... | collective-permute-start | bytes 73736 | tf_op jit(solution)/shard_map/ppermute | solution.py:20
  51.9 7.2 %copy-start = (bf16[192,1536]{1,0:T(8,128)(2,1)}, bf16[192,1536]{1,0:T(8,128)(2,1)S(1)}, u32[]{:S(2)}) copy-start(bf16[192,1536]{1,0:T(8,128)(2,1)S(1)} %collective-permute-done.3.h1.refs_1_) | copy-start | bytes 1769476
  60.0 8.1 %copy-start.3 = (bf16[192,1536]{1,0:T(8,128)(2,1)S(1)}, bf16[192,1536]{1,0:T(8,128)(2,1)}, u32[]{:S(2)}) copy-start(bf16[192,1536]{1,0:T(8,128)(2,1)} %gather.1.refs_0_) | copy-start | bytes 1769476
  68.1 7.3 %collective-permute-start.16 = (bf16[16,48,1536]{2,1,0:T(8,128)(2,1)}, bf16[16,48,1536]{2,1,0:T(8,128)(2,1)}, u32[]{:S(2)}, u32[]{:S(2)}) collective-permute-start(bf16[16,48,1536]{2,1,0:T(8,128)(2,1)} %get-tuple-element.30), channel_id=1, source_target_pairs={{0,1},{1,0},{2,3},{3,2},{4,5},{5,4},{6,7},{7,6},{8,9},{9,8},{10,11... | collective-permute-start | bytes 7077896 | tf_op jit(solution)/shard_map/ppermute | solution.py:20
  68.1 13.3 %collective-permute-start.6 = (bf16[192,1536]{1,0:T(8,128)(2,1)S(1)}, bf16[192,1536]{1,0:T(8,128)(2,1)S(1)}, u32[]{:S(2)}, u32[]{:S(2)}) collective-permute-start(bf16[192,1536]{1,0:T(8,128)(2,1)S(1)} %copy-done.3), channel_id=1, source_target_pairs={{0,1},{1,0},{2,3},{3,2},{4,5},{5,4},{6,7},{7,6},{8,9},{9,8},{10,11... | collective-permute-start | bytes 1769480 | tf_op jit(solution)/shard_map/ppermute | solution.py:20
  68.6 14.7 %collective-permute-start.7 = (bf16[192,1536]{1,0:T(8,128)(2,1)}, bf16[192,1536]{1,0:T(8,128)(2,1)S(1)}, u32[]{:S(2)}, u32[]{:S(2)}) collective-permute-start(bf16[192,1536]{1,0:T(8,128)(2,1)} %copy-done), channel_id=1, source_target_pairs={{0,1},{1,0},{2,3},{3,2},{4,5},{5,4},{6,7},{7,6},{8,9},{9,8},{10,11... | collective-permute-start | bytes 1769480 | tf_op jit(solution)/shard_map/ppermute | solution.py:20
  68.7 17.4 %collective-permute-start.8 = (bf16[192,1536]{1,0:T(8,128)(2,1)}, bf16[192,1536]{1,0:T(8,128)(2,1)S(1)}, u32[]{:S(2)}, u32[]{:S(2)}) collective-permute-start(bf16[192,1536]{1,0:T(8,128)(2,1)} %copy-done.1), channel_id=1, source_target_pairs={{0,1},{1,0},{2,3},{3,2},{4,5},{5,4},{6,7},{7,6},{8,9},{9,8},{10,11... | collective-permute-start | bytes 1769480 | tf_op jit(solution)/shard_map/ppermute | solution.py:20
  69.2 17.0 %collective-permute-start.9 = (bf16[192,1536]{1,0:T(8,128)(2,1)}, bf16[192,1536]{1,0:T(8,128)(2,1)S(1)}, u32[]{:S(2)}, u32[]{:S(2)}) collective-permute-start(bf16[192,1536]{1,0:T(8,128)(2,1)} %copy-done.2), channel_id=1, source_target_pairs={{0,1},{1,0},{2,3},{3,2},{4,5},{5,4},{6,7},{7,6},{8,9},{9,8},{10,11... | collective-permute-start | bytes 1769480 | tf_op jit(solution)/shard_map/ppermute | solution.py:20
  81.4 35.6 %collective-permute-start.17 = (bf16[4,48,1536]{2,1,0:T(8,128)(2,1)}, bf16[4,48,1536]{2,1,0:T(8,128)(2,1)S(1)}, u32[]{:S(2)}, u32[]{:S(2)}) collective-permute-start(bf16[4,48,1536]{2,1,0:T(8,128)(2,1)} %get-tuple-element.32), channel_id=1, source_target_pairs={{0,8},{1,9},{2,10},{3,11},{4,12},{5,13},{6,14},{7,15},{8,0},{9,1},... | collective-permute-start | bytes 1769480 | tf_op jit(solution)/shard_map/ppermute | solution.py:20
  81.4 4.7 %copy-start.4 = (bf16[192,1536]{1,0:T(8,128)(2,1)}, bf16[192,1536]{1,0:T(8,128)(2,1)S(1)}, u32[]{:S(2)}) copy-start(bf16[192,1536]{1,0:T(8,128)(2,1)S(1)} %collective-permute-done.6.refs_4_) | copy-start | bytes 1769476
  81.4 38.4 %collective-permute-start.18 = (bf16[4,48,1536]{2,1,0:T(8,128)(2,1)}, bf16[4,48,1536]{2,1,0:T(8,128)(2,1)S(1)}, u32[]{:S(2)}, u32[]{:S(2)}) collective-permute-start(bf16[4,48,1536]{2,1,0:T(8,128)(2,1)} %get-tuple-element.33), channel_id=1, source_target_pairs={{0,16},{1,17},{2,18},{3,19},{4,20},{5,21},{6,22},{7,23},{8,24},{9,... | collective-permute-start | bytes 1769480 | tf_op jit(solution)/shard_map/ppermute | solution.py:20
  83.3 2.8 %copy-start.5 = (bf16[192,1536]{1,0:T(8,128)(2,1)}, bf16[192,1536]{1,0:T(8,128)(2,1)S(1)}, u32[]{:S(2)}) copy-start(bf16[192,1536]{1,0:T(8,128)(2,1)S(1)} %collective-permute-done.7.refs_5_) | copy-start | bytes 1769476
  83.3 36.5 %collective-permute-start.19 = (bf16[4,48,1536]{2,1,0:T(8,128)(2,1)}, bf16[4,48,1536]{2,1,0:T(8,128)(2,1)}, u32[]{:S(2)}, u32[]{:S(2)}) collective-permute-start(bf16[4,48,1536]{2,1,0:T(8,128)(2,1)} %get-tuple-element.34), channel_id=1, source_target_pairs={{0,24},{1,25},{2,26},{3,27},{4,28},{5,29},{6,30},{7,31},{8,16},{9,... | collective-permute-start | bytes 1769480 | tf_op jit(solution)/shard_map/ppermute | solution.py:20
  112.9 1.4 collective-permute-start.20
  115.1 15.1 %collective-permute-start.21 = (f32[8,1536]{1,0:T(8,128)S(1)}, f32[8,1536]{1,0:T(8,128)S(1)}, u32[]{:S(2)}, u32[]{:S(2)}) collective-permute-start(f32[8,1536]{1,0:T(8,128)S(1)} %add.70), channel_id=1, source_target_pairs={{0,8},{1,9},{2,10},{3,11},{4,12},{5,13},{6,14},{7,15},{8,0},{9,1},... | collective-permute-start | bytes 147464 | tf_op jit(solution)/shard_map/ppermute | solution.py:20
  115.1 16.3 %collective-permute-start.22 = (f32[8,1536]{1,0:T(8,128)S(1)}, f32[8,1536]{1,0:T(8,128)S(1)}, u32[]{:S(2)}, u32[]{:S(2)}) collective-permute-start(f32[8,1536]{1,0:T(8,128)S(1)} %add.70), channel_id=1, source_target_pairs={{0,16},{1,17},{2,18},{3,19},{4,20},{5,21},{6,22},{7,23},{8,24},{9,... | collective-permute-start | bytes 147464 | tf_op jit(solution)/shard_map/ppermute | solution.py:20
  117.0 2.8 %copy-start.8 = (bf16[4,48,1536]{2,1,0:T(8,128)(2,1)}, bf16[4,48,1536]{2,1,0:T(8,128)(2,1)S(1)}, u32[]{:S(2)}) copy-start(bf16[4,48,1536]{2,1,0:T(8,128)(2,1)S(1)} %collective-permute-done.17.a1) | copy-start | bytes 1769476
  117.0 14.4 %collective-permute-start.23 = (f32[8,1536]{1,0:T(8,128)S(1)}, f32[8,1536]{1,0:T(8,128)S(1)}, u32[]{:S(2)}, u32[]{:S(2)}) collective-permute-start(f32[8,1536]{1,0:T(8,128)S(1)} %add.70), channel_id=1, source_target_pairs={{0,24},{1,25},{2,26},{3,27},{4,28},{5,29},{6,30},{7,31},{8,16},{9,... | collective-permute-start | bytes 147464 | tf_op jit(solution)/shard_map/ppermute | solution.py:20
  124.9 31.2 %collective-permute-start.24 = (bf16[48,1536]{1,0:T(8,128)(2,1)}, bf16[48,1536]{1,0:T(8,128)(2,1)S(1)}, u32[]{:S(2)}, u32[]{:S(2)}) collective-permute-start(bf16[48,1536]{1,0:T(8,128)(2,1)} %get-tuple-element.42), channel_id=1, source_target_pairs={{0,2},{1,3},{2,0},{3,1},{4,6},{5,7},{6,4},{7,5},{8,10},{9,11},{10,... | collective-permute-start | bytes 442376 | tf_op jit(solution)/shard_map/ppermute | solution.py:20
  126.3 29.8 %collective-permute-start.25 = (bf16[48,1536]{1,0:T(8,128)(2,1)}, bf16[48,1536]{1,0:T(8,128)(2,1)S(1)}, u32[]{:S(2)}, u32[]{:S(2)}) collective-permute-start(bf16[48,1536]{1,0:T(8,128)(2,1)} %get-tuple-element.43), channel_id=1, source_target_pairs={{0,4},{1,5},{2,6},{3,7},{4,0},{5,1},{6,2},{7,3},{8,12},{9,13},{10,... | collective-permute-start | bytes 442376 | tf_op jit(solution)/shard_map/ppermute | solution.py:20
  130.2 25.9 %collective-permute-start.26 = (bf16[48,1536]{1,0:T(8,128)(2,1)}, bf16[48,1536]{1,0:T(8,128)(2,1)S(1)}, u32[]{:S(2)}, u32[]{:S(2)}) collective-permute-start(bf16[48,1536]{1,0:T(8,128)(2,1)} %get-tuple-element.44), channel_id=1, source_target_pairs={{0,6},{1,7},{2,4},{3,5},{4,2},{5,3},{6,0},{7,1},{8,14},{9,15},{10,... | collective-permute-start | bytes 442376 | tf_op jit(solution)/shard_map/ppermute | solution.py:20
  131.4 14.6 %copy-start.10 = (f32[8,1536]{1,0:T(8,128)}, f32[8,1536]{1,0:T(8,128)S(1)}, u32[]{:S(2)}) copy-start(f32[8,1536]{1,0:T(8,128)S(1)} %add_add_fusion.refs_11_) | copy-start | bytes 147460
  131.4 10.8 %collective-permute-start.27 = (f32[8,1536]{1,0:T(8,128)S(1)}, f32[8,1536]{1,0:T(8,128)S(1)}, u32[]{:S(2)}, u32[]{:S(2)}) collective-permute-start(f32[8,1536]{1,0:T(8,128)S(1)} %add_add_fusion.refs_11_), channel_id=1, source_target_pairs={{0,2},{1,3},{2,0},{3,1},{4,6},{5,7},{6,4},{7,5},{8,10},{9,11},{10,... | collective-permute-start | bytes 147464 | tf_op jit(solution)/shard_map/ppermute | solution.py:20
  142.2 13.8 %copy-start.12 = (f32[8,1536]{1,0:T(8,128)}, f32[8,1536]{1,0:T(8,128)S(1)}, u32[]{:S(2)}) copy-start(f32[8,1536]{1,0:T(8,128)S(1)} %add.74.h2) | copy-start | bytes 147460
  142.2 22.5 %collective-permute-start.31 = (f32[8,1536]{1,0:T(8,128)S(1)}, f32[8,1536]{1,0:T(8,128)S(1)}, u32[]{:S(2)}, u32[]{:S(2)}) collective-permute-start(f32[8,1536]{1,0:T(8,128)S(1)} %add.74.h2), channel_id=1, source_target_pairs={{0,6},{1,7},{2,4},{3,5},{4,2},{5,3},{6,0},{7,1},{8,14},{9,15},{10,... | collective-permute-start | bytes 147464 | tf_op jit(solution)/shard_map/ppermute | solution.py:20
  160.1 6.1 %collective-permute-start.28 = (f32[48,384]{1,0:T(8,128)}, f32[48,384]{1,0:T(8,128)S(1)}, u32[]{:S(2)}, u32[]{:S(2)}) collective-permute-start(f32[48,384]{1,0:T(8,128)} %get-tuple-element.46), channel_id=1, source_target_pairs={{0,32},{32,0},{64,96},{96,64},{128,160},{160,128},{192,224},{224,1... | collective-permute-start | bytes 221192 | tf_op jit(solution)/shard_map/ppermute | solution.py:25
  161.6 6.1 %collective-permute-start.29 = (f32[48,384]{1,0:T(8,128)}, f32[48,384]{1,0:T(8,128)S(1)}, u32[]{:S(2)}, u32[]{:S(2)}) collective-permute-start(f32[48,384]{1,0:T(8,128)} %get-tuple-element.47), channel_id=1, source_target_pairs={{0,64},{32,96},{64,0},{96,32},{128,192},{160,224},{192,128},{224,1... | collective-permute-start | bytes 221192 | tf_op jit(solution)/shard_map/ppermute | solution.py:25
  164.3 5.8 %collective-permute-start.30 = (f32[48,384]{1,0:T(8,128)}, f32[48,384]{1,0:T(8,128)S(1)}, u32[]{:S(2)}, u32[]{:S(2)}) collective-permute-start(f32[48,384]{1,0:T(8,128)} %get-tuple-element.48), channel_id=1, source_target_pairs={{0,96},{32,64},{64,32},{96,0},{128,224},{160,192},{192,160},{224,1... | collective-permute-start | bytes 221192 | tf_op jit(solution)/shard_map/ppermute | solution.py:25
  166.2 3.9 %copy-start.22 = (f32[48,384]{1,0:T(8,128)}, f32[48,384]{1,0:T(8,128)S(1)}, u32[]{:S(2)}) copy-start(f32[48,384]{1,0:T(8,128)S(1)} %collective-permute-done.28.v1) | copy-start | bytes 221188
  172.3 4.7 %collective-permute-start.32 = (f32[56,384]{1,0:T(8,128)}, f32[56,384]{1,0:T(8,128)S(1)}, u32[]{:S(2)}, u32[]{:S(2)}) collective-permute-start(f32[56,384]{1,0:T(8,128)} %pack.1), channel_id=1, source_target_pairs={{0,128},{32,160},{64,192},{96,224},{128,0},{160,32},{192,64},{224,... | collective-permute-start | bytes 258056 | tf_op jit(solution)/shard_map/ppermute | solution.py:25
  177.9 7.7 %copy-start.11 = (f32[56,384]{1,0:T(8,128)}, f32[56,384]{1,0:T(8,128)S(1)}, u32[]{:S(2)}) copy-start(f32[56,384]{1,0:T(8,128)S(1)} %add.76.v0) | copy-start | bytes 258052
  177.9 4.8 %collective-permute-start.33 = (f32[56,384]{1,0:T(8,128)S(1)}, f32[56,384]{1,0:T(8,128)S(1)}, u32[]{:S(2)}, u32[]{:S(2)}) collective-permute-start(f32[56,384]{1,0:T(8,128)S(1)} %add.76.v0), channel_id=1, source_target_pairs={{0,32},{32,0},{64,96},{96,64},{128,160},{160,128},{192,224},{224,1... | collective-permute-start | bytes 258056 | tf_op jit(solution)/shard_map/ppermute | solution.py:25
  178.1 6.1 %collective-permute-start.34 = (f32[56,384]{1,0:T(8,128)S(1)}, f32[56,384]{1,0:T(8,128)S(1)}, u32[]{:S(2)}, u32[]{:S(2)}) collective-permute-start(f32[56,384]{1,0:T(8,128)S(1)} %add.76.v0), channel_id=1, source_target_pairs={{0,64},{32,96},{64,0},{96,32},{128,192},{160,224},{192,128},{224,1... | collective-permute-start | bytes 258056 | tf_op jit(solution)/shard_map/ppermute | solution.py:25
  180.0 5.7 %collective-permute-start.35 = (f32[56,384]{1,0:T(8,128)S(1)}, f32[56,384]{1,0:T(8,128)S(1)}, u32[]{:S(2)}, u32[]{:S(2)}) collective-permute-start(f32[56,384]{1,0:T(8,128)S(1)} %add.76.v0), channel_id=1, source_target_pairs={{0,96},{32,64},{64,32},{96,0},{128,224},{160,192},{192,160},{224,1... | collective-permute-start | bytes 258056 | tf_op jit(solution)/shard_map/ppermute | solution.py:25
  182.7 2.9 %copy-start.19 = (f32[56,384]{1,0:T(8,128)}, f32[56,384]{1,0:T(8,128)S(1)}, u32[]{:S(2)}) copy-start(f32[56,384]{1,0:T(8,128)S(1)} %collective-permute-done.33.v1) | copy-start | bytes 258052
  (14 other events, 16.1 us)

commit v5 on v2

--- a/solution.py
+++ b/solution.py
@@ -111,7 +111,7 @@
     )(lens, par, glu)
 
 
-def outer_kernel(core, sw, cot, h1, h2, h3, keep, send):
+def outer_kernel(core, sw, cot, h1, h2, keep, send):
     res = lax.dot_general(
         sw[...], cot[...], (((0,), (0,)), ((), ())), preferred_element_type=F32
     )
@@ -136,7 +136,6 @@
                 whole((frames, width)),
                 HBM,
                 HBM,
-                HBM,
             ],
             out_specs=(
                 pl.BlockSpec((4, 48, width), lambda i, *_: (i, 0, 0)),
@@ -255,9 +254,10 @@
     )(pos, *parts)
 
 
-def gather_kernel(w0, w1, w2, w3, held, out):
-    rows = w0.shape[0]
-    for n, w in enumerate((w0, w1, w2, w3)):
+def gather_kernel(*refs):
+    parts, out = refs[:-2], refs[-1]
+    rows = parts[0].shape[0]
+    for n, w in enumerate(parts):
         out[n * rows : n * rows + rows, :] = w[...]
 
 
@@ -265,10 +265,10 @@
     rows, width = w[0].shape
     return pl.pallas_call(
         gather_kernel,
-        out_shape=sds((4 * rows, width), BF16),
+        out_shape=sds((len(w) * rows, width), BF16),
         grid=(1,),
-        in_specs=[whole((rows, width))] * 4 + [HBM],
-        out_specs=whole((4 * rows, width)),
+        in_specs=[whole((rows, width))] * len(w) + [HBM],
+        out_specs=whole((len(w) * rows, width)),
         compiler_params=compiler(),
         name="gather",
         **params(0.1),
@@ -279,12 +279,13 @@
     y, z, core = pos[0], pos[2], pos[3]
     copies = []
     for n, piece in enumerate(pieces):
-        for j in range(16):
-            index = ((y ^ (j // 4)) * 4 + (z ^ (j % 4))) * 2 + (core ^ n)
+        dc, dy = n // 4, n % 4
+        for dz in range(4):
+            index = ((y ^ dy) * 4 + (z ^ dz)) * 2 + (core ^ dc)
             at = pl.multiple_of(index * 48, 48)
             copies.append(
                 pltpu.make_async_copy(
-                    piece.at[pl.ds(j * 48, 48), :], buf.at[pl.ds(at, 48), :], sem.at[n * 16 + j]
+                    piece.at[pl.ds(dz * 48, 48), :], buf.at[pl.ds(at, 48), :], sem.at[n * 4 + dz]
                 )
             )
     for c in copies:
@@ -294,7 +295,7 @@
 
 
 def project_kernel(pos, *refs):
-    pieces, (sw, res, _, _, out, buf, sem) = refs[:2], refs[2:]
+    pieces, (sw, res, _, _, out, buf, sem) = refs[:8], refs[8:]
 
     @pl.when(pl.program_id(0) == 0)
     def _():
@@ -313,7 +314,7 @@
         grid_spec=pltpu.PrefetchScalarGridSpec(
             num_scalar_prefetch=1,
             grid=(frames // rows,),
-            in_specs=[HBM] * 2 + [block, block, HBM, HBM],
+            in_specs=[HBM] * 8 + [block, block, HBM, HBM],
             out_specs=block,
             scratch_shapes=[pltpu.VMEM((width, width), BF16), pltpu.SemaphoreType.DMA((32,))],
         ),
@@ -324,8 +325,8 @@
 
 
 def backward_kernel(pos, *refs, rows, chunk, unroll):
-    pieces = refs[:2]
-    par, cot, nrm, rst, _, gconv, sums, buf, sem, grad = refs[2:]
+    pieces = refs[:8]
+    par, cot, nrm, rst, _, gconv, sums, buf, sem, grad = refs[8:]
     step = pl.program_id(0)
     width = cot.shape[1]
     length = pos[4]
@@ -370,7 +371,7 @@
         grid_spec=pltpu.PrefetchScalarGridSpec(
             num_scalar_prefetch=1,
             grid=(frames // rows,),
-            in_specs=[HBM] * 2
+            in_specs=[HBM] * 8
             + [whole((8, width)), block(width), block(width), block(128), HBM],
             out_specs=(block(width), whole((2, 8, width))),
             scratch_shapes=[
@@ -381,7 +382,7 @@
         ),
         compiler_params=compiler(),
         name="backward",
-        **params(21),
+        **params(0.1),
     )(pos, *pieces, par, cot, nrm, rst, held)
 
 
@@ -457,7 +458,7 @@
         ),
         compiler_params=compiler(),
         name="taps",
-        **params(10),
+        **params(0.1),
     )(pos, par, glu, gconv, norm_sums)
 
 
@@ -474,19 +475,19 @@
     par = lax.dynamic_update_slice(jnp.zeros((8, width), BF16), own, (0, f * 48))
     par = par + fsdp_move(par, core=1)
     par = (par + fsdp_move(par, y=1)) + (fsdp_move(par, y=2) + fsdp_move(par, y=3))
-    par = par + fsdp_move(par, z=1)
-    par = par + fsdp_move(par, z=3)
+    half = par + fsdp_move(par, z=1)
+    par = half + fsdp_move(half, z=3)
     par = par.astype(F32)
 
-    block = gather([proj_weight] + [fsdp_move(proj_weight, z=k) for k in (1, 2, 3)], own)
+    block = gather([proj_weight] + [fsdp_move(proj_weight, z=k) for k in (1, 2, 3)], half)
     near = [block] + [fsdp_move(block, y=k) for k in (1, 2, 3)]
 
     swished, normed, rstd = forward(lengths, par, glu)
-    keep, send = outer(core[None].astype(jnp.int32), swished, cot, near[1:])
+    keep, send = outer(core[None].astype(jnp.int32), swished, cot, (near[1], near[3]))
     recv = fsdp_move(send, core=1)
     a = stage1(pos, keep, recv)
-    mine = gather(near, a[0])
-    pieces = [mine, fsdp_move(mine, core=1)]
+    near[2] = gather(near[2:3], a[0])
+    pieces = near + [fsdp_move(p, core=1) for p in near]
     gconv, sums = backward(pos, pieces, par, cot, normed, rstd, a[0])
     glu_grad, small = taps(pos, par, glu, gconv, sums)
     v = stage2(pos, [a[0]] + [fsdp_move(a[k], y=k) for k in (1, 2, 3)], glu_grad)

time: 179 us -> 181 us (1.011)
  waiting for transfers between devices: 32.7 us -> 35.7 us
    ppermute x26 -> x29, waiting for transfers between devices: 29 us -> 32.3 us  [fsdp_move(): return lax.ppermute(value, 'fsdp', perm)]
    ppermute x26 -> x29, starting transfers between devices: 41.3 us -> 39.4 us  [fsdp_move(): return lax.ppermute(value, 'fsdp', perm)]
    unnamed x42 -> x44, local copies, waits for them, and re-layouts: 7.22 us -> 6.74 us
  transfers between devices with their start and end apart: 37 -> 40, of which waited for: 15 -> 12; matrix products, arithmetic and copies ran while one was open for 3% -> 3% of each run, Pallas kernels for 29% -> 32%
where the time goes in v5:
time: 181 us; the launch traced here: 180 us
  Pallas kernels  72.5 us (40%)
  starting transfers between devices  55.6 us (31%)
  waiting for transfers between devices  35.7 us (20%)
  local copies, waits for them, and re-layouts  8.24 us (5%)
  other arithmetic  5.94 us (3%)
    ppermute x29, starting transfers between devices, fsdp_move(): return lax.ppermute(value, 'fsdp', perm)  39.4 us
    ppermute x29, waiting for transfers between devices, fsdp_move(): return lax.ppermute(value, 'fsdp', perm)  32.3 us
    ppermute x11, starting transfers between devices, dp_move(): return lax.ppermute(value, 'dp', perm)  16.2 us
    pallas_call x1, Pallas kernels, backward(): pl.pallas_call(functools.partial(backward_kernel, rows=rows, chunk=chunk,...  15.7 us
    pallas_call x1, Pallas kernels, project(): pl.pallas_call(project_kernel, out_shape=sds((frames, width), BF16), grid...  10 us
    pallas_call x1, Pallas kernels, taps(): pl.pallas_call(functools.partial(taps_kernel, rows=rows, frames=frames, c...  9.98 us
    pallas_call x1, Pallas kernels, forward(): pl.pallas_call(functools.partial(forward_kernel, rows=rows, frames=frames...  9.58 us
    pallas_call x1, Pallas kernels, outer(): pl.pallas_call(outer_kernel, out_shape=(sds((16, 48, width), F32), sds((1...  8.11 us
  transfers between devices with their start and end apart: 40, of which 12 were waited for; matrix products, arithmetic and copies ran while one was open for 3% of the time, Pallas kernels for 32%

profile of v5, /device:TPU:32, one launch (start us, length us, event | category | flops | bytes accessed | tf_op | source)
XLA Modules:
  0.0 179.6 jit_solution(10492134303760969670)
XLA Ops:
  1.6 1.2 collective-permute-done.3
  3.7 3.3 %collective-permute-start.5 = (bf16[8,1536]{1,0:T(8,128)(2,1)S(1)}, bf16[8,1536]{1,0:T(8,128)(2,1)S(1)}, u32[]{:S(2)}, u32[]{:S(2)}) collective-permute-start(bf16[8,1536]{1,0:T(8,128)(2,1)S(1)} %add.83), channel_id=1, source_target_pairs={{0,16},{1,17},{2,18},{3,19},{4,20},{5,21},{6,22},{7,23},{8,24},{9,... | collective-permute-start | bytes 73736 | tf_op jit(solution)/shard_map/ppermute | solution.py:20
  7.0 1.1 collective-permute-start.6
  8.1 3.4 %collective-permute-start = (bf16[48,1536]{1,0:T(8,128)(2,1)}, bf16[48,1536]{1,0:T(8,128)(2,1)S(1)}, u32[]{:S(2)}, u32[]{:S(2)}) collective-permute-start(bf16[48,1536]{1,0:T(8,128)(2,1)} %refs_0_.1), channel_id=1, source_target_pairs={{0,2},{1,3},{2,0},{3,1},{4,6},{5,7},{6,4},{7,5},{8,10},{9,11},{10,... | collective-permute-start | bytes 442376 | tf_op jit(solution)/shard_map/ppermute | solution.py:20
  11.5 4.5 %collective-permute-start.1 = (bf16[48,1536]{1,0:T(8,128)(2,1)}, bf16[48,1536]{1,0:T(8,128)(2,1)S(1)}, u32[]{:S(2)}, u32[]{:S(2)}) collective-permute-start(bf16[48,1536]{1,0:T(8,128)(2,1)} %refs_0_.1), channel_id=1, source_target_pairs={{0,4},{1,5},{2,6},{3,7},{4,0},{5,1},{6,2},{7,3},{8,12},{9,13},{10,... | collective-permute-start | bytes 442376 | tf_op jit(solution)/shard_map/ppermute | solution.py:20
  16.0 2.1 %collective-permute-start.7 = (bf16[8,1536]{1,0:T(8,128)(2,1)S(1)}, bf16[8,1536]{1,0:T(8,128)(2,1)S(1)}, u32[]{:S(2)}, u32[]{:S(2)}) collective-permute-start(bf16[8,1536]{1,0:T(8,128)(2,1)S(1)} %add_add_fusion.2), channel_id=1, source_target_pairs={{0,2},{1,3},{2,0},{3,1},{4,6},{5,7},{6,4},{7,5},{8,10},{9,11},{10,... | collective-permute-start | bytes 73736 | tf_op jit(solution)/shard_map/ppermute | solution.py:20
  18.1 7.3 %collective-permute-done.7 = bf16[8,1536]{1,0:T(8,128)(2,1)S(1)} collective-permute-done((bf16[8,1536]{1,0:T(8,128)(2,1)S(1)}, bf16[8,1536]{1,0:T(8,128)(2,1)S(1)}, u32[]{:S(2)}, u32[]{:S(2)}) %collective-permute-start.7) | collective-permute-done | bytes 24608 | tf_op jit(solution)/shard_map/ppermute | solution.py:20
  26.0 3.1 %collective-permute-done.2.refs_3_ = bf16[48,1536]{1,0:T(8,128)(2,1)S(1)} collective-permute-done((bf16[48,1536]{1,0:T(8,128)(2,1)}, bf16[48,1536]{1,0:T(8,128)(2,1)S(1)}, u32[]{:S(2)}, u32[]{:S(2)}) %collective-permute-start.2) | collective-permute-done | bytes 147488 | tf_op jit(solution)/shard_map/ppermute | solution.py:20
  29.8 2.0 %gather.2.refs_0_ = bf16[192,1536]{1,0:T(8,128)(2,1)} custom-call(bf16[48,1536]{1,0:T(8,128)(2,1)} %refs_0_.1, bf16[48,1536]{1,0:T(8,128)(2,1)} %copy-done.13, bf16[48,1536]{1,0:T(8,128)(2,1)} %copy-done.15, bf16[48,1536]{1,0:T(8,128)(2,1)} %copy-done.16, bf16[8,1536]{1,0:T(8,128)(2,1)} %add.87.refs_4_), custom_call_target="tpu_custom_call" | custom-call | bytes 360000 | tf_op jit(solution)/shard_map/gather/pallas_call | solution.py:266
  31.7 1.7 collective-permute-start.8
  33.5 2.2 %collective-permute-start.11 = (bf16[192,1536]{1,0:T(8,128)(2,1)}, bf16[192,1536]{1,0:T(8,128)(2,1)S(1)}, u32[]{:S(2)}, u32[]{:S(2)}) collective-permute-start(bf16[192,1536]{1,0:T(8,128)(2,1)} %gather.2.refs_0_), channel_id=1, source_target_pairs={{0,24},{1,25},{2,26},{3,27},{4,28},{5,29},{6,30},{7,31},{8,16},{9,... | collective-permute-start | bytes 1769480 | tf_op jit(solution)/shard_map/ppermute | solution.py:20
  35.7 2.3 %collective-permute-start.10 = (bf16[8,1536]{1,0:T(8,128)(2,1)}, bf16[8,1536]{1,0:T(8,128)(2,1)S(1)}, u32[]{:S(2)}, u32[]{:S(2)}) collective-permute-start(bf16[8,1536]{1,0:T(8,128)(2,1)} %add.87.refs_4_), channel_id=1, source_target_pairs={{0,6},{1,7},{2,4},{3,5},{4,2},{5,3},{6,0},{7,1},{8,14},{9,15},{10,... | collective-permute-start | bytes 73736 | tf_op jit(solution)/shard_map/ppermute | solution.py:20
  38.6 3.4 %collective-permute-done.10 = bf16[8,1536]{1,0:T(8,128)(2,1)S(1)} collective-permute-done((bf16[8,1536]{1,0:T(8,128)(2,1)}, bf16[8,1536]{1,0:T(8,128)(2,1)S(1)}, u32[]{:S(2)}, u32[]{:S(2)}) %collective-permute-start.10) | collective-permute-done | bytes 24608 | tf_op jit(solution)/shard_map/ppermute | solution.py:20
  42.1 1.4 add_convert_fusion.par.refs_8_
  43.4 9.6 %forward.1 = (bf16[768,1536]{1,0:T(8,128)(2,1)}, f32[768,1536]{1,0:T(8,128)}, f32[768,128]{1,0:T(8,128)}) custom-call(s32[1]{0:T(128)S(6)} %copy.15.lens, f32[8,1536]{1,0:T(8,128)} %add_convert_fusion.par.refs_8_, bf16[768,1536]{1,0:T(8,128)(2,1)} %bitcast.14), custom_call_target="tpu_custom_call" | custom-call | bytes 360000 | tf_op jit(solution)/shard_map/forward/pallas_call | solution.py:98
  54.0 8.1 %outer.1 = (f32[16,48,1536]{2,1,0:T(8,128)}, bf16[16,48,1536]{2,1,0:T(8,128)(2,1)}) custom-call(s32[1]{0:T(128)} %bitcast.3.core, bf16[768,1536]{1,0:T(8,128)(2,1)} %get-tuple-element.26.sw.refs_8_, bf16[768,1536]{1,0:T(8,128)(2,1)} %bitcast.16, bf16[192,1536]{1,0:T(8,128)(2,1)} %copy-done, bf16[192,1536]{1,0:T(8,128)(2,1)} %copy-done.1), custom_call_target="tpu_custom_call" | custom-call | bytes 360000 | tf_op jit(solution)/shard_map/outer/pallas_call | solution.py:128
  63.9 3.7 %collective-permute-done.12 = bf16[16,48,1536]{2,1,0:T(8,128)(2,1)S(1)} collective-permute-done((bf16[16,48,1536]{2,1,0:T(8,128)(2,1)}, bf16[16,48,1536]{2,1,0:T(8,128)(2,1)S(1)}, u32[]{:S(2)}, u32[]{:S(2)}) %collective-permute-start.12) | collective-permute-done | bytes 2359328 | tf_op jit(solution)/shard_map/ppermute | solution.py:20
  67.5 1.4 copy-done.3
  69.0 6.0 %stage1.1 = (f32[4,48,1536]{2,1,0:T(8,128)}, bf16[4,48,1536]{2,1,0:T(8,128)(2,1)}, bf16[4,48,1536]{2,1,0:T(8,128)(2,1)}, bf16[4,48,1536]{2,1,0:T(8,128)(2,1)}) custom-call(s32[5]{0:T(128)} %stack.19.pos, f32[4,4,48,1536]{3,2,1,0:T(8,128)} %bitcast.19, bf16[4,4,48,1536]{3,2,1,0:T(8,128)(2,1)} %bitcast.20), custom_call_target="tpu_custom_call" | custom-call | bytes 360000 | tf_op jit(solution)/shard_map/stage1/pallas_call | solution.py:165
  74.9 4.6 %collective-permute-done.9.refs_0_ = bf16[192,1536]{1,0:T(8,128)(2,1)} collective-permute-done((bf16[192,1536]{1,0:T(8,128)(2,1)S(1)}, bf16[192,1536]{1,0:T(8,128)(2,1)}, u32[]{:S(2)}, u32[]{:S(2)}) %collective-permute-start.9) | collective-permute-done | bytes 589856 | tf_op jit(solution)/shard_map/ppermute | solution.py:20
  79.5 1.9 %gather.3.refs_2_ = bf16[192,1536]{1,0:T(8,128)(2,1)} custom-call(bf16[192,1536]{1,0:T(8,128)(2,1)} %collective-permute-done.9.refs_0_, f32[4,48,1536]{2,1,0:T(8,128)} %get-tuple-element.29.refs_1_.refs_12_.a0), custom_call_target="tpu_custom_call" | custom-call | bytes 360000 | tf_op jit(solution)/shard_map/gather/pallas_call | solution.py:266
  81.5 2.5 %collective-permute-start.18 = (bf16[4,48,1536]{2,1,0:T(8,128)(2,1)}, bf16[4,48,1536]{2,1,0:T(8,128)(2,1)S(1)}, u32[]{:S(2)}, u32[]{:S(2)}) collective-permute-start(bf16[4,48,1536]{2,1,0:T(8,128)(2,1)} %get-tuple-element.31), channel_id=1, source_target_pairs={{0,16},{1,17},{2,18},{3,19},{4,20},{5,21},{6,22},{7,23},{8,24},{9,... | collective-permute-start | bytes 1769480 | tf_op jit(solution)/shard_map/ppermute | solution.py:20
  84.0 2.2 %collective-permute-start.19 = (bf16[4,48,1536]{2,1,0:T(8,128)(2,1)S(1)}, bf16[4,48,1536]{2,1,0:T(8,128)(2,1)S(1)}, u32[]{:S(2)}, u32[]{:S(2)}) collective-permute-start(bf16[4,48,1536]{2,1,0:T(8,128)(2,1)S(1)} %copy-done.21), channel_id=1, source_target_pairs={{0,24},{1,25},{2,26},{3,27},{4,28},{5,29},{6,30},{7,31},{8,16},{9,... | collective-permute-start | bytes 1769480 | tf_op jit(solution)/shard_map/ppermute | solution.py:20
  87.0 15.7 %backward.1 = (f32[768,1536]{1,0:T(8,128)}, f32[2,8,1536]{2,1,0:T(8,128)}) custom-call(s32[5]{0:T(128)} %stack.19.pos, bf16[192,1536]{1,0:T(8,128)(2,1)} %gather.2.refs_0_, bf16[192,1536]{1,0:T(8,128)(2,1)} %copy-done, bf16[192,1536]{1,0:T(8,128)(2,1)} %gather.3.refs_2_, bf16[192,1536]{1,0:T(8,128)(2,1)} %copy-done.1, bf16[192,1536]{1,0:T(8,128)(2,1)} %copy-done.4, ...), custom_call_target="tpu_custom_call" | custom-call | bytes 360000 | tf_op jit(solution)/shard_map/backward/pallas_call | solution.py:368
  102.7 10.0 %taps.1 = (bf16[768,1536]{1,0:T(8,128)(2,1)}, f32[8,1536]{1,0:T(8,128)}) custom-call(s32[5]{0:T(128)} %stack.19.pos, f32[8,1536]{1,0:T(8,128)} %add_convert_fusion.par.refs_8_, bf16[768,1536]{1,0:T(8,128)(2,1)} %bitcast.15, f32[768,1536]{1,0:T(8,128)} %get-tuple-element.35.gconv, f32[2,8,1536]{2,1,0:T(8,128)} %get-tuple-element.36.norm_sums), custom_call_target="tpu_custom_call" | custom-call | bytes 360000 | tf_op jit(solution)/shard_map/taps/pallas_call | solution.py:444
  112.7 1.4 collective-permute-done.20
  115.0 1.6 collective-permute-start.23
  116.5 1.9 %collective-permute-start.21 = (f32[8,1536]{1,0:T(8,128)S(1)}, f32[8,1536]{1,0:T(8,128)S(1)}, u32[]{:S(2)}, u32[]{:S(2)}) collective-permute-start(f32[8,1536]{1,0:T(8,128)S(1)} %add.89), channel_id=1, source_target_pairs={{0,8},{1,9},{2,10},{3,11},{4,12},{5,13},{6,14},{7,15},{8,0},{9,1},... | collective-permute-start | bytes 147464 | tf_op jit(solution)/shard_map/ppermute | solution.py:20
  119.5 4.2 %stage2.1 = (f32[48,1536]{1,0:T(8,128)}, bf16[48,1536]{1,0:T(8,128)(2,1)}, bf16[48,1536]{1,0:T(8,128)(2,1)}, bf16[48,1536]{1,0:T(8,128)(2,1)}) custom-call(s32[5]{0:T(128)} %stack.19.pos, f32[4,48,1536]{2,1,0:T(8,128)} %get-tuple-element.29.refs_1_.refs_12_.a0, bf16[4,48,1536]{2,1,0:T(8,128)(2,1)} %copy-done.6, bf16[4,48,1536]{2,1,0:T(8,128)(2,1)} %copy-done.7, ...), custom_call_target="tpu_custom_call" | custom-call | bytes 10800000 | tf_op jit(solution)/shard_map/stage2/pallas_call | solution.py:193
  123.7 1.1 collective-permute-start.24
  124.8 3.8 %collective-permute-start.25 = (bf16[48,1536]{1,0:T(8,128)(2,1)}, bf16[48,1536]{1,0:T(8,128)(2,1)S(1)}, u32[]{:S(2)}, u32[]{:S(2)}) collective-permute-start(bf16[48,1536]{1,0:T(8,128)(2,1)} %get-tuple-element.41), channel_id=1, source_target_pairs={{0,4},{1,5},{2,6},{3,7},{4,0},{5,1},{6,2},{7,3},{8,12},{9,13},{10,... | collective-permute-start | bytes 442376 | tf_op jit(solution)/shard_map/ppermute | solution.py:20
  128.6 1.6 collective-permute-start.26
  130.9 10.0 %project.1.held = bf16[768,1536]{1,0:T(8,128)(2,1)} custom-call(s32[5]{0:T(128)} %stack.19.pos, bf16[192,1536]{1,0:T(8,128)(2,1)} %gather.2.refs_0_, bf16[192,1536]{1,0:T(8,128)(2,1)} %copy-done, bf16[192,1536]{1,0:T(8,128)(2,1)} %gather.3.refs_2_, bf16[192,1536]{1,0:T(8,128)(2,1)} %copy-done.1, bf16[192,1536]{1,0:T(8,128)(2,1)} %copy-done.4, ...), custom_call_target="tpu_custom_call" | custom-call | bytes 39600000 | tf_op jit(solution)/shard_map/project/pallas_call | solution.py:311
  141.0 1.9 %collective-permute-done.26.v3 = bf16[48,1536]{1,0:T(8,128)(2,1)S(1)} collective-permute-done((bf16[48,1536]{1,0:T(8,128)(2,1)}, bf16[48,1536]{1,0:T(8,128)(2,1)S(1)}, u32[]{:S(2)}, u32[]{:S(2)}) %collective-permute-start.26) | collective-permute-done | bytes 147488 | tf_op jit(solution)/shard_map/ppermute | solution.py:20
  143.6 2.6 %stage3.1 = (f32[48,384]{1,0:T(8,128)}, f32[48,384]{1,0:T(8,128)}, f32[48,384]{1,0:T(8,128)}, f32[48,384]{1,0:T(8,128)}) custom-call(s32[5]{0:T(128)} %stack.19.pos, f32[48,1536]{1,0:T(8,128)} %get-tuple-element.38.refs_10_.v0, bf16[48,1536]{1,0:T(8,128)(2,1)} %copy-done.11, bf16[48,1536]{1,0:T(8,128)(2,1)} %copy-done.12, bf16[48,1536]{1,0:T(8,128)(2,1)} %copy-done.14, ...), custom_call_target="tpu_custom_call" | custom-call | bytes 7200000 | tf_op jit(solution)/shard_map/stage3/pallas_call | solution.py:218
  146.2 3.0 %collective-permute-start.28 = (f32[48,384]{1,0:T(8,128)}, f32[48,384]{1,0:T(8,128)S(1)}, u32[]{:S(2)}, u32[]{:S(2)}) collective-permute-start(f32[48,384]{1,0:T(8,128)} %get-tuple-element.45), channel_id=1, source_target_pairs={{0,64},{32,96},{64,0},{96,32},{128,192},{160,224},{192,128},{224,1... | collective-permute-start | bytes 221192 | tf_op jit(solution)/shard_map/ppermute | solution.py:25
  149.2 1.1 collective-permute-start.29
  151.3 4.0 %collective-permute-done.34 = f32[8,1536]{1,0:T(8,128)S(1)} collective-permute-done((f32[8,1536]{1,0:T(8,128)S(1)}, f32[8,1536]{1,0:T(8,128)S(1)}, u32[]{:S(2)}, u32[]{:S(2)}) %collective-permute-start.34) | collective-permute-done | bytes 49184 | tf_op jit(solution)/shard_map/ppermute | solution.py:20
  155.4 2.1 %collective-permute-start.35 = (f32[8,1536]{1,0:T(8,128)S(1)}, f32[8,1536]{1,0:T(8,128)S(1)}, u32[]{:S(2)}, u32[]{:S(2)}) collective-permute-start(f32[8,1536]{1,0:T(8,128)S(1)} %add.97), channel_id=1, source_target_pairs={{0,6},{1,7},{2,4},{3,5},{4,2},{5,3},{6,0},{7,1},{8,14},{9,15},{10,... | collective-permute-start | bytes 147464 | tf_op jit(solution)/shard_map/ppermute | solution.py:20
  158.4 2.2 %collective-permute-start.30 = (f32[48,384]{1,0:T(8,128)S(1)}, f32[48,384]{1,0:T(8,128)S(1)}, u32[]{:S(2)}, u32[]{:S(2)}) collective-permute-start(f32[48,384]{1,0:T(8,128)S(1)} %add_add_fusion), channel_id=1, source_target_pairs={{0,128},{32,160},{64,192},{96,224},{128,0},{160,32},{192,64},{224,... | collective-permute-start | bytes 221192 | tf_op jit(solution)/shard_map/ppermute | solution.py:25
  160.5 1.6 collective-permute-done.35
  162.2 3.4 %collective-permute-start.37 = (f32[8,48]{1,0:T(8,128)S(1)}, f32[8,48]{1,0:T(8,128)S(1)}, u32[]{:S(2)}, u32[]{:S(2)}) collective-permute-start(f32[8,48]{1,0:T(8,128)S(1)} %dynamic-slice_add_fusion), channel_id=1, source_target_pairs={{0,64},{32,96},{64,0},{96,32},{128,192},{160,224},{192,128},{224,1... | collective-permute-start | bytes 4616 | tf_op jit(solution)/shard_map/ppermute | solution.py:25
  165.6 1.1 collective-permute-start.38
  166.8 2.1 %collective-permute-start.31 = (f32[48,384]{1,0:T(8,128)S(1)}, f32[48,384]{1,0:T(8,128)S(1)}, u32[]{:S(2)}, u32[]{:S(2)}) collective-permute-start(f32[48,384]{1,0:T(8,128)S(1)} %add.96.v0), channel_id=1, source_target_pairs={{0,32},{32,0},{64,96},{96,64},{128,160},{160,128},{192,224},{224,1... | collective-permute-start | bytes 221192 | tf_op jit(solution)/shard_map/ppermute | solution.py:25
  168.9 1.7 collective-permute-start.32
  170.5 1.1 collective-permute-start.33
  172.1 3.3 %collective-permute-done.39 = f32[8,48]{1,0:T(8,128)S(1)} collective-permute-done((f32[8,48]{1,0:T(8,128)S(1)}, f32[8,48]{1,0:T(8,128)S(1)}, u32[]{:S(2)}, u32[]{:S(2)}) %collective-permute-start.39) | collective-permute-done | bytes 1568 | tf_op jit(solution)/shard_map/ppermute | solution.py:25
  177.2 2.4 %join.1 = f32[48,1536]{1,0:T(8,128)} custom-call(s32[5]{0:T(128)} %stack.19.pos, f32[48,384]{1,0:T(8,128)} %copy-done.10, f32[48,384]{1,0:T(8,128)} %copy-done.17, f32[48,384]{1,0:T(8,128)} %copy-done.18, f32[48,384]{1,0:T(8,128)} %copy-done.19), custom_call_target="tpu_custom_call" | custom-call | bytes 7200000 | tf_op jit(solution)/shard_map/join/pallas_call | solution.py:242
  (105 shorter events, 14.2 us)
Async XLA Ops:
  1.5 1.3 collective-permute-start.3
  3.7 12.2 %collective-permute-start.5 = (bf16[8,1536]{1,0:T(8,128)(2,1)S(1)}, bf16[8,1536]{1,0:T(8,128)(2,1)S(1)}, u32[]{:S(2)}, u32[]{:S(2)}) collective-permute-start(bf16[8,1536]{1,0:T(8,128)(2,1)S(1)} %add.83), channel_id=1, source_target_pairs={{0,16},{1,17},{2,18},{3,19},{4,20},{5,21},{6,22},{7,23},{8,24},{9,... | collective-permute-start | bytes 73736 | tf_op jit(solution)/shard_map/ppermute | solution.py:20
  7.0 8.9 %collective-permute-start.6 = (bf16[8,1536]{1,0:T(8,128)(2,1)S(1)}, bf16[8,1536]{1,0:T(8,128)(2,1)S(1)}, u32[]{:S(2)}, u32[]{:S(2)}) collective-permute-start(bf16[8,1536]{1,0:T(8,128)(2,1)S(1)} %add.83), channel_id=1, source_target_pairs={{0,24},{1,25},{2,26},{3,27},{4,28},{5,29},{6,30},{7,31},{8,16},{9,... | collective-permute-start | bytes 73736 | tf_op jit(solution)/shard_map/ppermute | solution.py:20
  8.1 7.9 %collective-permute-start.4 = (bf16[8,1536]{1,0:T(8,128)(2,1)S(1)}, bf16[8,1536]{1,0:T(8,128)(2,1)S(1)}, u32[]{:S(2)}, u32[]{:S(2)}) collective-permute-start(bf16[8,1536]{1,0:T(8,128)(2,1)S(1)} %add.83), channel_id=1, source_target_pairs={{0,8},{1,9},{2,10},{3,11},{4,12},{5,13},{6,14},{7,15},{8,0},{9,1},... | collective-permute-start | bytes 73736 | tf_op jit(solution)/shard_map/ppermute | solution.py:20
  8.1 17.9 %collective-permute-start = (bf16[48,1536]{1,0:T(8,128)(2,1)}, bf16[48,1536]{1,0:T(8,128)(2,1)S(1)}, u32[]{:S(2)}, u32[]{:S(2)}) collective-permute-start(bf16[48,1536]{1,0:T(8,128)(2,1)} %refs_0_.1), channel_id=1, source_target_pairs={{0,2},{1,3},{2,0},{3,1},{4,6},{5,7},{6,4},{7,5},{8,10},{9,11},{10,... | collective-permute-start | bytes 442376 | tf_op jit(solution)/shard_map/ppermute | solution.py:20
  11.5 14.5 %collective-permute-start.1 = (bf16[48,1536]{1,0:T(8,128)(2,1)}, bf16[48,1536]{1,0:T(8,128)(2,1)S(1)}, u32[]{:S(2)}, u32[]{:S(2)}) collective-permute-start(bf16[48,1536]{1,0:T(8,128)(2,1)} %refs_0_.1), channel_id=1, source_target_pairs={{0,4},{1,5},{2,6},{3,7},{4,0},{5,1},{6,2},{7,3},{8,12},{9,13},{10,... | collective-permute-start | bytes 442376 | tf_op jit(solution)/shard_map/ppermute | solution.py:20
  15.9 13.1 %collective-permute-start.2 = (bf16[48,1536]{1,0:T(8,128)(2,1)}, bf16[48,1536]{1,0:T(8,128)(2,1)S(1)}, u32[]{:S(2)}, u32[]{:S(2)}) collective-permute-start(bf16[48,1536]{1,0:T(8,128)(2,1)} %refs_0_.1), channel_id=1, source_target_pairs={{0,6},{1,7},{2,4},{3,5},{4,2},{5,3},{6,0},{7,1},{8,14},{9,15},{10,... | collective-permute-start | bytes 442376 | tf_op jit(solution)/shard_map/ppermute | solution.py:20
  16.0 9.3 %collective-permute-start.7 = (bf16[8,1536]{1,0:T(8,128)(2,1)S(1)}, bf16[8,1536]{1,0:T(8,128)(2,1)S(1)}, u32[]{:S(2)}, u32[]{:S(2)}) collective-permute-start(bf16[8,1536]{1,0:T(8,128)(2,1)S(1)} %add_add_fusion.2), channel_id=1, source_target_pairs={{0,2},{1,3},{2,0},{3,1},{4,6},{5,7},{6,4},{7,5},{8,10},{9,11},{10,... | collective-permute-start | bytes 73736 | tf_op jit(solution)/shard_map/ppermute | solution.py:20
  25.9 3.1 %copy-start.13 = (bf16[48,1536]{1,0:T(8,128)(2,1)}, bf16[48,1536]{1,0:T(8,128)(2,1)S(1)}, u32[]{:S(2)}) copy-start(bf16[48,1536]{1,0:T(8,128)(2,1)S(1)} %collective-permute-done.refs_1_) | copy-start | bytes 442372
  26.0 3.1 %copy-start.15 = (bf16[48,1536]{1,0:T(8,128)(2,1)}, bf16[48,1536]{1,0:T(8,128)(2,1)S(1)}, u32[]{:S(2)}) copy-start(bf16[48,1536]{1,0:T(8,128)(2,1)S(1)} %collective-permute-done.1.refs_2_) | copy-start | bytes 442372
  31.7 21.3 %collective-permute-start.8 = (bf16[192,1536]{1,0:T(8,128)(2,1)}, bf16[192,1536]{1,0:T(8,128)(2,1)S(1)}, u32[]{:S(2)}, u32[]{:S(2)}) collective-permute-start(bf16[192,1536]{1,0:T(8,128)(2,1)} %gather.2.refs_0_), channel_id=1, source_target_pairs={{0,8},{1,9},{2,10},{3,11},{4,12},{5,13},{6,14},{7,15},{8,0},{9,1},... | collective-permute-start | bytes 1769480 | tf_op jit(solution)/shard_map/ppermute | solution.py:20
  33.5 19.5 %collective-permute-start.11 = (bf16[192,1536]{1,0:T(8,128)(2,1)}, bf16[192,1536]{1,0:T(8,128)(2,1)S(1)}, u32[]{:S(2)}, u32[]{:S(2)}) collective-permute-start(bf16[192,1536]{1,0:T(8,128)(2,1)} %gather.2.refs_0_), channel_id=1, source_target_pairs={{0,24},{1,25},{2,26},{3,27},{4,28},{5,29},{6,30},{7,31},{8,16},{9,... | collective-permute-start | bytes 1769480 | tf_op jit(solution)/shard_map/ppermute | solution.py:20
  35.7 6.4 %collective-permute-start.10 = (bf16[8,1536]{1,0:T(8,128)(2,1)}, bf16[8,1536]{1,0:T(8,128)(2,1)S(1)}, u32[]{:S(2)}, u32[]{:S(2)}) collective-permute-start(bf16[8,1536]{1,0:T(8,128)(2,1)} %add.87.refs_4_), channel_id=1, source_target_pairs={{0,6},{1,7},{2,4},{3,5},{4,2},{5,3},{6,0},{7,1},{8,14},{9,15},{10,... | collective-permute-start | bytes 73736 | tf_op jit(solution)/shard_map/ppermute | solution.py:20
  54.0 8.1 %copy-start.2 = (bf16[192,1536]{1,0:T(8,128)(2,1)S(1)}, bf16[192,1536]{1,0:T(8,128)(2,1)}, u32[]{:S(2)}) copy-start(bf16[192,1536]{1,0:T(8,128)(2,1)} %gather.2.refs_0_) | copy-start | bytes 1769476
  62.1 5.4 %collective-permute-start.12 = (bf16[16,48,1536]{2,1,0:T(8,128)(2,1)}, bf16[16,48,1536]{2,1,0:T(8,128)(2,1)S(1)}, u32[]{:S(2)}, u32[]{:S(2)}) collective-permute-start(bf16[16,48,1536]{2,1,0:T(8,128)(2,1)} %get-tuple-element.28), channel_id=1, source_target_pairs={{0,1},{1,0},{2,3},{3,2},{4,5},{5,4},{6,7},{7,6},{8,9},{9,8},{10,11... | collective-permute-start | bytes 7077896 | tf_op jit(solution)/shard_map/ppermute | solution.py:20
  62.2 17.4 %collective-permute-start.9 = (bf16[192,1536]{1,0:T(8,128)(2,1)S(1)}, bf16[192,1536]{1,0:T(8,128)(2,1)}, u32[]{:S(2)}, u32[]{:S(2)}) collective-permute-start(bf16[192,1536]{1,0:T(8,128)(2,1)S(1)} %copy-done.2), channel_id=1, source_target_pairs={{0,16},{1,17},{2,18},{3,19},{4,20},{5,21},{6,22},{7,23},{8,24},{9,... | collective-permute-start | bytes 1769480 | tf_op jit(solution)/shard_map/ppermute | solution.py:20
  62.4 19.0 %collective-permute-start.13 = (bf16[192,1536]{1,0:T(8,128)(2,1)S(1)}, bf16[192,1536]{1,0:T(8,128)(2,1)S(1)}, u32[]{:S(2)}, u32[]{:S(2)}) collective-permute-start(bf16[192,1536]{1,0:T(8,128)(2,1)S(1)} %copy-done.2), channel_id=1, source_target_pairs={{0,1},{1,0},{2,3},{3,2},{4,5},{5,4},{6,7},{7,6},{8,9},{9,8},{10,11... | collective-permute-start | bytes 1769480 | tf_op jit(solution)/shard_map/ppermute | solution.py:20
  62.7 21.3 %collective-permute-start.14 = (bf16[192,1536]{1,0:T(8,128)(2,1)}, bf16[192,1536]{1,0:T(8,128)(2,1)}, u32[]{:S(2)}, u32[]{:S(2)}) collective-permute-start(bf16[192,1536]{1,0:T(8,128)(2,1)} %copy-done), channel_id=1, source_target_pairs={{0,1},{1,0},{2,3},{3,2},{4,5},{5,4},{6,7},{7,6},{8,9},{9,8},{10,11... | collective-permute-start | bytes 1769480 | tf_op jit(solution)/shard_map/ppermute | solution.py:20
  63.6 22.5 %collective-permute-start.16 = (bf16[192,1536]{1,0:T(8,128)(2,1)}, bf16[192,1536]{1,0:T(8,128)(2,1)}, u32[]{:S(2)}, u32[]{:S(2)}) collective-permute-start(bf16[192,1536]{1,0:T(8,128)(2,1)} %copy-done.1), channel_id=1, source_target_pairs={{0,1},{1,0},{2,3},{3,2},{4,5},{5,4},{6,7},{7,6},{8,9},{9,8},{10,11... | collective-permute-start | bytes 1769480 | tf_op jit(solution)/shard_map/ppermute | solution.py:20
  74.9 9.0 %copy-start.21 = (bf16[4,48,1536]{2,1,0:T(8,128)(2,1)S(1)}, bf16[4,48,1536]{2,1,0:T(8,128)(2,1)}, u32[]{:S(2)}) copy-start(bf16[4,48,1536]{2,1,0:T(8,128)(2,1)} %get-tuple-element.32) | copy-start | bytes 1769476
  81.4 4.7 %collective-permute-start.15 = (bf16[192,1536]{1,0:T(8,128)(2,1)}, bf16[192,1536]{1,0:T(8,128)(2,1)S(1)}, u32[]{:S(2)}, u32[]{:S(2)}) collective-permute-start(bf16[192,1536]{1,0:T(8,128)(2,1)} %gather.3.refs_2_), channel_id=1, source_target_pairs={{0,1},{1,0},{2,3},{3,2},{4,5},{5,4},{6,7},{7,6},{8,9},{9,8},{10,11... | collective-permute-start | bytes 1769480 | tf_op jit(solution)/shard_map/ppermute | solution.py:20
  81.4 35.1 %collective-permute-start.17 = (bf16[4,48,1536]{2,1,0:T(8,128)(2,1)}, bf16[4,48,1536]{2,1,0:T(8,128)(2,1)S(1)}, u32[]{:S(2)}, u32[]{:S(2)}) collective-permute-start(bf16[4,48,1536]{2,1,0:T(8,128)(2,1)} %get-tuple-element.30), channel_id=1, source_target_pairs={{0,8},{1,9},{2,10},{3,11},{4,12},{5,13},{6,14},{7,15},{8,0},{9,1},... | collective-permute-start | bytes 1769480 | tf_op jit(solution)/shard_map/ppermute | solution.py:20
  81.4 4.7 %copy-start.4 = (bf16[192,1536]{1,0:T(8,128)(2,1)}, bf16[192,1536]{1,0:T(8,128)(2,1)S(1)}, u32[]{:S(2)}) copy-start(bf16[192,1536]{1,0:T(8,128)(2,1)S(1)} %collective-permute-done.13.refs_4_) | copy-start | bytes 1769476
  81.5 37.0 %collective-permute-start.18 = (bf16[4,48,1536]{2,1,0:T(8,128)(2,1)}, bf16[4,48,1536]{2,1,0:T(8,128)(2,1)S(1)}, u32[]{:S(2)}, u32[]{:S(2)}) collective-permute-start(bf16[4,48,1536]{2,1,0:T(8,128)(2,1)} %get-tuple-element.31), channel_id=1, source_target_pairs={{0,16},{1,17},{2,18},{3,19},{4,20},{5,21},{6,22},{7,23},{8,24},{9,... | collective-permute-start | bytes 1769480 | tf_op jit(solution)/shard_map/ppermute | solution.py:20
  84.0 34.5 %collective-permute-start.19 = (bf16[4,48,1536]{2,1,0:T(8,128)(2,1)S(1)}, bf16[4,48,1536]{2,1,0:T(8,128)(2,1)S(1)}, u32[]{:S(2)}, u32[]{:S(2)}) collective-permute-start(bf16[4,48,1536]{2,1,0:T(8,128)(2,1)S(1)} %copy-done.21), channel_id=1, source_target_pairs={{0,24},{1,25},{2,26},{3,27},{4,28},{5,29},{6,30},{7,31},{8,16},{9,... | collective-permute-start | bytes 1769480 | tf_op jit(solution)/shard_map/ppermute | solution.py:20
  112.7 1.4 collective-permute-start.20
  115.0 13.6 %collective-permute-start.22 = (f32[8,1536]{1,0:T(8,128)S(1)}, f32[8,1536]{1,0:T(8,128)S(1)}, u32[]{:S(2)}, u32[]{:S(2)}) collective-permute-start(f32[8,1536]{1,0:T(8,128)S(1)} %add.89), channel_id=1, source_target_pairs={{0,16},{1,17},{2,18},{3,19},{4,20},{5,21},{6,22},{7,23},{8,24},{9,... | collective-permute-start | bytes 147464 | tf_op jit(solution)/shard_map/ppermute | solution.py:20
  115.0 15.3 %collective-permute-start.23 = (f32[8,1536]{1,0:T(8,128)S(1)}, f32[8,1536]{1,0:T(8,128)S(1)}, u32[]{:S(2)}, u32[]{:S(2)}) collective-permute-start(f32[8,1536]{1,0:T(8,128)S(1)} %add.89), channel_id=1, source_target_pairs={{0,24},{1,25},{2,26},{3,27},{4,28},{5,29},{6,30},{7,31},{8,16},{9,... | collective-permute-start | bytes 147464 | tf_op jit(solution)/shard_map/ppermute | solution.py:20
  116.5 13.7 %collective-permute-start.21 = (f32[8,1536]{1,0:T(8,128)S(1)}, f32[8,1536]{1,0:T(8,128)S(1)}, u32[]{:S(2)}, u32[]{:S(2)}) collective-permute-start(f32[8,1536]{1,0:T(8,128)S(1)} %add.89), channel_id=1, source_target_pairs={{0,8},{1,9},{2,10},{3,11},{4,12},{5,13},{6,14},{7,15},{8,0},{9,1},... | collective-permute-start | bytes 147464 | tf_op jit(solution)/shard_map/ppermute | solution.py:20
  123.7 17.2 %collective-permute-start.24 = (bf16[48,1536]{1,0:T(8,128)(2,1)}, bf16[48,1536]{1,0:T(8,128)(2,1)S(1)}, u32[]{:S(2)}, u32[]{:S(2)}) collective-permute-start(bf16[48,1536]{1,0:T(8,128)(2,1)} %get-tuple-element.40), channel_id=1, source_target_pairs={{0,2},{1,3},{2,0},{3,1},{4,6},{5,7},{6,4},{7,5},{8,10},{9,11},{10,... | collective-permute-start | bytes 442376 | tf_op jit(solution)/shard_map/ppermute | solution.py:20
  124.8 16.1 %collective-permute-start.25 = (bf16[48,1536]{1,0:T(8,128)(2,1)}, bf16[48,1536]{1,0:T(8,128)(2,1)S(1)}, u32[]{:S(2)}, u32[]{:S(2)}) collective-permute-start(bf16[48,1536]{1,0:T(8,128)(2,1)} %get-tuple-element.41), channel_id=1, source_target_pairs={{0,4},{1,5},{2,6},{3,7},{4,0},{5,1},{6,2},{7,3},{8,12},{9,13},{10,... | collective-permute-start | bytes 442376 | tf_op jit(solution)/shard_map/ppermute | solution.py:20
  128.6 14.3 %collective-permute-start.26 = (bf16[48,1536]{1,0:T(8,128)(2,1)}, bf16[48,1536]{1,0:T(8,128)(2,1)S(1)}, u32[]{:S(2)}, u32[]{:S(2)}) collective-permute-start(bf16[48,1536]{1,0:T(8,128)(2,1)} %get-tuple-element.42), channel_id=1, source_target_pairs={{0,6},{1,7},{2,4},{3,5},{4,2},{5,3},{6,0},{7,1},{8,14},{9,15},{10,... | collective-permute-start | bytes 442376 | tf_op jit(solution)/shard_map/ppermute | solution.py:20
  140.9 9.5 %copy-start.9 = (f32[8,1536]{1,0:T(8,128)S(1)}, f32[8,1536]{1,0:T(8,128)}, u32[]{:S(2)}) copy-start(f32[8,1536]{1,0:T(8,128)} %add_add_fusion.1.refs_11_) | copy-start | bytes 147460
  146.2 11.2 %collective-permute-start.28 = (f32[48,384]{1,0:T(8,128)}, f32[48,384]{1,0:T(8,128)S(1)}, u32[]{:S(2)}, u32[]{:S(2)}) collective-permute-start(f32[48,384]{1,0:T(8,128)} %get-tuple-element.45), channel_id=1, source_target_pairs={{0,64},{32,96},{64,0},{96,32},{128,192},{160,224},{192,128},{224,1... | collective-permute-start | bytes 221192 | tf_op jit(solution)/shard_map/ppermute | solution.py:25
  149.2 8.2 %collective-permute-start.29 = (f32[48,384]{1,0:T(8,128)}, f32[48,384]{1,0:T(8,128)S(1)}, u32[]{:S(2)}, u32[]{:S(2)}) collective-permute-start(f32[48,384]{1,0:T(8,128)} %get-tuple-element.46), channel_id=1, source_target_pairs={{0,96},{32,64},{64,32},{96,0},{128,224},{160,192},{192,160},{224,1... | collective-permute-start | bytes 221192 | tf_op jit(solution)/shard_map/ppermute | solution.py:25
  150.4 7.1 %collective-permute-start.27 = (f32[48,384]{1,0:T(8,128)}, f32[48,384]{1,0:T(8,128)S(1)}, u32[]{:S(2)}, u32[]{:S(2)}) collective-permute-start(f32[48,384]{1,0:T(8,128)} %get-tuple-element.44), channel_id=1, source_target_pairs={{0,32},{32,0},{64,96},{96,64},{128,160},{160,128},{192,224},{224,1... | collective-permute-start | bytes 221192 | tf_op jit(solution)/shard_map/ppermute | solution.py:25
  150.4 5.0 %collective-permute-start.34 = (f32[8,1536]{1,0:T(8,128)S(1)}, f32[8,1536]{1,0:T(8,128)S(1)}, u32[]{:S(2)}, u32[]{:S(2)}) collective-permute-start(f32[8,1536]{1,0:T(8,128)S(1)} %copy-done.9), channel_id=1, source_target_pairs={{0,2},{1,3},{2,0},{3,1},{4,6},{5,7},{6,4},{7,5},{8,10},{9,11},{10,... | collective-permute-start | bytes 147464 | tf_op jit(solution)/shard_map/ppermute | solution.py:20
  155.4 6.8 %collective-permute-start.35 = (f32[8,1536]{1,0:T(8,128)S(1)}, f32[8,1536]{1,0:T(8,128)S(1)}, u32[]{:S(2)}, u32[]{:S(2)}) collective-permute-start(f32[8,1536]{1,0:T(8,128)S(1)} %add.97), channel_id=1, source_target_pairs={{0,6},{1,7},{2,4},{3,5},{4,2},{5,3},{6,0},{7,1},{8,14},{9,15},{10,... | collective-permute-start | bytes 147464 | tf_op jit(solution)/shard_map/ppermute | solution.py:20
  158.4 8.4 %collective-permute-start.30 = (f32[48,384]{1,0:T(8,128)S(1)}, f32[48,384]{1,0:T(8,128)S(1)}, u32[]{:S(2)}, u32[]{:S(2)}) collective-permute-start(f32[48,384]{1,0:T(8,128)S(1)} %add_add_fusion), channel_id=1, source_target_pairs={{0,128},{32,160},{64,192},{96,224},{128,0},{160,32},{192,64},{224,... | collective-permute-start | bytes 221192 | tf_op jit(solution)/shard_map/ppermute | solution.py:25
  162.2 8.3 %collective-permute-start.37 = (f32[8,48]{1,0:T(8,128)S(1)}, f32[8,48]{1,0:T(8,128)S(1)}, u32[]{:S(2)}, u32[]{:S(2)}) collective-permute-start(f32[8,48]{1,0:T(8,128)S(1)} %dynamic-slice_add_fusion), channel_id=1, source_target_pairs={{0,64},{32,96},{64,0},{96,32},{128,192},{160,224},{192,128},{224,1... | collective-permute-start | bytes 4616 | tf_op jit(solution)/shard_map/ppermute | solution.py:25
  165.6 6.0 %collective-permute-start.38 = (f32[8,48]{1,0:T(8,128)S(1)}, f32[8,48]{1,0:T(8,128)S(1)}, u32[]{:S(2)}, u32[]{:S(2)}) collective-permute-start(f32[8,48]{1,0:T(8,128)S(1)} %dynamic-slice_add_fusion), channel_id=1, source_target_pairs={{0,96},{32,64},{64,32},{96,0},{128,224},{160,192},{192,160},{224,1... | collective-permute-start | bytes 4616 | tf_op jit(solution)/shard_map/ppermute | solution.py:25
  166.7 4.9 %collective-permute-start.36 = (f32[8,48]{1,0:T(8,128)S(1)}, f32[8,48]{1,0:T(8,128)S(1)}, u32[]{:S(2)}, u32[]{:S(2)}) collective-permute-start(f32[8,48]{1,0:T(8,128)S(1)} %dynamic-slice_add_fusion), channel_id=1, source_target_pairs={{0,32},{32,0},{64,96},{96,64},{128,160},{160,128},{192,224},{224,1... | collective-permute-start | bytes 4616 | tf_op jit(solution)/shard_map/ppermute | solution.py:25
  166.7 9.3 %copy-start.10 = (f32[48,384]{1,0:T(8,128)}, f32[48,384]{1,0:T(8,128)S(1)}, u32[]{:S(2)}) copy-start(f32[48,384]{1,0:T(8,128)S(1)} %add.96.v0) | copy-start | bytes 221188
  166.8 9.2 %collective-permute-start.31 = (f32[48,384]{1,0:T(8,128)S(1)}, f32[48,384]{1,0:T(8,128)S(1)}, u32[]{:S(2)}, u32[]{:S(2)}) collective-permute-start(f32[48,384]{1,0:T(8,128)S(1)} %add.96.v0), channel_id=1, source_target_pairs={{0,32},{32,0},{64,96},{96,64},{128,160},{160,128},{192,224},{224,1... | collective-permute-start | bytes 221192 | tf_op jit(solution)/shard_map/ppermute | solution.py:25
  168.9 7.1 %collective-permute-start.32 = (f32[48,384]{1,0:T(8,128)S(1)}, f32[48,384]{1,0:T(8,128)S(1)}, u32[]{:S(2)}, u32[]{:S(2)}) collective-permute-start(f32[48,384]{1,0:T(8,128)S(1)} %add.96.v0), channel_id=1, source_target_pairs={{0,64},{32,96},{64,0},{96,32},{128,192},{160,224},{192,128},{224,1... | collective-permute-start | bytes 221192 | tf_op jit(solution)/shard_map/ppermute | solution.py:25
  170.5 5.6 %collective-permute-start.33 = (f32[48,384]{1,0:T(8,128)S(1)}, f32[48,384]{1,0:T(8,128)S(1)}, u32[]{:S(2)}, u32[]{:S(2)}) collective-permute-start(f32[48,384]{1,0:T(8,128)S(1)} %add.96.v0), channel_id=1, source_target_pairs={{0,96},{32,64},{64,32},{96,0},{128,224},{160,192},{192,160},{224,1... | collective-permute-start | bytes 221192 | tf_op jit(solution)/shard_map/ppermute | solution.py:25
  171.7 3.7 %collective-permute-start.39 = (f32[8,48]{1,0:T(8,128)S(1)}, f32[8,48]{1,0:T(8,128)S(1)}, u32[]{:S(2)}, u32[]{:S(2)}) collective-permute-start(f32[8,48]{1,0:T(8,128)S(1)} %add_add_fusion.3), channel_id=1, source_target_pairs={{0,128},{32,160},{64,192},{96,224},{128,0},{160,32},{192,64},{224,... | collective-permute-start | bytes 4616 | tf_op jit(solution)/shard_map/ppermute | solution.py:25
  175.4 4.2 %copy-start.20 = (f32[8,48]{1,0:T(8,128)}, f32[8,48]{1,0:T(8,128)S(1)}, u32[]{:S(2)}) copy-start(f32[8,48]{1,0:T(8,128)S(1)} %add.102) | copy-start | bytes 4612
  (14 other events, 15.1 us)
